TPU v7x, 32 devices: a whole 2x2x4 slice. The times are simulated.
32 devices in a mesh: tm: 4 (over z), node: 8 (over y, x, core).
Axes of the slice: x: 2, y: 2, z: 4, core: 2. Of those that a mesh axis runs over, the one named last changes fastest.
Arguments:
- memory: float32 [4096, 256], P('node'), may hold values from -6 to 6
- src_slot: int32 [4, 8, 512], P('tm', 'node'), may hold values from 0 to 1023, as said below
- dst_slot: int32 [4, 8, 512], P('tm', 'node'), may hold values from 0 to 1023, as said below
- event_time: float32 [4, 8, 512], P('tm', 'node'), may hold values from 0 to 200
- touched_rows: int32 [4, 8, 8, 128], P('tm', 'node'), may hold values from 0 to 511, as said below
- time_freq: float32 [128], replicated, may hold values from 0.01 to 1
- msg_weight: bfloat16 [640, 256], replicated, may hold values from -0.25 to 0.25
- msg_bias: float32 [256], replicated, may hold values from -3 to 3
- gate_weight: bfloat16 [256, 512], replicated, may hold values from -0.375 to 0.375
- update_bias: float32 [256], replicated, may hold values from -5 to 1
Outputs:
- period_memory: float32 [4, 4096, 256], P('tm', 'node')
Inputs may be any that keep to these rules, and one draw needn't show every extreme that they name: touched_rows[t, o, b] holds 128 distinct rows among the 512 rows that owner o keeps. `src_slot`: slot s of event block b in period t stands for node (s // 128) * 512 + touched_rows[t, s // 128, b, s % 128]. `dst_slot`: read as src_slot.
All inputs are finite; a program needn't handle non-finite values.
Results may differ from a plain program's by a relative error of at most 0.0019.
Values may be sent and summed in bfloat16 or wider, within the bound.
No kernel may reach another device: no remote copies, remote signals or barrier semaphores. Data moves between devices by JAX's collectives and lax.ppermute only.
A program may use at most 64 MiB of HBM per device.

v0:
```python
import jax
import jax.numpy as jnp
from jax import lax
from jax.sharding import PartitionSpec as P


def advance(memory_state, pieces):
    updated = pieces[0] * memory_state + pieces[1]
    return (updated, updated)


def one_hot_rows(indices, width):
    return (indices[:, None] == jnp.arange(width, dtype=jnp.int32)[None, :]).astype(jnp.bfloat16)


def summed_over_rows(hot, values):
    upper = values.astype(jnp.bfloat16)
    lower = (values - upper.astype(jnp.float32)).astype(jnp.bfloat16)
    dims = (((0,), (0,)), ((), ()))
    first = lax.dot_general(hot, upper, dims, preferred_element_type=jnp.float32)
    second = lax.dot_general(hot, lower, dims, preferred_element_type=jnp.float32)
    return first + second


def shards(
    memory,
    src_slot,
    dst_slot,
    event_time,
    touched_rows,
    time_freq,
    msg_weight,
    msg_bias,
    gate_weight,
    update_bias,
):
    row_lists = touched_rows[0, 0]
    blocks, capacity = row_lists.shape
    node_rows, breadth = memory.shape
    slot_total = blocks * capacity
    flat_rows = row_lists.reshape(-1)
    row_hot = one_hot_rows(flat_rows, node_rows)
    picked = jnp.dot(
        row_hot, memory.astype(jnp.bfloat16), preferred_element_type=jnp.float32
    ).astype(jnp.bfloat16)
    fetched = lax.all_to_all(
        picked.reshape(blocks, capacity, breadth), "node", split_axis=0, concat_axis=0, tiled=True
    )
    slot_table = fetched.reshape(slot_total, breadth)
    sources = src_slot[0, 0]
    targets = dst_slot[0, 0]
    all_slots = jnp.concatenate([sources, targets])
    slot_hot = one_hot_rows(all_slots, slot_total)
    both_rows = jnp.dot(slot_hot, slot_table, preferred_element_type=jnp.float32).astype(
        jnp.bfloat16
    )
    events = sources.shape[0]
    from_rows = both_rows[:events]
    to_rows = both_rows[events:]
    encoding = jnp.cos(event_time[0, 0][:, None] * time_freq[None, :]).astype(jnp.bfloat16)
    inputs = jnp.concatenate(
        [
            jnp.concatenate([from_rows, to_rows, encoding], 1),
            jnp.concatenate([to_rows, from_rows, encoding], 1),
        ],
        0,
    )
    messages = jax.nn.relu(
        jnp.dot(inputs, msg_weight, preferred_element_type=jnp.float32) + msg_bias
    )
    totals = summed_over_rows(slot_hot, messages)
    counts = jnp.sum(slot_hot, axis=0, dtype=jnp.float32)
    got_totals, got_counts = (
        lax.all_to_all(
            totals.reshape(blocks, capacity, breadth).astype(jnp.bfloat16),
            "node",
            split_axis=0,
            concat_axis=0,
            tiled=True,
        ).astype(jnp.float32),
        lax.all_to_all(
            counts.reshape(blocks, capacity).astype(jnp.bfloat16),
            "node",
            split_axis=0,
            concat_axis=0,
            tiled=True,
        ).astype(jnp.float32),
    )
    node_totals = summed_over_rows(row_hot, got_totals.reshape(slot_total, breadth))
    node_counts = jnp.dot(
        got_counts.reshape(1, slot_total),
        row_hot.astype(jnp.float32),
        precision=lax.Precision.HIGHEST,
    )[0]
    mean_msg = (node_totals / jnp.maximum(node_counts, 1.0)[:, None]).astype(jnp.bfloat16)
    gate_terms = jnp.dot(mean_msg, gate_weight, preferred_element_type=jnp.float32)
    update = jax.nn.sigmoid(gate_terms[:, :breadth] + update_bias)
    candidate = jnp.tanh(gate_terms[:, breadth:])
    touched = (node_counts > 0.0)[:, None]
    keep_rate = jnp.where(touched, 1.0 - update, 1.0)
    write_term = jnp.where(touched, update * candidate, 0.0)
    tm_count = lax.axis_size("tm")
    row_share = node_rows // tm_count
    keep_parts, write_parts = (
        lax.all_to_all(
            keep_rate.reshape(tm_count, row_share, breadth),
            "tm",
            split_axis=0,
            concat_axis=0,
            tiled=True,
        ),
        lax.all_to_all(
            write_term.reshape(tm_count, row_share, breadth),
            "tm",
            split_axis=0,
            concat_axis=0,
            tiled=True,
        ),
    )
    row_start = lax.axis_index("tm") * row_share
    initial = lax.dynamic_slice_in_dim(memory, row_start, row_share, 0)
    final_state, history = lax.scan(advance, initial, (keep_parts, write_parts))
    returned = lax.all_to_all(history, "tm", split_axis=0, concat_axis=0, tiled=True)
    result = returned.reshape(node_rows, breadth)
    return result[None]


def solution(mesh):
    return jax.shard_map(
        shards,
        mesh=mesh,
        in_specs=(
            P("node", None),
            P("tm", "node", None),
            P("tm", "node", None),
            P("tm", "node", None),
            P("tm", "node", None, None),
            P(),
            P(),
            P(),
            P(),
            P(),
        ),
        out_specs=P("tm", "node", None),
        check_vma=False,
    )
```

profile of v0, /device:TPU:2, one launch (start us, length us, event | category | flops | bytes accessed | tf_op | source)
XLA Modules:
  0.0 96.0 jit_solution(1006169828845790491)
XLA Ops:
  0.0 2.4 %fusion.26 = bf16[1024,256]{1,0:T(8,128)(2,1)} fusion(s32[1024]{0:T(1024)} %bitcast.43, f32[512,256]{1,0:T(8,128)} %param.12), kind=kOutput, calls=%fused_computation.32 | convolution fusion | flops 269352960 | bytes 1052672 | tf_op jit(solution)/shard_map/dot_general | solution.py:43
  2.4 4.3 %all-to-all-start.1 = ((bf16[8,128,256]{2,1,0:T(8,128)(2,1)}), bf16[8,128,256]{2,1,0:T(8,128)(2,1)S(1)}, u32[]{:S(2)}, u32[]{:S(2)}) async-start(bf16[8,128,256]{2,1,0:T(8,128)(2,1)} %bitcast.8), calls=%async_computation.1 | async-start | bytes 1048576 | tf_op jit(solution)/shard_map/all_to_all | solution.py:46
  6.7 0.5 fusion.4
  7.2 0.6 copy.12
  7.8 0.9 cosine_convert_fusion
  8.7 6.2 %all-to-all-done.1 = bf16[8,128,256]{2,1,0:T(8,128)(2,1)S(1)} async-done(((bf16[8,128,256]{2,1,0:T(8,128)(2,1)}), bf16[8,128,256]{2,1,0:T(8,128)(2,1)S(1)}, u32[]{:S(2)}, u32[]{:S(2)}) %all-to-all-start.1) | async-done | bytes 524320 | tf_op jit(solution)/shard_map/all_to_all | solution.py:46
  15.0 4.7 %all-to-all-start = ((bf16[8,1,128]{2,1,0:T(2,128)(2,1)}), bf16[8,1,128]{2,1,0:T(2,128)(2,1)S(1)}, u32[]{:S(2)}, u32[]{:S(2)}) async-start(bf16[8,1,128]{2,1,0:T(2,128)(2,1)} %copy.12), calls=%async_computation | async-start | bytes 8192 | tf_op jit(solution)/shard_map/all_to_all | solution.py:81
  19.7 1.1 %fusion.27 = bf16[1024,256]{0,1:T(8,128)(2,1)S(1)} fusion(bf16[1024,256]{1,0:T(8,128)(2,1)S(1)} %bitcast.34, s32[1024]{0:T(1024)S(1)} %pad_add_fusion), kind=kOutput, calls=%fused_computation.33 | convolution fusion | flops 538181632 | bytes 1052672 | tf_op jit(solution)/shard_map/dot_general | solution.py:54
  20.8 0.0 copy-start.8
  20.9 0.6 copy-done.8
  21.5 0.6 fusion.12
  22.1 1.4 %fusion = f32[1024,256]{1,0:T(8,128)S(1)} fusion(s32[1024]{0:T(1024)S(1)} %pad_add_fusion, f32[1024,256]{1,0:T(8,128)S(1)} %fusion.12), kind=kOutput, calls=%fused_computation.4 | convolution fusion | flops 538968064 | bytes 2101248 | tf_op jit(solution)/shard_map/dot_general | solution.py:21
  23.5 2.2 %fusion.25 = bf16[1024,256]{1,0:T(8,128)(2,1)} fusion(f32[1024,256]{1,0:T(8,128)S(1)} %fusion, s32[1024]{0:T(1024)S(1)} %pad_add_fusion, f32[1024,256]{1,0:T(8,128)S(1)} %fusion.12), kind=kOutput, calls=%fused_computation.31 | convolution fusion | flops 538705920 | bytes 2625536 | tf_op jit(solution)/shard_map/dot_general | solution.py:20
  25.8 0.0 all-to-all-done
  25.8 4.4 %all-to-all-start.2 = ((bf16[8,128,256]{2,1,0:T(8,128)(2,1)}), bf16[8,128,256]{2,1,0:T(8,128)(2,1)S(1)}, u32[]{:S(2)}, u32[]{:S(2)}) async-start(bf16[8,128,256]{2,1,0:T(8,128)(2,1)} %bitcast.11), calls=%async_computation.2 | async-start | bytes 1048576 | tf_op jit(solution)/shard_map/all_to_all | solution.py:74
  30.2 0.5 fusion.8
  30.7 7.7 %all-to-all-done.2 = bf16[8,128,256]{2,1,0:T(8,128)(2,1)S(1)} async-done(((bf16[8,128,256]{2,1,0:T(8,128)(2,1)}), bf16[8,128,256]{2,1,0:T(8,128)(2,1)S(1)}, u32[]{:S(2)}, u32[]{:S(2)}) %all-to-all-start.2) | async-done | bytes 524320 | tf_op jit(solution)/shard_map/all_to_all | solution.py:74
  38.4 0.9 fusion.5
  39.3 0.1 copy-done.6
  39.4 1.2 %fusion.31 = f32[512,512]{1,0:T(8,128)S(1)} fusion(bf16[256,512]{1,0:T(8,128)(2,1)S(1)} %copy-done.6, f32[512,256]{1,0:T(8,128)S(1)} %fusion.5, bf16[1024,256]{1,0:T(8,128)(2,1)S(1)} %bitcast.36, s32[1024]{0:T(1024)S(1)} %bitcast.46, f32[512]{0:T(512)S(1)} %broadcast_maximum_fusion), kind=kOutput, calls=%fused_computation.37 | convolution fusion | flops 403570688 | bytes 2365440 | tf_op jit(solution)/shard_map/dot_general | solution.py:96
  40.5 1.0 %fusion.38 = (f32[512,256]{1,0:T(8,128)}, f32[512,256]{1,0:T(8,128)S(1)}) fusion(f32[512,512]{1,0:T(8,128)S(1)} %fusion.31, pred[512]{0:T(512)(128)(4,1)S(1)} %broadcast_compare_fusion, f32[256]{0:T(256)S(1)} %copy-done.4), kind=kLoop, calls=%fused_computation.46 | loop fusion | flops 1048576 | bytes 2098688 | tf_op jit(solution)/shard_map/jit(_where)/select_n | solution.py:101
  41.6 19.4 %all_to_all.31 = f32[4,128,256]{2,1,0:T(8,128)S(1)} all-to-all(f32[4,128,256]{2,1,0:T(8,128)S(1)} %bitcast.33), channel_id=1, replica_groups=mesh['tm'=4,'node'=8] {'tm'}, dimensions={0} | all-to-all | bytes 1048576 | tf_op jit(solution)/shard_map/all_to_all | solution.py:105
  61.0 3.5 %all-to-all-start.4 = ((f32[4,128,256]{2,1,0:T(8,128)}), f32[4,128,256]{2,1,0:T(8,128)S(1)}, u32[]{:S(2)}, u32[]{:S(2)}) async-start(f32[4,128,256]{2,1,0:T(8,128)} %bitcast.14), calls=%async_computation.4 | async-start | bytes 1048576 | tf_op jit(solution)/shard_map/all_to_all | solution.py:112
  64.5 0.9 constant_dynamic-slice_fusion
  65.4 13.1 %all-to-all-done.4 = f32[4,128,256]{2,1,0:T(8,128)S(1)} async-done(((f32[4,128,256]{2,1,0:T(8,128)}), f32[4,128,256]{2,1,0:T(8,128)S(1)}, u32[]{:S(2)}, u32[]{:S(2)}) %all-to-all-start.4) | async-done | bytes 524320 | tf_op jit(solution)/shard_map/all_to_all | solution.py:112
  78.5 0.3 while.12
  78.5 0.1 bitcast_dynamic-update-slice_fusion.2
  78.5 0.1 bitcast_dynamic-update-slice_fusion.2
  78.6 0.1 bitcast_dynamic-update-slice_fusion.2
  78.7 0.1 bitcast_dynamic-update-slice_fusion.2
  78.8 16.4 %all_to_all.32 = f32[4,128,256]{2,1,0:T(8,128)S(1)} all-to-all(f32[4,128,256]{2,1,0:T(8,128)S(1)} %get-tuple-element.32), channel_id=1, replica_groups=mesh['tm'=4,'node'=8] {'tm'}, dimensions={0} | all-to-all | bytes 1048576 | tf_op jit(solution)/shard_map/all_to_all | solution.py:123
  95.2 0.8 copy.26
  (20 shorter events, 0.1 us)
Async XLA Ops:
  0.0 20.9 %copy-start = (bf16[640,256]{1,0:T(8,128)(2,1)S(1)}, bf16[640,256]{1,0:T(8,128)(2,1)}, u32[]{:S(2)}) copy-start(bf16[640,256]{1,0:T(8,128)(2,1)} %param.18) | copy-start | bytes 983044
  0.0 6.7 %copy-start.2 = (s32[1,1,512]{2,1,0:T(1,128)S(1)}, s32[1,1,512]{2,1,0:T(1,128)}, u32[]{:S(2)}) copy-start(s32[1,1,512]{2,1,0:T(1,128)} %param.14) | copy-start | bytes 6148
  0.0 6.7 %copy-start.3 = (s32[1,1,512]{2,1,0:T(1,128)S(1)}, s32[1,1,512]{2,1,0:T(1,128)}, u32[]{:S(2)}) copy-start(s32[1,1,512]{2,1,0:T(1,128)} %param.13) | copy-start | bytes 6148
  0.0 7.8 %copy-start.1 = (f32[1,1,512]{2,1,0:T(1,128)S(1)}, f32[1,1,512]{2,1,0:T(1,128)}, u32[]{:S(2)}) copy-start(f32[1,1,512]{2,1,0:T(1,128)} %param.15) | copy-start | bytes 6148
  0.0 7.8 %copy-start.5 = (f32[128]{0:T(128)S(1)}, f32[128]{0:T(128)}, u32[]{:S(2)}) copy-start(f32[128]{0:T(128)} %param.17) | copy-start | bytes 1540
  2.4 12.5 %all-to-all-start.1 = ((bf16[8,128,256]{2,1,0:T(8,128)(2,1)}), bf16[8,128,256]{2,1,0:T(8,128)(2,1)S(1)}, u32[]{:S(2)}, u32[]{:S(2)}) async-start(bf16[8,128,256]{2,1,0:T(8,128)(2,1)} %bitcast.8), calls=%async_computation.1 | async-start | bytes 1048576 | tf_op jit(solution)/shard_map/all_to_all | solution.py:46
  15.0 10.8 %all-to-all-start = ((bf16[8,1,128]{2,1,0:T(2,128)(2,1)}), bf16[8,1,128]{2,1,0:T(2,128)(2,1)S(1)}, u32[]{:S(2)}, u32[]{:S(2)}) async-start(bf16[8,1,128]{2,1,0:T(2,128)(2,1)} %copy.12), calls=%async_computation | async-start | bytes 8192 | tf_op jit(solution)/shard_map/all_to_all | solution.py:81
  20.8 0.7 copy-start.8
  25.8 4.4 %copy-start.7 = (s32[1,1,8,128]{3,2,1,0:T(8,128)S(1)}, s32[1,1,8,128]{3,2,1,0:T(8,128)}, u32[]{:S(2)}) copy-start(s32[1,1,8,128]{3,2,1,0:T(8,128)} %param.16) | copy-start | bytes 12292
  25.8 12.6 %all-to-all-start.2 = ((bf16[8,128,256]{2,1,0:T(8,128)(2,1)}), bf16[8,128,256]{2,1,0:T(8,128)(2,1)S(1)}, u32[]{:S(2)}, u32[]{:S(2)}) async-start(bf16[8,128,256]{2,1,0:T(8,128)(2,1)} %bitcast.11), calls=%async_computation.2 | async-start | bytes 1048576 | tf_op jit(solution)/shard_map/all_to_all | solution.py:74
  38.4 1.0 copy-start.6
  39.4 1.2 %copy-start.4 = (f32[256]{0:T(256)S(1)}, f32[256]{0:T(256)}, u32[]{:S(2)}) copy-start(f32[256]{0:T(256)} %param.21) | copy-start | bytes 3076
  61.0 17.5 %all-to-all-start.4 = ((f32[4,128,256]{2,1,0:T(8,128)}), f32[4,128,256]{2,1,0:T(8,128)S(1)}, u32[]{:S(2)}, u32[]{:S(2)}) async-start(f32[4,128,256]{2,1,0:T(8,128)} %bitcast.14), calls=%async_computation.4 | async-start | bytes 1048576 | tf_op jit(solution)/shard_map/all_to_all | solution.py:112
where the time goes:
time: 96.6 us; the launch traced here: 96 us
  blocking collectives  35.8 us (37%)
  waiting for transfers between devices  27 us (28%)
  starting transfers between devices  16.8 us (17%)
  matrix products  10.4 us (11%)
  local copies, waits for them, and re-layouts  3.05 us (3%)
  other arithmetic  2.73 us (3%)
    all_to_all x1, blocking collectives, shards(): lax.all_to_all(keep_rate.reshape(tm_count, row_share, breadth), 'tm', spl...  19.4 us
    all_to_all x1, blocking collectives, shards(): lax.all_to_all(history, 'tm', split_axis=0, concat_axis=0, tiled=True)  16.4 us
    all_to_all x1, waiting for transfers between devices, shards(): lax.all_to_all(write_term.reshape(tm_count, row_share, breadth), 'tm', sp...  13.1 us
    all_to_all x1, waiting for transfers between devices, shards(): lax.all_to_all(totals.reshape(blocks, capacity, breadth).astype(jnp.bfloa...  7.75 us
    all_to_all x1, waiting for transfers between devices, shards(): lax.all_to_all(picked.reshape(blocks, capacity, breadth), 'node', split_a...  6.21 us
    all_to_all x1, starting transfers between devices, shards(): lax.all_to_all(counts.reshape(blocks, capacity).astype(jnp.bfloat16), 'no...  4.7 us
    all_to_all x1, starting transfers between devices, shards(): lax.all_to_all(totals.reshape(blocks, capacity, breadth).astype(jnp.bfloa...  4.36 us
    all_to_all x1, starting transfers between devices, shards(): lax.all_to_all(picked.reshape(blocks, capacity, breadth), 'node', split_a...  4.25 us
  transfers between devices with their start and end apart: 4, of which 3 were waited for; matrix products, arithmetic and copies ran while one was open for 9% of the time, Pallas kernels for 0%

commit v1 on v0

v1 whole, which is shorter than its diff:
```python
import functools

import jax
import jax.numpy as jnp
from jax import lax
from jax.experimental import pallas as pl
from jax.experimental.pallas import tpu as pltpu
from jax.sharding import PartitionSpec as P

PIECES = 2
BASE = 32.0
VMEM_LIMIT = 20 << 20
F32 = jnp.float32
BF16 = jnp.bfloat16


def dot(a, b, dims=((1,), (0,))):
    return lax.dot_general(a, b, (dims, ((), ())), preferred_element_type=F32)


def call(kernel, outs, *args, flops=0):
    outs = [jax.ShapeDtypeStruct(shape, dtype) for shape, dtype in outs]
    moved = sum(x.size * x.dtype.itemsize for x in [*args, *outs])
    return pl.pallas_call(
        kernel,
        out_shape=outs,
        in_specs=[pl.BlockSpec(memory_space=pltpu.VMEM)] * len(args),
        out_specs=[pl.BlockSpec(memory_space=pltpu.VMEM)] * len(outs),
        cost_estimate=pl.CostEstimate(flops=flops, bytes_accessed=moved, transcendentals=0),
        compiler_params=pltpu.CompilerParams(vmem_limit_bytes=VMEM_LIMIT),
    )(*args)


def columns_of(row):
    return jnp.transpose(jnp.broadcast_to(row, (row.shape[1], row.shape[1])))


def hot_rows(row, width):
    count = row.shape[1]
    column = jnp.concatenate([columns_of(row)] * (width // count), 1)
    lanes = lax.broadcasted_iota(jnp.int32, (count, width), 1)
    return jnp.where(column == lanes, 1.0, 0.0).astype(BF16)


def hot_columns(row, start, height):
    sublanes = lax.broadcasted_iota(jnp.int32, (height, row.shape[1]), 0) + start
    return jnp.where(row == sublanes, 1.0, 0.0).astype(BF16)


def pick_kernel(side, lists_ref, memory_ref, out_ref):
    me = lax.axis_index("node")
    stale = memory_ref[...].astype(BF16)
    for chip in range(out_ref.shape[0]):
        row = lists_ref[pl.ds(me ^ (2 * chip + side), 1), :]
        hot = hot_rows(row, memory_ref.shape[0])
        out_ref[chip] = dot(hot, stale).astype(BF16)


def prep_kernel(
    slots_ref, time_ref, freq_ref, weight_ref, bias_ref, hot_ref, turned_ref, base_ref, code_ref
):
    me = lax.axis_index("node")
    slots_all, ends = hot_ref.shape
    blocks, capacity = code_ref.shape[0], code_ref.shape[2] // 2
    slots = slots_ref[...]
    slots = ((slots // capacity) ^ me) * capacity + slots % capacity
    counts = jnp.zeros((8, slots_all), F32)
    ones = jnp.ones((8, capacity), BF16)
    for i in range(ends // capacity):
        rows = slice(i * capacity, (i + 1) * capacity)
        turned = hot_rows(slots[:, rows], slots_all)
        turned_ref[rows] = turned
        counts = counts + dot(ones, turned)
    for j in range(blocks):
        hot_ref[j * capacity : (j + 1) * capacity] = hot_columns(slots, j * capacity, capacity)
    upper = jnp.floor(counts * (1.0 / BASE))
    lower = counts - BASE * upper
    for j in range(blocks):
        lanes = slice(j * capacity, (j + 1) * capacity)
        code = jnp.concatenate([upper[:, lanes], lower[:, lanes]], 1)
        code_ref[j] = code[: code_ref.shape[1]].astype(BF16)
    width = freq_ref.shape[1]
    stale_part = weight_ref.shape[0] - width
    for i in range(time_ref.shape[1] // width):
        rows = slice(i * width, (i + 1) * width)
        encoding = jnp.cos(columns_of(time_ref[:, rows]) * freq_ref[...]).astype(BF16)
        base_ref[rows] = dot(encoding, weight_ref[stale_part:]) + bias_ref[...]


def message_kernel(chips, *refs):
    tables, (turned_ref, hot_ref, weight_ref, base_ref, code_ref) = refs[:-7], refs[-7:-2]
    other_ref, message_ref = refs[-2:]
    capacity, breadth = tables[0].shape
    rows = None
    for j, table in enumerate(tables[:2]):
        part = dot(turned_ref[:, j * capacity : (j + 1) * capacity], table[...])
        rows = part if rows is None else rows + part
    for chip in range(1, chips):
        lanes = slice(2 * chip * capacity, 2 * (chip + 1) * capacity)
        table = tables[chip + 1][...].reshape(2 * capacity, breadth)
        rows = rows + dot(turned_ref[:, lanes], table)
    rows = rows.astype(BF16)
    events = rows.shape[0] // 2
    first = dot(rows, weight_ref[:breadth])
    second = dot(rows, weight_ref[breadth : 2 * breadth])
    base = base_ref[...]
    message_ref[:events] = jnp.maximum(first[:events] + second[events:] + base, 0.0).astype(BF16)
    message_ref[events:] = jnp.maximum(first[events:] + second[:events] + base, 0.0).astype(BF16)
    messages = message_ref[...]
    for chip in range(chips):
        j = 2 * chip + 1
        sums = dot(hot_ref[j * capacity : (j + 1) * capacity], messages)
        other_ref[chip, :capacity] = sums.astype(BF16)
        other_ref[chip, capacity:] = code_ref[j]


def own_kernel(hot_ref, message_ref, own_ref):
    messages = message_ref[...]
    chips, capacity, _ = own_ref.shape
    for chip in range(chips):
        rows = slice(2 * chip * capacity, (2 * chip + 1) * capacity)
        own_ref[chip] = dot(hot_ref[rows], messages).astype(BF16)


def rows_kernel(lists_ref, rowhot_ref):
    me = lax.axis_index("node")
    blocks, capacity = lists_ref.shape
    for j in range(blocks):
        row = lists_ref[pl.ds(me ^ j, 1), :]
        rowhot_ref[:, j * capacity : (j + 1) * capacity] = hot_columns(
            row, 0, rowhot_ref.shape[0]
        )


def mean_kernel(chips, rowhot_ref, *refs):
    loads, mean_ref = refs[:-1], refs[-1]
    breadth = mean_ref.shape[1]
    pair = rowhot_ref.shape[1] // chips
    capacity = pair // 2
    totals, counts = None, None
    for chip, load in enumerate(loads):
        hot = rowhot_ref[:, chip * pair : (chip + 1) * pair]
        part = dot(hot, load[:pair])
        first = load[pair : pair + 1].astype(F32)
        second = load[pair + 1 : pair + 2].astype(F32)
        upper = jnp.concatenate([first[:, :capacity], second[:, :capacity]], 1)
        lower = jnp.concatenate([first[:, capacity:], second[:, capacity:]], 1)
        code = jnp.concatenate(
            [
                jnp.broadcast_to(upper, (breadth // 2, pair)),
                jnp.broadcast_to(lower, (breadth // 2, pair)),
            ],
            0,
        ).astype(BF16)
        count = dot(hot, code, ((1,), (1,)))
        totals = part if totals is None else totals + part
        counts = count if counts is None else counts + count
    counts = BASE * counts[:, : breadth // 2] + counts[:, breadth // 2 :]
    counts = jnp.concatenate([counts, counts], 1)
    mean = jnp.where(counts > 0.0, totals / jnp.maximum(counts, 1.0), -1.0)
    mean_ref[...] = mean.astype(BF16)


def gates(mean_code, gate_weight, update_bias):
    breadth = mean_code.shape[1]
    terms = dot(mean_code, gate_weight)
    update = jax.nn.sigmoid(terms[:, :breadth] + update_bias)
    candidate = jnp.tanh(terms[:, breadth:])
    touched = mean_code.astype(F32) >= 0.0
    keep_rate = jnp.where(touched, 1.0 - update, 1.0)
    write_term = jnp.where(touched, update * candidate, 0.0)
    return keep_rate, write_term


def hubs_of(periods):
    return (periods - 1) // 2, (periods - 1) // 2 + 1


def rounds_of(first, second):
    second = second[1:] + second[:1]
    longest = max(len(first), len(second))
    first = first + [None] * (longest - len(first))
    second = second + [None] * (longest - len(second))
    return list(zip(first, second))


def plan_of(periods):
    low, high = hubs_of(periods)
    came = rounds_of(
        [t for t in range(periods - 1) if t != low], [t for t in range(periods - 1) if t != high]
    )
    went = rounds_of(
        [t for t in range(1, periods) if t != low], [t for t in range(1, periods) if t != high]
    )
    return low, high, came, went


def hub_kernel(periods, own_ref, memory_ref, weight_ref, bias_ref, *refs):
    hub_low, hub_high, came, went = plan_of(periods)
    means, outs = refs[: len(came)], refs[len(came) :]
    is_high = lax.axis_index("tm") == hub_high
    own_gates = gates(own_ref[...], weight_ref[...], bias_ref[...])
    came_gates = [gates(mean[...], weight_ref[...], bias_ref[...]) for mean in means]
    state = memory_ref[...]
    states = []
    for t in range(periods - 1):
        low = next((g for g, r in zip(came_gates, came) if r[0] == t), own_gates)
        high = next((g for g, r in zip(came_gates, came) if r[1] == t), own_gates)
        rate, term = (jnp.where(is_high, b, a) for a, b in zip(low, high))
        state = rate * state + term
        states.append(state)
    for (low, high), out in zip(went, outs):
        low_state = states[(high if low is None else low) - 1]
        high_state = states[(low if high is None else high) - 1]
        out[...] = jnp.where(is_high, high_state, low_state)
    outs[-1][...] = jnp.where(is_high, states[hub_high - 1], states[max(hub_low - 1, 0)])


def node_swap(value, distance):
    size = lax.axis_size("node")
    return lax.ppermute(value, "node", [(i, i ^ distance) for i in range(size)])


def shards(
    memory,
    src_slot,
    dst_slot,
    event_time,
    touched_rows,
    time_freq,
    msg_weight,
    msg_bias,
    gate_weight,
    update_bias,
):
    period = lax.axis_index("tm")
    periods = lax.axis_size("tm")
    blocks, capacity = touched_rows.shape[2:]
    node_rows, breadth = memory.shape
    events = src_slot.shape[2]
    chips = blocks // 2
    lists = touched_rows[0, 0]

    def picked(side):
        return call(
            functools.partial(pick_kernel, side),
            [((chips, capacity, breadth), BF16)],
            lists,
            memory,
            flops=chips * capacity * breadth * node_rows * 2,
        )[0]

    from_partner = node_swap(picked(1), 1)
    own = picked(0)
    sources, targets, times, from_partner = lax.optimization_barrier(
        (src_slot[0], dst_slot[0], event_time[0], from_partner)
    )
    tables = [own[0], from_partner[0]] + [
        node_swap(jnp.stack([own[chip], from_partner[chip]]), 2 * chip)
        for chip in range(1, chips)
    ]
    ends = 2 * events
    slots = blocks * capacity
    hot, turned, base, code = call(
        prep_kernel,
        [
            ((slots, ends), BF16),
            ((ends, slots), BF16),
            ((events, breadth), F32),
            ((blocks, 1, 2 * capacity), BF16),
        ],
        jnp.concatenate([sources, targets], 1),
        times,
        time_freq[None],
        msg_weight,
        msg_bias[None],
    )
    other, messages = call(
        functools.partial(message_kernel, chips),
        [((chips, capacity + 1, breadth), BF16), ((ends, breadth), BF16)],
        *tables,
        turned,
        hot,
        msg_weight,
        base,
        code,
        flops=ends * slots * breadth * 3,
    )
    partner = node_swap(other, 1)
    own_sums = call(
        own_kernel,
        [((chips, capacity, breadth), BF16)],
        hot,
        messages,
        flops=ends * slots * breadth,
    )[0]
    loads = []
    for chip in range(chips):
        load = jnp.concatenate(
            [own_sums[chip], partner[chip, :capacity], code[2 * chip], partner[chip, capacity:]], 0
        )
        loads.append(node_swap(load, 2 * chip) if chip else load)
    rowhot = call(rows_kernel, [((node_rows, slots), BF16)], lists)[0]
    mean_code = call(
        functools.partial(mean_kernel, chips),
        [((node_rows, breadth), BF16)],
        rowhot,
        *loads,
        flops=4 * node_rows * slots * breadth,
    )[0]

    half = node_rows // 2
    size = half // PIECES
    hub_low, hub_high, came, went = plan_of(periods)
    is_high = period == hub_high
    bias = update_bias[None]
    got_means = []
    for piece in range(PIECES):
        got = []
        for low, high in came:
            pairs = [(s, h) for s, h in ((low, hub_low), (high, hub_high)) if s is not None]
            start = jnp.where(period == (-1 if high is None else high), half, 0) + piece * size
            sent = lax.dynamic_slice_in_dim(mean_code, start, size, 0)
            got.append(lax.ppermute(sent, "tm", pairs))
        got_means.append(got)
    keep, write = gates(mean_code, gate_weight, bias)
    before_low, before_high = [], []
    for piece in range(PIECES):
        start = jnp.where(is_high, half, 0) + piece * size
        outs = call(
            functools.partial(hub_kernel, periods),
            [((size, breadth), F32)] * (len(went) + 1),
            lax.dynamic_slice_in_dim(mean_code, start, size, 0),
            lax.dynamic_slice_in_dim(memory, start, size, 0),
            gate_weight,
            bias,
            *got_means[piece],
            flops=2 * (len(came) + 1) * size * breadth * breadth * 2,
        )
        first = piece * size
        prior_low = jnp.where(period == 0, memory[first : first + size], outs[-1])
        first += half
        prior_high = jnp.where(period == 0, memory[first : first + size], outs[-1])
        for r, (low, high) in enumerate(went):
            pairs = [(h, d) for d, h in ((low, hub_low), (high, hub_high)) if d is not None]
            got = lax.ppermute(outs[r].astype(jnp.float16), "tm", pairs)
            got = got.astype(F32)
            if low is not None:
                prior_low = jnp.where(period == low, got, prior_low)
            if high is not None:
                prior_high = jnp.where(period == high, got, prior_high)
        before_low.append(prior_low)
        before_high.append(prior_high)
    before = jnp.concatenate(before_low + before_high, 0)
    return (keep * before + write)[None]


def solution(mesh):
    return jax.shard_map(
        shards,
        mesh=mesh,
        in_specs=(
            P("node", None),
            P("tm", "node", None),
            P("tm", "node", None),
            P("tm", "node", None),
            P("tm", "node", None, None),
            P(),
            P(),
            P(),
            P(),
            P(),
        ),
        out_specs=P("tm", "node", None),
        check_vma=False,
    )
```

time: 96.6 us -> 55.3 us (0.57)
  the two profiles are of different devices: /device:TPU:2 before, /device:TPU:16 now
where the time goes in v1:
time: 55.3 us; the launch traced here: 55 us
  starting transfers between devices  28.3 us (51%)
  waiting for transfers between devices  15.5 us (28%)
  Pallas kernels  7.28 us (13%)
  local copies, waits for them, and re-layouts  1.96 us (4%)
  other arithmetic  1.26 us (2%)
    ppermute x4, starting transfers between devices, shards(): got.append(lax.ppermute(sent, 'tm', pairs))  11.7 us
    ppermute x8, waiting for transfers between devices, node_swap(): return lax.ppermute(value, 'node', [(i, i ^ distance) for i in range(size)])  11.6 us
    ppermute x4, starting transfers between devices, shards(): got = lax.ppermute(outs[r].astype(jnp.float16), 'tm', pairs)  9.06 us
    ppermute x8, starting transfers between devices, node_swap(): return lax.ppermute(value, 'node', [(i, i ^ distance) for i in range(size)])  7.51 us
    pallas_call x9, Pallas kernels, call(): pl.pallas_call(kernel, out_shape=outs, in_specs=[pl.BlockSpec(memory_spac...  7.28 us
    ppermute x4, waiting for transfers between devices, shards(): got = lax.ppermute(outs[r].astype(jnp.float16), 'tm', pairs)  3.91 us
    unnamed x24, local copies, waits for them, and re-layouts  1.8 us
  transfers between devices with their start and end apart: 16, of which 8 were waited for; matrix products, arithmetic and copies ran while one was open for 1% of the time, Pallas kernels for 7%

profile of v1, /device:TPU:16, one launch (start us, length us, event | category | flops | bytes accessed | tf_op | source)
XLA Modules:
  0.0 55.0 jit_solution(13025549907125444513)
XLA Ops:
  0.0 1.1 %copy-done = f32[512,256]{1,0:T(8,128)S(1)} copy-done((f32[512,256]{1,0:T(8,128)S(1)}, f32[512,256]{1,0:T(8,128)}, u32[]{:S(2)}) %copy-start) | copy-done | bytes 524312
  1.1 0.7 %copy-done.4 = s32[1,1,8,128]{3,2,1,0:T(8,128)S(1)} copy-done((s32[1,1,8,128]{3,2,1,0:T(8,128)S(1)}, s32[1,1,8,128]{3,2,1,0:T(8,128)}, u32[]{:S(2)}) %copy-start.4) | copy-done | bytes 4120
  1.8 0.4 shard_map.101
  2.2 0.4 shard_map.103
  2.6 1.1 %collective-permute-done = bf16[4,128,256]{2,1,0:T(8,128)(2,1)S(1)} collective-permute-done((bf16[4,128,256]{2,1,0:T(8,128)(2,1)S(1)}, bf16[4,128,256]{2,1,0:T(8,128)(2,1)S(1)}, u32[]{:S(2)}, u32[]{:S(2)}) %collective-permute-start) | collective-permute-done | bytes 262176 | tf_op jit(solution)/shard_map/ppermute | solution.py:221
  3.8 1.6 %collective-permute-start.1 = (bf16[2,128,256]{2,1,0:T(8,128)(2,1)S(1)}, bf16[2,128,256]{2,1,0:T(8,128)(2,1)S(1)}, u32[]{:S(2)}, u32[]{:S(2)}) collective-permute-start(bf16[2,128,256]{2,1,0:T(8,128)(2,1)S(1)} %pad_maximum_fusion.4), channel_id=1, source_target_pairs={{0,2},{1,3},{2,0},{3,1},{4,6},{5,7},{6,4},{7,5},{8,10},{9,11},{10,... | collective-permute-start | bytes 393224 | tf_op jit(solution)/shard_map/ppermute | solution.py:221
  5.4 1.6 %collective-permute-start.2 = (bf16[2,128,256]{2,1,0:T(8,128)(2,1)S(1)}, bf16[2,128,256]{2,1,0:T(8,128)(2,1)S(1)}, u32[]{:S(2)}, u32[]{:S(2)}) collective-permute-start(bf16[2,128,256]{2,1,0:T(8,128)(2,1)S(1)} %pad_maximum_fusion.5), channel_id=1, source_target_pairs={{0,4},{1,5},{2,6},{3,7},{4,0},{5,1},{6,2},{7,3},{8,12},{9,13},{10,... | collective-permute-start | bytes 393224 | tf_op jit(solution)/shard_map/ppermute | solution.py:221
  7.0 0.5 collective-permute-start.3
  7.5 2.0 %shard_map.102 = (bf16[1024,1024]{1,0:T(8,128)(2,1)S(1)}, bf16[1024,1024]{1,0:T(8,128)(2,1)S(1)}, f32[512,256]{1,0:T(8,128)S(1)}, bf16[8,1,256]{2,1,0:T(2,128)(2,1)S(1)}) custom-call(s32[1,1024]{1,0:T(1,128)S(1)} %pad_add_fusion.slots_ref, f32[1,512]{1,0:T(1,128)S(1)} %bitcast.52, f32[1,128]{1,0:T(1,128)S(1)} %bitcast.54, bf16[640,256]{1,0:T(8,128)(2,1)S(1)} %copy-done.3, ...), custom_call_target="tpu_custom_call" | custom-call | bytes 5058048 | tf_op jit(solution)/shard_map/pallas_call | solution.py:24
  9.6 3.9 %collective-permute-done.2.refs_3_ = bf16[2,128,256]{2,1,0:T(8,128)(2,1)S(1)} collective-permute-done((bf16[2,128,256]{2,1,0:T(8,128)(2,1)S(1)}, bf16[2,128,256]{2,1,0:T(8,128)(2,1)S(1)}, u32[]{:S(2)}, u32[]{:S(2)}) %collective-permute-start.2) | collective-permute-done | bytes 131104 | tf_op jit(solution)/shard_map/ppermute | solution.py:221
  13.5 2.4 %shard_map.104 = (bf16[4,129,256]{2,1,0:T(8,128)(2,1)S(1)}, bf16[1024,256]{1,0:T(8,128)(2,1)S(1)}) custom-call(bf16[128,256]{1,0:T(8,128)(2,1)S(1)} %get-tuple-element.66.refs_0_, bf16[128,256]{1,0:T(8,128)(2,1)S(1)} %get-tuple-element.70.refs_1_, bf16[2,128,256]{2,1,0:T(8,128)(2,1)S(1)} %collective-permute-done.1.refs_2_, ...), custom_call_target="tpu_custom_call" | custom-call | flops 805306368 | bytes 6363136 | tf_op jit(solution)/shard_map/pallas_call | solution.py:24
  16.0 0.4 shard_map.105
  16.5 1.0 %collective-permute-done.4 = bf16[4,129,256]{2,1,0:T(8,128)(2,1)S(1)} collective-permute-done((bf16[4,129,256]{2,1,0:T(8,128)(2,1)S(1)}, bf16[4,129,256]{2,1,0:T(8,128)(2,1)S(1)}, u32[]{:S(2)}, u32[]{:S(2)}) %collective-permute-start.4) | collective-permute-done | bytes 264224 | tf_op jit(solution)/shard_map/ppermute | solution.py:221
  17.6 1.5 %collective-permute-start.7 = (bf16[258,256]{1,0:T(8,128)(2,1)S(1)}, bf16[258,256]{1,0:T(8,128)(2,1)S(1)}, u32[]{:S(2)}, u32[]{:S(2)}) collective-permute-start(bf16[258,256]{1,0:T(8,128)(2,1)S(1)} %pad_maximum_fusion.3), channel_id=1, source_target_pairs={{0,6},{1,7},{2,4},{3,5},{4,2},{5,3},{6,0},{7,1},{8,14},{9,15},{10,... | collective-permute-start | bytes 396296 | tf_op jit(solution)/shard_map/ppermute | solution.py:221
  19.1 1.2 %collective-permute-start.6 = (bf16[258,256]{1,0:T(8,128)(2,1)S(1)}, bf16[258,256]{1,0:T(8,128)(2,1)S(1)}, u32[]{:S(2)}, u32[]{:S(2)}) collective-permute-start(bf16[258,256]{1,0:T(8,128)(2,1)S(1)} %pad_maximum_fusion.2), channel_id=1, source_target_pairs={{0,4},{1,5},{2,6},{3,7},{4,0},{5,1},{6,2},{7,3},{8,12},{9,13},{10,... | collective-permute-start | bytes 396296 | tf_op jit(solution)/shard_map/ppermute | solution.py:221
  20.4 0.9 %collective-permute-start.5 = (bf16[258,256]{1,0:T(8,128)(2,1)S(1)}, bf16[258,256]{1,0:T(8,128)(2,1)S(1)}, u32[]{:S(2)}, u32[]{:S(2)}) collective-permute-start(bf16[258,256]{1,0:T(8,128)(2,1)S(1)} %pad_maximum_fusion.1), channel_id=1, source_target_pairs={{0,2},{1,3},{2,0},{3,1},{4,6},{5,7},{6,4},{7,5},{8,10},{9,11},{10,... | collective-permute-start | bytes 396296 | tf_op jit(solution)/shard_map/ppermute | solution.py:221
  21.3 0.3 shard_map.100.rowhot_ref
  21.7 3.3 %collective-permute-done.7.refs_3_ = bf16[258,256]{1,0:T(8,128)(2,1)S(1)} collective-permute-done((bf16[258,256]{1,0:T(8,128)(2,1)S(1)}, bf16[258,256]{1,0:T(8,128)(2,1)S(1)}, u32[]{:S(2)}, u32[]{:S(2)}) %collective-permute-start.7) | collective-permute-done | bytes 132128 | tf_op jit(solution)/shard_map/ppermute | solution.py:221
  25.0 2.0 %collective-permute-done.6.refs_2_ = bf16[258,256]{1,0:T(8,128)(2,1)S(1)} collective-permute-done((bf16[258,256]{1,0:T(8,128)(2,1)S(1)}, bf16[258,256]{1,0:T(8,128)(2,1)S(1)}, u32[]{:S(2)}, u32[]{:S(2)}) %collective-permute-start.6) | collective-permute-done | bytes 132128 | tf_op jit(solution)/shard_map/ppermute | solution.py:221
  27.2 0.7 %shard_map.106 = bf16[512,256]{1,0:T(8,128)(2,1)S(1)} custom-call(bf16[512,1024]{1,0:T(8,128)(2,1)S(1)} %shard_map.100.rowhot_ref, bf16[258,256]{1,0:T(8,128)(2,1)S(1)} %pad_maximum_fusion.refs_0_, bf16[258,256]{1,0:T(8,128)(2,1)S(1)} %collective-permute-done.5.refs_1_, bf16[258,256]{1,0:T(8,128)(2,1)S(1)} %collective-permute-done.6.refs_2_, ...), custom_call_target="tpu_custom_call" | custom-call | flops 536870912 | bytes 1839104 | tf_op jit(solution)/shard_map/pallas_call | solution.py:24
  27.9 1.3 %collective-permute-start.12 = (bf16[128,256]{1,0:T(8,128)(2,1)S(1)}, bf16[128,256]{1,0:T(8,128)(2,1)S(1)}, u32[]{:S(2)}, u32[]{:S(2)}) collective-permute-start(bf16[128,256]{1,0:T(8,128)(2,1)S(1)} %get-tuple-element.55), channel_id=1, source_target_pairs={{0,8},{8,16},{1,9},{9,17},{2,10},{10,18},{3,11},{11,19},{4,12},{12... | collective-permute-start | bytes 196616 | tf_op jit(solution)/shard_map/ppermute | solution.py:324
  29.2 4.6 %collective-permute-start.13 = (bf16[128,256]{1,0:T(8,128)(2,1)S(1)}, bf16[128,256]{1,0:T(8,128)(2,1)S(1)}, u32[]{:S(2)}, u32[]{:S(2)}) collective-permute-start(bf16[128,256]{1,0:T(8,128)(2,1)S(1)} %get-tuple-element.54), channel_id=1, source_target_pairs={{16,8},{0,16},{17,9},{1,17},{18,10},{2,18},{19,11},{3,19},{20,12},... | collective-permute-start | bytes 196616 | tf_op jit(solution)/shard_map/ppermute | solution.py:324
  33.8 1.3 %collective-permute-start.8 = (bf16[128,256]{1,0:T(8,128)(2,1)S(1)}, bf16[128,256]{1,0:T(8,128)(2,1)S(1)}, u32[]{:S(2)}, u32[]{:S(2)}) collective-permute-start(bf16[128,256]{1,0:T(8,128)(2,1)S(1)} %get-tuple-element.57), channel_id=1, source_target_pairs={{0,8},{8,16},{1,9},{9,17},{2,10},{10,18},{3,11},{11,19},{4,12},{12... | collective-permute-start | bytes 196616 | tf_op jit(solution)/shard_map/ppermute | solution.py:324
  35.1 4.6 %collective-permute-start.9 = (bf16[128,256]{1,0:T(8,128)(2,1)S(1)}, bf16[128,256]{1,0:T(8,128)(2,1)S(1)}, u32[]{:S(2)}, u32[]{:S(2)}) collective-permute-start(bf16[128,256]{1,0:T(8,128)(2,1)S(1)} %get-tuple-element.53), channel_id=1, source_target_pairs={{16,8},{0,16},{17,9},{1,17},{18,10},{2,18},{19,11},{3,19},{20,12},... | collective-permute-start | bytes 196616 | tf_op jit(solution)/shard_map/ppermute | solution.py:324
  39.8 0.4 shard_map.108
  40.1 1.3 %collective-permute-start.14 = (f16[128,256]{1,0:T(8,128)(2,1)S(1)}, f16[128,256]{1,0:T(8,128)(2,1)S(1)}, u32[]{:S(2)}, u32[]{:S(2)}) collective-permute-start(f16[128,256]{1,0:T(8,128)(2,1)S(1)} %convert_element_type.32), channel_id=1, source_target_pairs={{8,24},{16,8},{9,25},{17,9},{10,26},{18,10},{11,27},{19,11},{12,28... | collective-permute-start | bytes 196616 | tf_op jit(solution)/shard_map/ppermute | solution.py:346
  41.5 1.9 %collective-permute-start.15 = (f16[128,256]{1,0:T(8,128)(2,1)S(1)}, f16[128,256]{1,0:T(8,128)(2,1)S(1)}, u32[]{:S(2)}, u32[]{:S(2)}) collective-permute-start(f16[128,256]{1,0:T(8,128)(2,1)S(1)} %convert_element_type.34), channel_id=1, source_target_pairs={{8,16},{16,24},{9,17},{17,25},{10,18},{18,26},{11,19},{19,27},{12,... | collective-permute-start | bytes 196616 | tf_op jit(solution)/shard_map/ppermute | solution.py:346
  43.4 0.4 shard_map.107
  43.8 3.9 %collective-permute-start.10 = (f16[128,256]{1,0:T(8,128)(2,1)S(1)}, f16[128,256]{1,0:T(8,128)(2,1)S(1)}, u32[]{:S(2)}, u32[]{:S(2)}) collective-permute-start(f16[128,256]{1,0:T(8,128)(2,1)S(1)} %convert_element_type.28), channel_id=1, source_target_pairs={{8,24},{16,8},{9,25},{17,9},{10,26},{18,10},{11,27},{19,11},{12,28... | collective-permute-start | bytes 196616 | tf_op jit(solution)/shard_map/ppermute | solution.py:346
  47.8 1.9 %collective-permute-start.11 = (f16[128,256]{1,0:T(8,128)(2,1)S(1)}, f16[128,256]{1,0:T(8,128)(2,1)S(1)}, u32[]{:S(2)}, u32[]{:S(2)}) collective-permute-start(f16[128,256]{1,0:T(8,128)(2,1)S(1)} %convert_element_type.30), channel_id=1, source_target_pairs={{8,16},{16,24},{9,17},{17,25},{10,18},{18,26},{11,19},{19,27},{12,... | collective-permute-start | bytes 196616 | tf_op jit(solution)/shard_map/ppermute | solution.py:346
  50.0 3.9 %collective-permute-done.11 = f16[128,256]{1,0:T(8,128)(2,1)S(1)} collective-permute-done((f16[128,256]{1,0:T(8,128)(2,1)S(1)}, f16[128,256]{1,0:T(8,128)(2,1)S(1)}, u32[]{:S(2)}, u32[]{:S(2)}) %collective-permute-start.11) | collective-permute-done | bytes 65568 | tf_op jit(solution)/shard_map/ppermute | solution.py:346
  54.0 1.0 %fusion.3 = f32[1,512,256]{2,1,0:T(8,128)} fusion(f32[512,512]{1,0:T(8,128)S(1)} %fusion.10, f32[128,256]{1,0:T(8,128)S(1)} %get-tuple-element.41, f32[128,256]{1,0:T(8,128)S(1)} %get-tuple-element.38, f32[128,256]{1,0:T(8,128)S(1)} %get-tuple-element.42, f32[128,256]{1,0:T(8,128)S(1)} %get-tuple-element.37, bf16[512,256]{1,0:T(8,128)(2,1)S(1)} %shard_map.106, ...), kind=kLoop, calls=%fused_computation.4 | loop fusion | flops 1966080 | bytes 2360320 | tf_op jit(solution)/shard_map/broadcast_in_dim | solution.py:355
  (56 shorter events, 1.1 us)
Async XLA Ops:
  0.0 7.5 %copy-start.9 = (f32[128]{0:T(128)S(1)}, f32[128]{0:T(128)}, u32[]{:S(2)}) copy-start(f32[128]{0:T(128)} %param.15) | copy-start | bytes 1540
  0.0 7.5 %copy-start.8 = (f32[256]{0:T(256)S(1)}, f32[256]{0:T(256)}, u32[]{:S(2)}) copy-start(f32[256]{0:T(256)} %param.17) | copy-start | bytes 3076
  0.0 1.1 %copy-start = (f32[512,256]{1,0:T(8,128)S(1)}, f32[512,256]{1,0:T(8,128)}, u32[]{:S(2)}) copy-start(f32[512,256]{1,0:T(8,128)} %memory_ref.3) | copy-start | bytes 1572868
  1.1 0.7 %copy-start.4 = (s32[1,1,8,128]{3,2,1,0:T(8,128)S(1)}, s32[1,1,8,128]{3,2,1,0:T(8,128)}, u32[]{:S(2)}) copy-start(s32[1,1,8,128]{3,2,1,0:T(8,128)} %param.14) | copy-start | bytes 12292
  1.8 5.7 %copy-start.10 = (s32[1,1,512]{2,1,0:T(1,128)S(1)}, s32[1,1,512]{2,1,0:T(1,128)}, u32[]{:S(2)}) copy-start(s32[1,1,512]{2,1,0:T(1,128)} %param.12) | copy-start | bytes 6148
  1.8 5.7 %copy-start.11 = (s32[1,1,512]{2,1,0:T(1,128)S(1)}, s32[1,1,512]{2,1,0:T(1,128)}, u32[]{:S(2)}) copy-start(s32[1,1,512]{2,1,0:T(1,128)} %param.11) | copy-start | bytes 6148
  1.8 5.8 %copy-start.3 = (bf16[640,256]{1,0:T(8,128)(2,1)S(1)}, bf16[640,256]{1,0:T(8,128)(2,1)}, u32[]{:S(2)}) copy-start(bf16[640,256]{1,0:T(8,128)(2,1)} %refs_7_.1) | copy-start | bytes 983044
  1.8 5.8 %copy-start.7 = (f32[1,1,512]{2,1,0:T(1,128)S(1)}, f32[1,1,512]{2,1,0:T(1,128)}, u32[]{:S(2)}) copy-start(f32[1,1,512]{2,1,0:T(1,128)} %param.13) | copy-start | bytes 6148
  2.1 1.6 %collective-permute-start = (bf16[4,128,256]{2,1,0:T(8,128)(2,1)S(1)}, bf16[4,128,256]{2,1,0:T(8,128)(2,1)S(1)}, u32[]{:S(2)}, u32[]{:S(2)}) collective-permute-start(bf16[4,128,256]{2,1,0:T(8,128)(2,1)S(1)} %shard_map.101), channel_id=1, source_target_pairs={{0,1},{1,0},{2,3},{3,2},{4,5},{5,4},{6,7},{7,6},{8,9},{9,8},{10,11... | collective-permute-start | bytes 786440 | tf_op jit(solution)/shard_map/ppermute | solution.py:221
  3.8 5.8 %collective-permute-start.1 = (bf16[2,128,256]{2,1,0:T(8,128)(2,1)S(1)}, bf16[2,128,256]{2,1,0:T(8,128)(2,1)S(1)}, u32[]{:S(2)}, u32[]{:S(2)}) collective-permute-start(bf16[2,128,256]{2,1,0:T(8,128)(2,1)S(1)} %pad_maximum_fusion.4), channel_id=1, source_target_pairs={{0,2},{1,3},{2,0},{3,1},{4,6},{5,7},{6,4},{7,5},{8,10},{9,11},{10,... | collective-permute-start | bytes 393224 | tf_op jit(solution)/shard_map/ppermute | solution.py:221
  5.4 8.1 %collective-permute-start.2 = (bf16[2,128,256]{2,1,0:T(8,128)(2,1)S(1)}, bf16[2,128,256]{2,1,0:T(8,128)(2,1)S(1)}, u32[]{:S(2)}, u32[]{:S(2)}) collective-permute-start(bf16[2,128,256]{2,1,0:T(8,128)(2,1)S(1)} %pad_maximum_fusion.5), channel_id=1, source_target_pairs={{0,4},{1,5},{2,6},{3,7},{4,0},{5,1},{6,2},{7,3},{8,12},{9,13},{10,... | collective-permute-start | bytes 393224 | tf_op jit(solution)/shard_map/ppermute | solution.py:221
  7.0 6.5 %collective-permute-start.3 = (bf16[2,128,256]{2,1,0:T(8,128)(2,1)S(1)}, bf16[2,128,256]{2,1,0:T(8,128)(2,1)S(1)}, u32[]{:S(2)}, u32[]{:S(2)}) collective-permute-start(bf16[2,128,256]{2,1,0:T(8,128)(2,1)S(1)} %pad_maximum_fusion.6), channel_id=1, source_target_pairs={{0,6},{1,7},{2,4},{3,5},{4,2},{5,3},{6,0},{7,1},{8,14},{9,15},{10,... | collective-permute-start | bytes 393224 | tf_op jit(solution)/shard_map/ppermute | solution.py:221
  15.9 1.6 %collective-permute-start.4 = (bf16[4,129,256]{2,1,0:T(8,128)(2,1)S(1)}, bf16[4,129,256]{2,1,0:T(8,128)(2,1)S(1)}, u32[]{:S(2)}, u32[]{:S(2)}) collective-permute-start(bf16[4,129,256]{2,1,0:T(8,128)(2,1)S(1)} %get-tuple-element.30), channel_id=1, source_target_pairs={{0,1},{1,0},{2,3},{3,2},{4,5},{5,4},{6,7},{7,6},{8,9},{9,8},{10,11... | collective-permute-start | bytes 792584 | tf_op jit(solution)/shard_map/ppermute | solution.py:221
  16.0 5.3 %copy-start.5 = (s32[1,1,8,128]{3,2,1,0:T(8,128)S(1)}, s32[1,1,8,128]{3,2,1,0:T(8,128)}, u32[]{:S(2)}) copy-start(s32[1,1,8,128]{3,2,1,0:T(8,128)} %param.14) | copy-start | bytes 12292
  17.6 7.4 %collective-permute-start.7 = (bf16[258,256]{1,0:T(8,128)(2,1)S(1)}, bf16[258,256]{1,0:T(8,128)(2,1)S(1)}, u32[]{:S(2)}, u32[]{:S(2)}) collective-permute-start(bf16[258,256]{1,0:T(8,128)(2,1)S(1)} %pad_maximum_fusion.3), channel_id=1, source_target_pairs={{0,6},{1,7},{2,4},{3,5},{4,2},{5,3},{6,0},{7,1},{8,14},{9,15},{10,... | collective-permute-start | bytes 396296 | tf_op jit(solution)/shard_map/ppermute | solution.py:221
  19.1 7.9 %collective-permute-start.6 = (bf16[258,256]{1,0:T(8,128)(2,1)S(1)}, bf16[258,256]{1,0:T(8,128)(2,1)S(1)}, u32[]{:S(2)}, u32[]{:S(2)}) collective-permute-start(bf16[258,256]{1,0:T(8,128)(2,1)S(1)} %pad_maximum_fusion.2), channel_id=1, source_target_pairs={{0,4},{1,5},{2,6},{3,7},{4,0},{5,1},{6,2},{7,3},{8,12},{9,13},{10,... | collective-permute-start | bytes 396296 | tf_op jit(solution)/shard_map/ppermute | solution.py:221
  20.3 19.3 %copy-start.1 = (f32[512,256]{1,0:T(8,128)S(1)}, f32[512,256]{1,0:T(8,128)}, u32[]{:S(2)}) copy-start(f32[512,256]{1,0:T(8,128)} %memory_ref.3) | copy-start | bytes 1572868
  20.3 19.4 %copy-start.2 = (bf16[256,512]{1,0:T(8,128)(2,1)S(1)}, bf16[256,512]{1,0:T(8,128)(2,1)}, u32[]{:S(2)}) copy-start(bf16[256,512]{1,0:T(8,128)(2,1)} %weight_ref.5) | copy-start | bytes 786436
  20.4 19.4 %copy-start.6 = (f32[256]{0:T(256)S(1)}, f32[256]{0:T(256)}, u32[]{:S(2)}) copy-start(f32[256]{0:T(256)} %param.19) | copy-start | bytes 3076
  20.4 6.8 %collective-permute-start.5 = (bf16[258,256]{1,0:T(8,128)(2,1)S(1)}, bf16[258,256]{1,0:T(8,128)(2,1)S(1)}, u32[]{:S(2)}, u32[]{:S(2)}) collective-permute-start(bf16[258,256]{1,0:T(8,128)(2,1)S(1)} %pad_maximum_fusion.1), channel_id=1, source_target_pairs={{0,2},{1,3},{2,0},{3,1},{4,6},{5,7},{6,4},{7,5},{8,10},{9,11},{10,... | collective-permute-start | bytes 396296 | tf_op jit(solution)/shard_map/ppermute | solution.py:221
  27.9 11.8 %collective-permute-start.12 = (bf16[128,256]{1,0:T(8,128)(2,1)S(1)}, bf16[128,256]{1,0:T(8,128)(2,1)S(1)}, u32[]{:S(2)}, u32[]{:S(2)}) collective-permute-start(bf16[128,256]{1,0:T(8,128)(2,1)S(1)} %get-tuple-element.55), channel_id=1, source_target_pairs={{0,8},{8,16},{1,9},{9,17},{2,10},{10,18},{3,11},{11,19},{4,12},{12... | collective-permute-start | bytes 196616 | tf_op jit(solution)/shard_map/ppermute | solution.py:324
  29.2 10.5 %collective-permute-start.13 = (bf16[128,256]{1,0:T(8,128)(2,1)S(1)}, bf16[128,256]{1,0:T(8,128)(2,1)S(1)}, u32[]{:S(2)}, u32[]{:S(2)}) collective-permute-start(bf16[128,256]{1,0:T(8,128)(2,1)S(1)} %get-tuple-element.54), channel_id=1, source_target_pairs={{16,8},{0,16},{17,9},{1,17},{18,10},{2,18},{19,11},{3,19},{20,12},... | collective-permute-start | bytes 196616 | tf_op jit(solution)/shard_map/ppermute | solution.py:324
  33.8 9.6 %collective-permute-start.8 = (bf16[128,256]{1,0:T(8,128)(2,1)S(1)}, bf16[128,256]{1,0:T(8,128)(2,1)S(1)}, u32[]{:S(2)}, u32[]{:S(2)}) collective-permute-start(bf16[128,256]{1,0:T(8,128)(2,1)S(1)} %get-tuple-element.57), channel_id=1, source_target_pairs={{0,8},{8,16},{1,9},{9,17},{2,10},{10,18},{3,11},{11,19},{4,12},{12... | collective-permute-start | bytes 196616 | tf_op jit(solution)/shard_map/ppermute | solution.py:324
  35.1 8.3 %collective-permute-start.9 = (bf16[128,256]{1,0:T(8,128)(2,1)S(1)}, bf16[128,256]{1,0:T(8,128)(2,1)S(1)}, u32[]{:S(2)}, u32[]{:S(2)}) collective-permute-start(bf16[128,256]{1,0:T(8,128)(2,1)S(1)} %get-tuple-element.53), channel_id=1, source_target_pairs={{16,8},{0,16},{17,9},{1,17},{18,10},{2,18},{19,11},{3,19},{20,12},... | collective-permute-start | bytes 196616 | tf_op jit(solution)/shard_map/ppermute | solution.py:324
  40.1 9.8 %collective-permute-start.14 = (f16[128,256]{1,0:T(8,128)(2,1)S(1)}, f16[128,256]{1,0:T(8,128)(2,1)S(1)}, u32[]{:S(2)}, u32[]{:S(2)}) collective-permute-start(f16[128,256]{1,0:T(8,128)(2,1)S(1)} %convert_element_type.32), channel_id=1, source_target_pairs={{8,24},{16,8},{9,25},{17,9},{10,26},{18,10},{11,27},{19,11},{12,28... | collective-permute-start | bytes 196616 | tf_op jit(solution)/shard_map/ppermute | solution.py:346
  41.5 8.5 %collective-permute-start.15 = (f16[128,256]{1,0:T(8,128)(2,1)S(1)}, f16[128,256]{1,0:T(8,128)(2,1)S(1)}, u32[]{:S(2)}, u32[]{:S(2)}) collective-permute-start(f16[128,256]{1,0:T(8,128)(2,1)S(1)} %convert_element_type.34), channel_id=1, source_target_pairs={{8,16},{16,24},{9,17},{17,25},{10,18},{18,26},{11,19},{19,27},{12,... | collective-permute-start | bytes 196616 | tf_op jit(solution)/shard_map/ppermute | solution.py:346
  43.8 6.2 %collective-permute-start.10 = (f16[128,256]{1,0:T(8,128)(2,1)S(1)}, f16[128,256]{1,0:T(8,128)(2,1)S(1)}, u32[]{:S(2)}, u32[]{:S(2)}) collective-permute-start(f16[128,256]{1,0:T(8,128)(2,1)S(1)} %convert_element_type.28), channel_id=1, source_target_pairs={{8,24},{16,8},{9,25},{17,9},{10,26},{18,10},{11,27},{19,11},{12,28... | collective-permute-start | bytes 196616 | tf_op jit(solution)/shard_map/ppermute | solution.py:346
  47.8 6.2 %collective-permute-start.11 = (f16[128,256]{1,0:T(8,128)(2,1)S(1)}, f16[128,256]{1,0:T(8,128)(2,1)S(1)}, u32[]{:S(2)}, u32[]{:S(2)}) collective-permute-start(f16[128,256]{1,0:T(8,128)(2,1)S(1)} %convert_element_type.30), channel_id=1, source_target_pairs={{8,16},{16,24},{9,17},{17,25},{10,18},{18,26},{11,19},{19,27},{12,... | collective-permute-start | bytes 196616 | tf_op jit(solution)/shard_map/ppermute | solution.py:346

commit v2 on v1

v2 whole, which is shorter than its diff:
```python
import jax
import jax.numpy as jnp
from jax import lax
from jax.experimental import pallas as pl
from jax.experimental.pallas import tpu as pltpu
from jax.sharding import PartitionSpec as P

BASE = 32.0
VMEM_LIMIT = 20 << 20
F32 = jnp.float32
BF16 = jnp.bfloat16


def dot(a, b, dims=((1,), (0,))):
    return lax.dot_general(a, b, (dims, ((), ())), preferred_element_type=F32)


def call(kernel, outs, *args, flops=0, scratch=(), raw_out=()):
    outs = [jax.ShapeDtypeStruct(shape, dtype) for shape, dtype in outs]
    moved = sum(x.size * x.dtype.itemsize for x in [*args, *outs])

    def specs(count, raw):
        return [
            pl.BlockSpec(memory_space=pl.ANY if i in raw else pltpu.VMEM) for i in range(count)
        ]

    return pl.pallas_call(
        kernel,
        out_shape=outs,
        in_specs=specs(len(args), ()),
        out_specs=specs(len(outs), raw_out),
        scratch_shapes=list(scratch),
        cost_estimate=pl.CostEstimate(flops=flops, bytes_accessed=moved, transcendentals=0),
        compiler_params=pltpu.CompilerParams(vmem_limit_bytes=VMEM_LIMIT),
    )(*args)


def columns_of(row):
    return jnp.transpose(jnp.broadcast_to(row, (row.shape[1], row.shape[1])))


def hot_rows(row, width):
    count = row.shape[1]
    column = jnp.concatenate([columns_of(row)] * (width // count), 1)
    lanes = lax.broadcasted_iota(jnp.int32, (count, width), 1)
    return jnp.where(column == lanes, 1.0, 0.0).astype(BF16)


def hot_columns(row, start, height):
    sublanes = lax.broadcasted_iota(jnp.int32, (height, row.shape[1]), 0) + start
    return jnp.where(row == sublanes, 1.0, 0.0).astype(BF16)


def fetch_kernel(lists_ref, memory_ref, out_ref, stale_ref):
    me = lax.axis_index("node")
    stale = memory_ref[...].astype(BF16)
    stale_ref[...] = stale
    for chip in range(out_ref.shape[0]):
        hot = hot_rows(lists_ref[pl.ds(me ^ (2 * chip + 1), 1), :], stale.shape[0])
        out_ref[chip] = dot(hot, stale).astype(BF16)


def pick_kernel(lists_ref, stale_ref, out_ref):
    me = lax.axis_index("node")
    stale = stale_ref[...]
    for chip in range(out_ref.shape[0]):
        hot = hot_rows(lists_ref[pl.ds(me ^ (2 * chip), 1), :], stale.shape[0])
        out_ref[chip] = dot(hot, stale).astype(BF16)


def prep_kernel(
    slots_ref, time_ref, freq_ref, weight_ref, bias_ref, hot_ref, turned_ref, base_ref, code_ref
):
    me = lax.axis_index("node")
    slots_all, ends = hot_ref.shape
    blocks, capacity = code_ref.shape[0], code_ref.shape[2] // 2
    slots = slots_ref[...]
    slots = ((slots // capacity) ^ me) * capacity + slots % capacity
    counts = jnp.zeros((8, slots_all), F32)
    ones = jnp.ones((8, capacity), BF16)
    for i in range(ends // capacity):
        rows = slice(i * capacity, (i + 1) * capacity)
        turned = hot_rows(slots[:, rows], slots_all)
        turned_ref[rows] = turned
        counts = counts + dot(ones, turned)
    for j in range(blocks):
        hot_ref[j * capacity : (j + 1) * capacity] = hot_columns(slots, j * capacity, capacity)
    upper = jnp.floor(counts * (1.0 / BASE))
    lower = counts - BASE * upper
    for j in range(blocks):
        lanes = slice(j * capacity, (j + 1) * capacity)
        code = jnp.concatenate([upper[:, lanes], lower[:, lanes]], 1)
        code_ref[j] = code[: code_ref.shape[1]].astype(BF16)
    width = freq_ref.shape[1]
    stale_part = weight_ref.shape[0] - width
    for i in range(time_ref.shape[1] // width):
        rows = slice(i * width, (i + 1) * width)
        encoding = jnp.cos(columns_of(time_ref[:, rows]) * freq_ref[...]).astype(BF16)
        base_ref[rows] = dot(encoding, weight_ref[stale_part:]) + bias_ref[...]


def gathered(turned_ref, start, tables):
    rows = None
    for table in tables:
        stop = start + table.shape[0]
        part = dot(turned_ref[:, start:stop], table)
        rows = part if rows is None else rows + part
        start = stop
    return rows


def gather_kernel(own_ref, partner_ref, near_ref, turned_ref, rows_ref):
    capacity, breadth = own_ref.shape
    tables = [
        jnp.concatenate([own_ref[...], partner_ref[...]], 0),
        near_ref[...].reshape(2 * capacity, breadth),
    ]
    rows_ref[...] = gathered(turned_ref, 0, tables)


def message_kernel(rows_ref, *refs):
    tables, (turned_ref, hot_ref, weight_ref, base_ref, code_ref) = refs[:-7], refs[-7:-2]
    other_ref, message_ref = refs[-2:]
    _, capacity, breadth = tables[0].shape
    tables = [table[...].reshape(2 * capacity, breadth) for table in tables]
    rows = (rows_ref[...] + gathered(turned_ref, 4 * capacity, tables)).astype(BF16)
    events = rows.shape[0] // 2
    first = dot(rows, weight_ref[:breadth])
    second = dot(rows, weight_ref[breadth : 2 * breadth])
    base = base_ref[...]
    message_ref[:events] = jnp.maximum(first[:events] + second[events:] + base, 0.0).astype(BF16)
    message_ref[events:] = jnp.maximum(first[events:] + second[:events] + base, 0.0).astype(BF16)
    messages = message_ref[...]
    for chip in range(other_ref.shape[0]):
        j = 2 * chip + 1
        sums = dot(hot_ref[j * capacity : (j + 1) * capacity], messages)
        other_ref[chip, :capacity] = sums.astype(BF16)
        other_ref[chip, capacity:] = code_ref[j]


def own_kernel(hot_ref, message_ref, own_ref):
    messages = message_ref[...]
    chips, capacity, _ = own_ref.shape
    for chip in range(chips):
        rows = slice(2 * chip * capacity, (2 * chip + 1) * capacity)
        own_ref[chip] = dot(hot_ref[rows], messages).astype(BF16)


def rows_kernel(lists_ref, rowhot_ref):
    me = lax.axis_index("node")
    blocks, capacity = lists_ref.shape
    for j in range(blocks):
        row = lists_ref[pl.ds(me ^ j, 1), :]
        rowhot_ref[:, j * capacity : (j + 1) * capacity] = hot_columns(
            row, 0, rowhot_ref.shape[0]
        )


def load_totals(rowhot_ref, start, loads):
    totals, counts = None, None
    for load in loads:
        breadth = load.shape[1]
        pair = 2 * (load.shape[0] // 2 - 1)
        capacity = pair // 2
        hot = rowhot_ref[:, start : start + pair]
        start += pair
        part = dot(hot, load[:pair])
        first = load[pair : pair + 1].astype(F32)
        second = load[pair + 1 : pair + 2].astype(F32)
        code = [
            jnp.broadcast_to(
                jnp.concatenate([first[:, lanes], second[:, lanes]], 1), (breadth // 2, pair)
            )
            for lanes in (slice(None, capacity), slice(capacity, None))
        ]
        count = dot(hot, jnp.concatenate(code, 0).astype(BF16), ((1,), (1,)))
        totals = part if totals is None else totals + part
        counts = count if counts is None else counts + count
    return totals, counts


def part_kernel(own_ref, near_ref, rowhot_ref, totals_ref, counts_ref):
    totals_ref[...], counts_ref[...] = load_totals(rowhot_ref, 0, [own_ref, near_ref])


def mean_kernel(totals_ref, counts_ref, rowhot_ref, *refs):
    loads, mean_ref = refs[:-1], refs[-1]
    breadth = mean_ref.shape[1]
    start = 4 * (loads[0].shape[0] // 2 - 1)
    totals, counts = load_totals(rowhot_ref, start, loads)
    totals = totals_ref[...] + totals
    counts = counts_ref[...] + counts
    counts = BASE * counts[:, : breadth // 2] + counts[:, breadth // 2 :]
    counts = jnp.concatenate([counts, counts], 1)
    mean = jnp.where(counts > 0.0, totals / jnp.maximum(counts, 1.0), -1.0)
    mean_ref[...] = mean.astype(BF16)


def gates(mean_code, gate_weight, update_bias):
    breadth = mean_code.shape[1]
    terms = dot(mean_code, gate_weight)
    update = jax.nn.sigmoid(terms[:, :breadth] + update_bias)
    candidate = jnp.tanh(terms[:, breadth:])
    touched = mean_code.astype(F32) >= 0.0
    keep_rate = jnp.where(touched, 1.0 - update, 1.0)
    write_term = jnp.where(touched, update * candidate, 0.0)
    return keep_rate, write_term


def gate_kernel(mean_ref, weight_ref, bias_ref, keep_ref, write_ref):
    keep_ref[...], write_ref[...] = gates(mean_ref[...], weight_ref[...], bias_ref[...])


def state_kernel(keep_all_ref, write_all_ref, memory_ref, weight_ref, bias_ref, *refs):
    periods = (len(refs) - 3) // 2 + 1
    means, outs, scratch = refs[: periods - 1], refs[periods - 1 : -3], refs[-3:]
    keep_ref, write_ref, state_ref = scratch
    me = lax.axis_index("tm")
    share = outs[0].shape[0]
    rows = pl.ds(pl.multiple_of(me * share, share), share)
    keep_ref[0], write_ref[0] = keep_all_ref[rows], write_all_ref[rows]
    for k, mean in enumerate(means):
        keep, write = gates(mean[...], weight_ref[...], bias_ref[...])
        keep_ref[k + 1], write_ref[k + 1] = keep, write
    state = memory_ref[rows]
    state_ref[0] = state
    for t in range(periods - 1):
        state = keep_ref[t ^ me] * state + write_ref[t ^ me]
        state_ref[t + 1] = state
    for k, out in enumerate(outs):
        out[...] = state_ref[me ^ k]


def final_kernel(keep_ref, write_ref, *refs):
    periods = (len(refs) - 3)
    befores, (out_any, made_ref, sems) = refs[:periods], refs[periods:]
    me = lax.axis_index("tm")
    share = befores[0].shape[0]
    copies = []
    for k, before in enumerate(befores):
        rows = pl.ds(pl.multiple_of((me ^ k) * share, share), share)
        made_ref[k] = keep_ref[rows] * before[...] + write_ref[rows]
        copies.append(pltpu.make_async_copy(made_ref.at[k], out_any.at[rows], sems.at[k]))
        copies[-1].start()
    for copy in copies:
        copy.wait()


def swap(axis, value, distance):
    size = lax.axis_size(axis)
    return lax.ppermute(value, axis, [(i, i ^ distance) for i in range(size)])


def shards(
    memory,
    src_slot,
    dst_slot,
    event_time,
    touched_rows,
    time_freq,
    msg_weight,
    msg_bias,
    gate_weight,
    update_bias,
):
    period = lax.axis_index("tm")
    periods = lax.axis_size("tm")
    blocks, capacity = touched_rows.shape[2:]
    node_rows, breadth = memory.shape
    events = src_slot.shape[2]
    chips = blocks // 2
    lists = jnp.maximum(touched_rows[0, 0], 0)

    pick_flops = chips * capacity * breadth * node_rows * 2
    other_picks, stale = call(
        fetch_kernel,
        [((chips, capacity, breadth), BF16), ((node_rows, breadth), BF16)],
        lists,
        memory,
        flops=pick_flops,
    )
    from_partner = swap("node", other_picks, 1)
    own = call(pick_kernel, [((chips, capacity, breadth), BF16)], lists, stale, flops=pick_flops)[0]
    sources, targets, times, from_partner = lax.optimization_barrier(
        (src_slot[0], dst_slot[0], event_time[0], from_partner)
    )
    tables = [own[0], from_partner[0]] + [
        swap("node", jnp.stack([own[chip], from_partner[chip]]), 2 * chip)
        for chip in range(1, chips)
    ]
    ends = 2 * events
    slots = blocks * capacity
    hot, turned, base, code = call(
        prep_kernel,
        [
            ((slots, ends), BF16),
            ((ends, slots), BF16),
            ((events, breadth), F32),
            ((blocks, 1, 2 * capacity), BF16),
        ],
        jnp.concatenate([sources, targets], 1),
        times,
        time_freq[None],
        msg_weight,
        msg_bias[None],
    )
    rows = call(
        gather_kernel,
        [((ends, breadth), F32)],
        *tables[:3],
        turned,
        flops=8 * ends * capacity * breadth,
    )[0]
    other, messages = call(
        message_kernel,
        [((chips, capacity + 1, breadth), BF16), ((ends, breadth), BF16)],
        rows,
        *tables[3:],
        turned,
        hot,
        msg_weight,
        base,
        code,
        flops=ends * slots * breadth * 3,
    )
    partner = swap("node", other, 1)
    own_sums = call(
        own_kernel,
        [((chips, capacity, breadth), BF16)],
        hot,
        messages,
        flops=ends * slots * breadth,
    )[0]
    loads = []
    for chip in range(chips):
        load = jnp.concatenate(
            [own_sums[chip], partner[chip, :capacity], code[2 * chip], partner[chip, capacity:]], 0
        )
        loads.append(swap("node", load, 2 * chip) if chip else load)
    rowhot = call(rows_kernel, [((node_rows, slots), BF16)], lists)[0]
    totals, counts = call(
        part_kernel,
        [((node_rows, breadth), F32)] * 2,
        *loads[:2],
        rowhot,
        flops=16 * node_rows * capacity * breadth,
    )
    mean_code = call(
        mean_kernel,
        [((node_rows, breadth), BF16)],
        totals,
        counts,
        rowhot,
        *loads[2:],
        flops=4 * node_rows * slots * breadth,
    )[0]

    share = node_rows // periods
    bias = update_bias[None]
    means = [
        swap("tm", lax.dynamic_slice_in_dim(mean_code, (period ^ k) * share, share, 0), k)
        for k in range(1, periods)
    ]
    keep, write = call(
        gate_kernel,
        [((node_rows, breadth), F32)] * 2,
        mean_code,
        gate_weight,
        bias,
        flops=4 * node_rows * breadth * breadth,
    )
    states = call(
        state_kernel,
        [((share, breadth), F32)] * periods,
        keep,
        write,
        memory,
        gate_weight,
        bias,
        *means,
        flops=4 * node_rows * breadth * breadth,
        scratch=[pltpu.VMEM((periods, share, breadth), F32)] * 3,
    )
    befores = [states[0]] + [
        swap("tm", states[k].astype(jnp.float16), k).astype(F32)
        for k in range(1, periods)
    ]
    result = call(
        final_kernel,
        [((node_rows, breadth), F32)],
        keep,
        write,
        *befores,
        scratch=[pltpu.VMEM((periods, share, breadth), F32), pltpu.SemaphoreType.DMA((periods,))],
        raw_out=(0,),
    )[0]
    return result[None]


def solution(mesh):
    return jax.shard_map(
        shards,
        mesh=mesh,
        in_specs=(
            P("node", None),
            P("tm", "node", None),
            P("tm", "node", None),
            P("tm", "node", None),
            P("tm", "node", None, None),
            P(),
            P(),
            P(),
            P(),
            P(),
        ),
        out_specs=P("tm", "node", None),
        check_vma=False,
    )
```

time: 55.3 us -> 49.1 us (0.89)
  the two profiles are of different devices: /device:TPU:16 before, /device:TPU:0 now
where the time goes in v2:
time: 49.1 us; the launch traced here: 48.9 us
  waiting for transfers between devices  20.7 us (42%)
  starting transfers between devices  17.9 us (36%)
  Pallas kernels  7.86 us (16%)
  local copies, waits for them, and re-layouts  1.2 us (2%)
  other arithmetic  0.91 us (2%)
    ppermute x14, waiting for transfers between devices, swap(): return lax.ppermute(value, axis, [(i, i ^ distance) for i in range(size)])  20.7 us
    ppermute x14, starting transfers between devices, swap(): return lax.ppermute(value, axis, [(i, i ^ distance) for i in range(size)])  17.9 us
    pallas_call x12, Pallas kernels, call(): pl.pallas_call(kernel, out_shape=outs, in_specs=specs(len(args), ()), out...  7.86 us
    unnamed x20, local copies, waits for them, and re-layouts  1.08 us
  transfers between devices with their start and end apart: 14, of which 10 were waited for; matrix products, arithmetic and copies ran while one was open for 0% of the time, Pallas kernels for 9%

profile of v2, /device:TPU:0, one launch (start us, length us, event | category | flops | bytes accessed | tf_op | source)
XLA Modules:
  0.0 48.9 jit_solution(6900930726653305737)
XLA Ops:
  0.0 0.8 %maximum_bitcast_fusion.lists_ref = s32[8,128]{1,0:T(8,128)S(1)} fusion(s32[1,1,8,128]{3,2,1,0:T(8,128)} %param.14), kind=kLoop, calls=%fused_computation.18 | loop fusion | flops 1024 | bytes 8192 | tf_op jit(solution)/shard_map/max | solution.py:272
  0.8 1.0 %copy-done = f32[512,256]{1,0:T(8,128)S(1)} copy-done((f32[512,256]{1,0:T(8,128)S(1)}, f32[512,256]{1,0:T(8,128)}, u32[]{:S(2)}) %copy-start) | copy-done | bytes 524312
  1.8 0.4 shard_map.100
  2.2 0.6 %collective-permute-start = (bf16[4,128,256]{2,1,0:T(8,128)(2,1)S(1)}, bf16[4,128,256]{2,1,0:T(8,128)(2,1)S(1)}, u32[]{:S(2)}, u32[]{:S(2)}) collective-permute-start(bf16[4,128,256]{2,1,0:T(8,128)(2,1)S(1)} %get-tuple-element.25), channel_id=1, source_target_pairs={{0,1},{1,0},{2,3},{3,2},{4,5},{5,4},{6,7},{7,6},{8,9},{9,8},{10,11... | collective-permute-start | bytes 786440 | tf_op jit(solution)/shard_map/ppermute | solution.py:251
  3.1 0.4 shard_map.102
  3.4 0.4 collective-permute-done
  3.9 2.9 %collective-permute-start.1 = (bf16[2,128,256]{2,1,0:T(8,128)(2,1)S(1)}, bf16[2,128,256]{2,1,0:T(8,128)(2,1)S(1)}, u32[]{:S(2)}, u32[]{:S(2)}) collective-permute-start(bf16[2,128,256]{2,1,0:T(8,128)(2,1)S(1)} %pad_maximum_fusion.4), channel_id=1, source_target_pairs={{0,2},{1,3},{2,0},{3,1},{4,6},{5,7},{6,4},{7,5},{8,10},{9,11},{10,... | collective-permute-start | bytes 393224 | tf_op jit(solution)/shard_map/ppermute | solution.py:251
  6.9 1.6 %collective-permute-start.2 = (bf16[2,128,256]{2,1,0:T(8,128)(2,1)S(1)}, bf16[2,128,256]{2,1,0:T(8,128)(2,1)S(1)}, u32[]{:S(2)}, u32[]{:S(2)}) collective-permute-start(bf16[2,128,256]{2,1,0:T(8,128)(2,1)S(1)} %pad_maximum_fusion.5), channel_id=1, source_target_pairs={{0,4},{1,5},{2,6},{3,7},{4,0},{5,1},{6,2},{7,3},{8,12},{9,13},{10,... | collective-permute-start | bytes 393224 | tf_op jit(solution)/shard_map/ppermute | solution.py:251
  8.6 2.0 %shard_map.101 = (bf16[1024,1024]{1,0:T(8,128)(2,1)S(1)}, bf16[1024,1024]{1,0:T(8,128)(2,1)S(1)}, f32[512,256]{1,0:T(8,128)S(1)}, bf16[8,1,256]{2,1,0:T(2,128)(2,1)S(1)}) custom-call(s32[1,1024]{1,0:T(1,128)S(1)} %pad_add_fusion.slots_ref, f32[1,512]{1,0:T(1,128)S(1)} %bitcast.47, f32[1,128]{1,0:T(1,128)S(1)} %bitcast.49, bf16[640,256]{1,0:T(8,128)(2,1)S(1)} %copy-done.2, ...), custom_call_target="tpu_custom_call" | custom-call | bytes 5058048 | tf_op jit(solution)/shard_map/pallas_call | solution.py:27
  10.7 0.4 shard_map.103.rows_ref
  11.2 3.8 %collective-permute-done.2.refs_0_ = bf16[2,128,256]{2,1,0:T(8,128)(2,1)S(1)} collective-permute-done((bf16[2,128,256]{2,1,0:T(8,128)(2,1)S(1)}, bf16[2,128,256]{2,1,0:T(8,128)(2,1)S(1)}, u32[]{:S(2)}, u32[]{:S(2)}) %collective-permute-start.2) | collective-permute-done | bytes 131104 | tf_op jit(solution)/shard_map/ppermute | solution.py:251
  15.0 1.5 %shard_map.104 = (bf16[4,129,256]{2,1,0:T(8,128)(2,1)S(1)}, bf16[1024,256]{1,0:T(8,128)(2,1)S(1)}) custom-call(f32[1024,256]{1,0:T(8,128)S(1)} %shard_map.103.rows_ref, bf16[2,128,256]{2,1,0:T(8,128)(2,1)S(1)} %collective-permute-done.2.refs_0_, bf16[2,128,256]{2,1,0:T(8,128)(2,1)S(1)} %collective-permute-done.3.refs_1_, ...), custom_call_target="tpu_custom_call" | custom-call | flops 805306368 | bytes 7149568 | tf_op jit(solution)/shard_map/pallas_call | solution.py:27
  16.6 0.4 shard_map.105
  17.1 1.0 %collective-permute-done.4 = bf16[4,129,256]{2,1,0:T(8,128)(2,1)S(1)} collective-permute-done((bf16[4,129,256]{2,1,0:T(8,128)(2,1)S(1)}, bf16[4,129,256]{2,1,0:T(8,128)(2,1)S(1)}, u32[]{:S(2)}, u32[]{:S(2)}) %collective-permute-start.4) | collective-permute-done | bytes 264224 | tf_op jit(solution)/shard_map/ppermute | solution.py:251
  18.2 1.6 %collective-permute-start.7 = (bf16[258,256]{1,0:T(8,128)(2,1)S(1)}, bf16[258,256]{1,0:T(8,128)(2,1)S(1)}, u32[]{:S(2)}, u32[]{:S(2)}) collective-permute-start(bf16[258,256]{1,0:T(8,128)(2,1)S(1)} %pad_maximum_fusion.3), channel_id=1, source_target_pairs={{0,6},{1,7},{2,4},{3,5},{4,2},{5,3},{6,0},{7,1},{8,14},{9,15},{10,... | collective-permute-start | bytes 396296 | tf_op jit(solution)/shard_map/ppermute | solution.py:251
  19.8 1.5 %collective-permute-start.5 = (bf16[258,256]{1,0:T(8,128)(2,1)S(1)}, bf16[258,256]{1,0:T(8,128)(2,1)S(1)}, u32[]{:S(2)}, u32[]{:S(2)}) collective-permute-start(bf16[258,256]{1,0:T(8,128)(2,1)S(1)} %pad_maximum_fusion.1), channel_id=1, source_target_pairs={{0,2},{1,3},{2,0},{3,1},{4,6},{5,7},{6,4},{7,5},{8,10},{9,11},{10,... | collective-permute-start | bytes 396296 | tf_op jit(solution)/shard_map/ppermute | solution.py:251
  21.3 0.6 %collective-permute-start.6 = (bf16[258,256]{1,0:T(8,128)(2,1)S(1)}, bf16[258,256]{1,0:T(8,128)(2,1)S(1)}, u32[]{:S(2)}, u32[]{:S(2)}) collective-permute-start(bf16[258,256]{1,0:T(8,128)(2,1)S(1)} %pad_maximum_fusion.2), channel_id=1, source_target_pairs={{0,4},{1,5},{2,6},{3,7},{4,0},{5,1},{6,2},{7,3},{8,12},{9,13},{10,... | collective-permute-start | bytes 396296 | tf_op jit(solution)/shard_map/ppermute | solution.py:251
  21.9 5.8 %collective-permute-done.5.near_ref = bf16[258,256]{1,0:T(8,128)(2,1)S(1)} collective-permute-done((bf16[258,256]{1,0:T(8,128)(2,1)S(1)}, bf16[258,256]{1,0:T(8,128)(2,1)S(1)}, u32[]{:S(2)}, u32[]{:S(2)}) %collective-permute-start.5) | collective-permute-done | bytes 132128 | tf_op jit(solution)/shard_map/ppermute | solution.py:251
  27.7 0.4 shard_map.107
  28.2 0.5 shard_map.108.mean_ref
  28.7 3.7 %collective-permute-start.10 = (bf16[128,256]{1,0:T(8,128)(2,1)S(1)}, bf16[128,256]{1,0:T(8,128)(2,1)S(1)}, u32[]{:S(2)}, u32[]{:S(2)}) collective-permute-start(bf16[128,256]{1,0:T(8,128)(2,1)S(1)} %get-tuple-element.53), channel_id=1, source_target_pairs={{0,24},{8,16},{16,8},{24,0},{1,25},{9,17},{17,9},{25,1},{2,26},{10... | collective-permute-start | bytes 196616 | tf_op jit(solution)/shard_map/ppermute | solution.py:251
  32.4 0.8 %collective-permute-start.9 = (bf16[128,256]{1,0:T(8,128)(2,1)S(1)}, bf16[128,256]{1,0:T(8,128)(2,1)S(1)}, u32[]{:S(2)}, u32[]{:S(2)}) collective-permute-start(bf16[128,256]{1,0:T(8,128)(2,1)S(1)} %get-tuple-element.54), channel_id=1, source_target_pairs={{0,16},{8,24},{16,0},{24,8},{1,17},{9,25},{17,1},{25,9},{2,18},{10... | collective-permute-start | bytes 196616 | tf_op jit(solution)/shard_map/ppermute | solution.py:251
  33.5 1.4 %collective-permute-done.10.refs_2_ = bf16[128,256]{1,0:T(8,128)(2,1)S(1)} collective-permute-done((bf16[128,256]{1,0:T(8,128)(2,1)S(1)}, bf16[128,256]{1,0:T(8,128)(2,1)S(1)}, u32[]{:S(2)}, u32[]{:S(2)}) %collective-permute-start.10) | collective-permute-done | bytes 65568 | tf_op jit(solution)/shard_map/ppermute | solution.py:251
  35.0 1.8 %collective-permute-done.8.refs_0_ = bf16[128,256]{1,0:T(8,128)(2,1)S(1)} collective-permute-done((bf16[128,256]{1,0:T(8,128)(2,1)S(1)}, bf16[128,256]{1,0:T(8,128)(2,1)S(1)}, u32[]{:S(2)}, u32[]{:S(2)}) %collective-permute-start.8) | collective-permute-done | bytes 65568 | tf_op jit(solution)/shard_map/ppermute | solution.py:251
  36.8 0.8 %collective-permute-done.9.refs_1_ = bf16[128,256]{1,0:T(8,128)(2,1)S(1)} collective-permute-done((bf16[128,256]{1,0:T(8,128)(2,1)S(1)}, bf16[128,256]{1,0:T(8,128)(2,1)S(1)}, u32[]{:S(2)}, u32[]{:S(2)}) %collective-permute-start.9) | collective-permute-done | bytes 65568 | tf_op jit(solution)/shard_map/ppermute | solution.py:251
  37.6 0.4 shard_map.110
  38.0 2.1 %collective-permute-start.11 = (f16[128,256]{1,0:T(8,128)(2,1)S(1)}, f16[128,256]{1,0:T(8,128)(2,1)S(1)}, u32[]{:S(2)}, u32[]{:S(2)}) collective-permute-start(f16[128,256]{1,0:T(8,128)(2,1)S(1)} %convert_element_type.18), channel_id=1, source_target_pairs={{0,8},{8,0},{16,24},{24,16},{1,9},{9,1},{17,25},{25,17},{2,10},{10... | collective-permute-start | bytes 196616 | tf_op jit(solution)/shard_map/ppermute | solution.py:251
  40.1 1.8 %collective-permute-start.12 = (f16[128,256]{1,0:T(8,128)(2,1)S(1)}, f16[128,256]{1,0:T(8,128)(2,1)S(1)}, u32[]{:S(2)}, u32[]{:S(2)}) collective-permute-start(f16[128,256]{1,0:T(8,128)(2,1)S(1)} %convert_element_type.20), channel_id=1, source_target_pairs={{0,16},{8,24},{16,0},{24,8},{1,17},{9,25},{17,1},{25,9},{2,18},{10... | collective-permute-start | bytes 196616 | tf_op jit(solution)/shard_map/ppermute | solution.py:251
  41.9 0.7 %collective-permute-start.13 = (f16[128,256]{1,0:T(8,128)(2,1)S(1)}, f16[128,256]{1,0:T(8,128)(2,1)S(1)}, u32[]{:S(2)}, u32[]{:S(2)}) collective-permute-start(f16[128,256]{1,0:T(8,128)(2,1)S(1)} %convert_element_type.22), channel_id=1, source_target_pairs={{0,24},{8,16},{16,8},{24,0},{1,25},{9,17},{17,9},{25,1},{2,26},{10... | collective-permute-start | bytes 196616 | tf_op jit(solution)/shard_map/ppermute | solution.py:251
  42.7 3.5 %collective-permute-done.12 = f16[128,256]{1,0:T(8,128)(2,1)S(1)} collective-permute-done((f16[128,256]{1,0:T(8,128)(2,1)S(1)}, f16[128,256]{1,0:T(8,128)(2,1)S(1)}, u32[]{:S(2)}, u32[]{:S(2)}) %collective-permute-start.12) | collective-permute-done | bytes 65568 | tf_op jit(solution)/shard_map/ppermute | solution.py:251
  46.2 1.9 %collective-permute-done.13 = f16[128,256]{1,0:T(8,128)(2,1)S(1)} collective-permute-done((f16[128,256]{1,0:T(8,128)(2,1)S(1)}, f16[128,256]{1,0:T(8,128)(2,1)S(1)}, u32[]{:S(2)}, u32[]{:S(2)}) %collective-permute-start.13) | collective-permute-done | bytes 65568 | tf_op jit(solution)/shard_map/ppermute | solution.py:251
  48.1 0.9 %shard_map.111 = f32[512,256]{1,0:T(8,128)} custom-call(f32[512,256]{1,0:T(8,128)S(1)} %get-tuple-element.39.keep_all_ref.keep_ref, f32[512,256]{1,0:T(8,128)S(1)} %get-tuple-element.40.write_all_ref.write_ref, f32[128,256]{1,0:T(8,128)S(1)} %get-tuple-element.41.refs_0_, f32[128,256]{1,0:T(8,128)S(1)} %convert_element_type.19.refs_1_, ...), custom_call_target="tpu_custom_call" | custom-call | bytes 2097152 | tf_op jit(solution)/shard_map/pallas_call | solution.py:27
  (50 shorter events, 1.2 us)
Async XLA Ops:
  0.0 8.6 %copy-start.9 = (s32[1,1,512]{2,1,0:T(1,128)S(1)}, s32[1,1,512]{2,1,0:T(1,128)}, u32[]{:S(2)}) copy-start(s32[1,1,512]{2,1,0:T(1,128)} %param.11) | copy-start | bytes 6148
  0.0 8.6 %copy-start.8 = (s32[1,1,512]{2,1,0:T(1,128)S(1)}, s32[1,1,512]{2,1,0:T(1,128)}, u32[]{:S(2)}) copy-start(s32[1,1,512]{2,1,0:T(1,128)} %param.12) | copy-start | bytes 6148
  0.0 8.6 %copy-start.5 = (f32[1,1,512]{2,1,0:T(1,128)S(1)}, f32[1,1,512]{2,1,0:T(1,128)}, u32[]{:S(2)}) copy-start(f32[1,1,512]{2,1,0:T(1,128)} %param.13) | copy-start | bytes 6148
  0.0 8.6 %copy-start.7 = (f32[128]{0:T(128)S(1)}, f32[128]{0:T(128)}, u32[]{:S(2)}) copy-start(f32[128]{0:T(128)} %param.15) | copy-start | bytes 1540
  0.0 8.6 %copy-start.6 = (f32[256]{0:T(256)S(1)}, f32[256]{0:T(256)}, u32[]{:S(2)}) copy-start(f32[256]{0:T(256)} %param.17) | copy-start | bytes 3076
  0.8 1.0 %copy-start = (f32[512,256]{1,0:T(8,128)S(1)}, f32[512,256]{1,0:T(8,128)}, u32[]{:S(2)}) copy-start(f32[512,256]{1,0:T(8,128)} %memory_ref.3) | copy-start | bytes 1572868
  1.8 6.8 %copy-start.2 = (bf16[640,256]{1,0:T(8,128)(2,1)S(1)}, bf16[640,256]{1,0:T(8,128)(2,1)}, u32[]{:S(2)}) copy-start(bf16[640,256]{1,0:T(8,128)(2,1)} %refs_4_.1) | copy-start | bytes 983044
  2.2 1.7 %collective-permute-start = (bf16[4,128,256]{2,1,0:T(8,128)(2,1)S(1)}, bf16[4,128,256]{2,1,0:T(8,128)(2,1)S(1)}, u32[]{:S(2)}, u32[]{:S(2)}) collective-permute-start(bf16[4,128,256]{2,1,0:T(8,128)(2,1)S(1)} %get-tuple-element.25), channel_id=1, source_target_pairs={{0,1},{1,0},{2,3},{3,2},{4,5},{5,4},{6,7},{7,6},{8,9},{9,8},{10,11... | collective-permute-start | bytes 786440 | tf_op jit(solution)/shard_map/ppermute | solution.py:251
  3.9 6.8 %collective-permute-start.1 = (bf16[2,128,256]{2,1,0:T(8,128)(2,1)S(1)}, bf16[2,128,256]{2,1,0:T(8,128)(2,1)S(1)}, u32[]{:S(2)}, u32[]{:S(2)}) collective-permute-start(bf16[2,128,256]{2,1,0:T(8,128)(2,1)S(1)} %pad_maximum_fusion.4), channel_id=1, source_target_pairs={{0,2},{1,3},{2,0},{3,1},{4,6},{5,7},{6,4},{7,5},{8,10},{9,11},{10,... | collective-permute-start | bytes 393224 | tf_op jit(solution)/shard_map/ppermute | solution.py:251
  6.9 8.1 %collective-permute-start.2 = (bf16[2,128,256]{2,1,0:T(8,128)(2,1)S(1)}, bf16[2,128,256]{2,1,0:T(8,128)(2,1)S(1)}, u32[]{:S(2)}, u32[]{:S(2)}) collective-permute-start(bf16[2,128,256]{2,1,0:T(8,128)(2,1)S(1)} %pad_maximum_fusion.5), channel_id=1, source_target_pairs={{0,4},{1,5},{2,6},{3,7},{4,0},{5,1},{6,2},{7,3},{8,12},{9,13},{10,... | collective-permute-start | bytes 393224 | tf_op jit(solution)/shard_map/ppermute | solution.py:251
  8.5 6.5 %collective-permute-start.3 = (bf16[2,128,256]{2,1,0:T(8,128)(2,1)S(1)}, bf16[2,128,256]{2,1,0:T(8,128)(2,1)S(1)}, u32[]{:S(2)}, u32[]{:S(2)}) collective-permute-start(bf16[2,128,256]{2,1,0:T(8,128)(2,1)S(1)} %pad_maximum_fusion.6), channel_id=1, source_target_pairs={{0,6},{1,7},{2,4},{3,5},{4,2},{5,3},{6,0},{7,1},{8,14},{9,15},{10,... | collective-permute-start | bytes 393224 | tf_op jit(solution)/shard_map/ppermute | solution.py:251
  16.5 1.6 %collective-permute-start.4 = (bf16[4,129,256]{2,1,0:T(8,128)(2,1)S(1)}, bf16[4,129,256]{2,1,0:T(8,128)(2,1)S(1)}, u32[]{:S(2)}, u32[]{:S(2)}) collective-permute-start(bf16[4,129,256]{2,1,0:T(8,128)(2,1)S(1)} %get-tuple-element.36), channel_id=1, source_target_pairs={{0,1},{1,0},{2,3},{3,2},{4,5},{5,4},{6,7},{7,6},{8,9},{9,8},{10,11... | collective-permute-start | bytes 792584 | tf_op jit(solution)/shard_map/ppermute | solution.py:251
  18.2 10.0 %collective-permute-start.7 = (bf16[258,256]{1,0:T(8,128)(2,1)S(1)}, bf16[258,256]{1,0:T(8,128)(2,1)S(1)}, u32[]{:S(2)}, u32[]{:S(2)}) collective-permute-start(bf16[258,256]{1,0:T(8,128)(2,1)S(1)} %pad_maximum_fusion.3), channel_id=1, source_target_pairs={{0,6},{1,7},{2,4},{3,5},{4,2},{5,3},{6,0},{7,1},{8,14},{9,15},{10,... | collective-permute-start | bytes 396296 | tf_op jit(solution)/shard_map/ppermute | solution.py:251
  19.8 8.0 %collective-permute-start.5 = (bf16[258,256]{1,0:T(8,128)(2,1)S(1)}, bf16[258,256]{1,0:T(8,128)(2,1)S(1)}, u32[]{:S(2)}, u32[]{:S(2)}) collective-permute-start(bf16[258,256]{1,0:T(8,128)(2,1)S(1)} %pad_maximum_fusion.1), channel_id=1, source_target_pairs={{0,2},{1,3},{2,0},{3,1},{4,6},{5,7},{6,4},{7,5},{8,10},{9,11},{10,... | collective-permute-start | bytes 396296 | tf_op jit(solution)/shard_map/ppermute | solution.py:251
  21.3 6.9 %collective-permute-start.6 = (bf16[258,256]{1,0:T(8,128)(2,1)S(1)}, bf16[258,256]{1,0:T(8,128)(2,1)S(1)}, u32[]{:S(2)}, u32[]{:S(2)}) collective-permute-start(bf16[258,256]{1,0:T(8,128)(2,1)S(1)} %pad_maximum_fusion.2), channel_id=1, source_target_pairs={{0,4},{1,5},{2,6},{3,7},{4,0},{5,1},{6,2},{7,3},{8,12},{9,13},{10,... | collective-permute-start | bytes 396296 | tf_op jit(solution)/shard_map/ppermute | solution.py:251
  21.9 11.3 %copy-start.3 = (bf16[256,512]{1,0:T(8,128)(2,1)S(1)}, bf16[256,512]{1,0:T(8,128)(2,1)}, u32[]{:S(2)}) copy-start(bf16[256,512]{1,0:T(8,128)(2,1)} %weight_ref.5) | copy-start | bytes 786436
  21.9 11.3 %copy-start.4 = (f32[256]{0:T(256)S(1)}, f32[256]{0:T(256)}, u32[]{:S(2)}) copy-start(f32[256]{0:T(256)} %param.19) | copy-start | bytes 3076
  28.2 9.4 %copy-start.1 = (f32[512,256]{1,0:T(8,128)S(1)}, f32[512,256]{1,0:T(8,128)}, u32[]{:S(2)}) copy-start(f32[512,256]{1,0:T(8,128)} %memory_ref.3) | copy-start | bytes 1572868
  28.7 6.2 %collective-permute-start.10 = (bf16[128,256]{1,0:T(8,128)(2,1)S(1)}, bf16[128,256]{1,0:T(8,128)(2,1)S(1)}, u32[]{:S(2)}, u32[]{:S(2)}) collective-permute-start(bf16[128,256]{1,0:T(8,128)(2,1)S(1)} %get-tuple-element.53), channel_id=1, source_target_pairs={{0,24},{8,16},{16,8},{24,0},{1,25},{9,17},{17,9},{25,1},{2,26},{10... | collective-permute-start | bytes 196616 | tf_op jit(solution)/shard_map/ppermute | solution.py:251
  32.4 4.4 %collective-permute-start.8 = (bf16[128,256]{1,0:T(8,128)(2,1)S(1)}, bf16[128,256]{1,0:T(8,128)(2,1)S(1)}, u32[]{:S(2)}, u32[]{:S(2)}) collective-permute-start(bf16[128,256]{1,0:T(8,128)(2,1)S(1)} %get-tuple-element.55), channel_id=1, source_target_pairs={{0,8},{8,0},{16,24},{24,16},{1,9},{9,1},{17,25},{25,17},{2,10},{10... | collective-permute-start | bytes 196616 | tf_op jit(solution)/shard_map/ppermute | solution.py:251
  32.4 5.2 %collective-permute-start.9 = (bf16[128,256]{1,0:T(8,128)(2,1)S(1)}, bf16[128,256]{1,0:T(8,128)(2,1)S(1)}, u32[]{:S(2)}, u32[]{:S(2)}) collective-permute-start(bf16[128,256]{1,0:T(8,128)(2,1)S(1)} %get-tuple-element.54), channel_id=1, source_target_pairs={{0,16},{8,24},{16,0},{24,8},{1,17},{9,25},{17,1},{25,9},{2,18},{10... | collective-permute-start | bytes 196616 | tf_op jit(solution)/shard_map/ppermute | solution.py:251
  38.0 4.7 %collective-permute-start.11 = (f16[128,256]{1,0:T(8,128)(2,1)S(1)}, f16[128,256]{1,0:T(8,128)(2,1)S(1)}, u32[]{:S(2)}, u32[]{:S(2)}) collective-permute-start(f16[128,256]{1,0:T(8,128)(2,1)S(1)} %convert_element_type.18), channel_id=1, source_target_pairs={{0,8},{8,0},{16,24},{24,16},{1,9},{9,1},{17,25},{25,17},{2,10},{10... | collective-permute-start | bytes 196616 | tf_op jit(solution)/shard_map/ppermute | solution.py:251
  40.1 6.1 %collective-permute-start.12 = (f16[128,256]{1,0:T(8,128)(2,1)S(1)}, f16[128,256]{1,0:T(8,128)(2,1)S(1)}, u32[]{:S(2)}, u32[]{:S(2)}) collective-permute-start(f16[128,256]{1,0:T(8,128)(2,1)S(1)} %convert_element_type.20), channel_id=1, source_target_pairs={{0,16},{8,24},{16,0},{24,8},{1,17},{9,25},{17,1},{25,9},{2,18},{10... | collective-permute-start | bytes 196616 | tf_op jit(solution)/shard_map/ppermute | solution.py:251
  41.9 6.1 %collective-permute-start.13 = (f16[128,256]{1,0:T(8,128)(2,1)S(1)}, f16[128,256]{1,0:T(8,128)(2,1)S(1)}, u32[]{:S(2)}, u32[]{:S(2)}) collective-permute-start(f16[128,256]{1,0:T(8,128)(2,1)S(1)} %convert_element_type.22), channel_id=1, source_target_pairs={{0,24},{8,16},{16,8},{24,0},{1,25},{9,17},{17,9},{25,1},{2,26},{10... | collective-permute-start | bytes 196616 | tf_op jit(solution)/shard_map/ppermute | solution.py:251

commit v3 on v2

--- a/solution.py
+++ b/solution.py
@@ -6,6 +6,7 @@
 from jax.sharding import PartitionSpec as P
 
 BASE = 32.0
+WEIGHT = 16
 VMEM_LIMIT = 20 << 20
 F32 = jnp.float32
 BF16 = jnp.bfloat16
@@ -30,7 +31,7 @@
         in_specs=specs(len(args), ()),
         out_specs=specs(len(outs), raw_out),
         scratch_shapes=list(scratch),
-        cost_estimate=pl.CostEstimate(flops=flops, bytes_accessed=moved, transcendentals=0),
+        cost_estimate=pl.CostEstimate(flops=WEIGHT * flops, bytes_accessed=moved, transcendentals=0),
         compiler_params=pltpu.CompilerParams(vmem_limit_bytes=VMEM_LIMIT),
     )(*args)
 
@@ -51,25 +52,31 @@
     return jnp.where(row == sublanes, 1.0, 0.0).astype(BF16)
 
 
-def fetch_kernel(lists_ref, memory_ref, out_ref, stale_ref):
+def lists_kernel(lists_ref, out_ref):
+    out_ref[...] = lists_ref[...]
+
+
+def picked(lists_ref, chip, stale):
     me = lax.axis_index("node")
+    hot = hot_rows(lists_ref[pl.ds(me ^ (2 * chip), 1), :], stale.shape[0])
+    return dot(hot, stale).astype(BF16)
+
+
+def pick_kernel(lists_ref, memory_ref, out_ref):
     stale = memory_ref[...].astype(BF16)
-    stale_ref[...] = stale
     for chip in range(out_ref.shape[0]):
-        hot = hot_rows(lists_ref[pl.ds(me ^ (2 * chip + 1), 1), :], stale.shape[0])
-        out_ref[chip] = dot(hot, stale).astype(BF16)
-
-
-def pick_kernel(lists_ref, stale_ref, out_ref):
-    me = lax.axis_index("node")
-    stale = stale_ref[...]
-    for chip in range(out_ref.shape[0]):
-        hot = hot_rows(lists_ref[pl.ds(me ^ (2 * chip), 1), :], stale.shape[0])
-        out_ref[chip] = dot(hot, stale).astype(BF16)
+        out_ref[chip] = picked(lists_ref, chip, stale)
+
+
+def pair_kernel(lists_ref, memory_ref, own_ref, *out_refs):
+    stale = memory_ref[...].astype(BF16)
+    for chip, out_ref in enumerate(out_refs):
+        out_ref[0] = own_ref[chip]
+        out_ref[1] = picked(lists_ref, chip, stale)
 
 
 def prep_kernel(
-    slots_ref, time_ref, freq_ref, weight_ref, bias_ref, hot_ref, turned_ref, base_ref, code_ref
+    slots_ref, packed_ref, weight_ref, hot_ref, turned_ref, base_ref, code_ref, stale_weight_ref
 ):
     me = lax.axis_index("node")
     slots_all, ends = hot_ref.shape
@@ -91,12 +98,16 @@
         lanes = slice(j * capacity, (j + 1) * capacity)
         code = jnp.concatenate([upper[:, lanes], lower[:, lanes]], 1)
         code_ref[j] = code[: code_ref.shape[1]].astype(BF16)
-    width = freq_ref.shape[1]
-    stale_part = weight_ref.shape[0] - width
-    for i in range(time_ref.shape[1] // width):
+    events, _ = base_ref.shape
+    stale_part = stale_weight_ref.shape[0]
+    width = weight_ref.shape[0] - stale_part
+    stale_weight_ref[...] = weight_ref[:stale_part]
+    freq = packed_ref[:, events : events + width]
+    bias = packed_ref[:, events + width :]
+    for i in range(events // width):
         rows = slice(i * width, (i + 1) * width)
-        encoding = jnp.cos(columns_of(time_ref[:, rows]) * freq_ref[...]).astype(BF16)
-        base_ref[rows] = dot(encoding, weight_ref[stale_part:]) + bias_ref[...]
+        encoding = jnp.cos(columns_of(packed_ref[:, rows]) * freq).astype(BF16)
+        base_ref[rows] = dot(encoding, weight_ref[stale_part:]) + bias
 
 
 def gathered(turned_ref, start, tables):
@@ -109,12 +120,9 @@
     return rows
 
 
-def gather_kernel(own_ref, partner_ref, near_ref, turned_ref, rows_ref):
-    capacity, breadth = own_ref.shape
-    tables = [
-        jnp.concatenate([own_ref[...], partner_ref[...]], 0),
-        near_ref[...].reshape(2 * capacity, breadth),
-    ]
+def gather_kernel(own_ref, near_ref, turned_ref, rows_ref):
+    _, capacity, breadth = own_ref.shape
+    tables = [table[...].reshape(2 * capacity, breadth) for table in (own_ref, near_ref)]
     rows_ref[...] = gathered(turned_ref, 0, tables)
 
 
@@ -269,45 +277,47 @@
     node_rows, breadth = memory.shape
     events = src_slot.shape[2]
     chips = blocks // 2
-    lists = jnp.maximum(touched_rows[0, 0], 0)
+    lists = call(
+        lists_kernel, [((blocks, capacity), jnp.int32)], touched_rows[0, 0], flops=1 << 26
+    )[0]
 
     pick_flops = chips * capacity * breadth * node_rows * 2
-    other_picks, stale = call(
-        fetch_kernel,
-        [((chips, capacity, breadth), BF16), ((node_rows, breadth), BF16)],
-        lists,
-        memory,
+    partner_memory = swap("node", memory, 1)
+    partner_lists = swap("node", touched_rows[0, 0], 1)
+    own = call(
+        pick_kernel, [((chips, capacity, breadth), BF16)], lists, memory, flops=pick_flops
+    )[0]
+    tables = call(
+        pair_kernel,
+        [((2, capacity, breadth), BF16)] * chips,
+        partner_lists,
+        partner_memory,
+        own,
         flops=pick_flops,
     )
-    from_partner = swap("node", other_picks, 1)
-    own = call(pick_kernel, [((chips, capacity, breadth), BF16)], lists, stale, flops=pick_flops)[0]
-    sources, targets, times, from_partner = lax.optimization_barrier(
-        (src_slot[0], dst_slot[0], event_time[0], from_partner)
-    )
-    tables = [own[0], from_partner[0]] + [
-        swap("node", jnp.stack([own[chip], from_partner[chip]]), 2 * chip)
-        for chip in range(1, chips)
-    ]
+    sources, targets, times = src_slot[0], dst_slot[0], event_time[0]
+    tables = [swap("node", tables[chip], 2 * chip) if chip else tables[0] for chip in range(chips)]
     ends = 2 * events
     slots = blocks * capacity
-    hot, turned, base, code = call(
+    packed = jnp.concatenate([times, time_freq[None], msg_bias[None]], 1)
+    slot_row = jnp.concatenate([sources, targets], 1)
+    hot, turned, base, code, stale_weight = call(
         prep_kernel,
         [
             ((slots, ends), BF16),
             ((ends, slots), BF16),
             ((events, breadth), F32),
             ((blocks, 1, 2 * capacity), BF16),
+            ((2 * breadth, breadth), BF16),
         ],
-        jnp.concatenate([sources, targets], 1),
-        times,
-        time_freq[None],
+        slot_row,
+        packed,
         msg_weight,
-        msg_bias[None],
     )
     rows = call(
         gather_kernel,
         [((ends, breadth), F32)],
-        *tables[:3],
+        *tables[:2],
         turned,
         flops=8 * ends * capacity * breadth,
     )[0]
@@ -315,10 +325,10 @@
         message_kernel,
         [((chips, capacity + 1, breadth), BF16), ((ends, breadth), BF16)],
         rows,
-        *tables[3:],
+        *tables[2:],
         turned,
         hot,
-        msg_weight,
+        stale_weight,
         base,
         code,
         flops=ends * slots * breadth * 3,

time: 49.1 us -> 49.9 us (1.016)
  waiting for transfers between devices: 20.7 us -> 21.9 us
  other arithmetic: 0.91 us -> 0.12 us
  local copies, waits for them, and re-layouts: 1.2 us -> 1.78 us
    ppermute x14 -> x15, waiting for transfers between devices: 20.7 us -> 21.9 us  [swap(): return lax.ppermute(value, axis, [(i, i ^ distance) for i in range(size)])]
    max x1 -> x0, other arithmetic: 0.75 us -> none  [shards(): lists = jnp.maximum(touched_rows[0, 0], 0)]
    unnamed x20, local copies, waits for them, and re-layouts: 1.08 us -> 1.7 us
    ppermute x14 -> x15, starting transfers between devices: 17.9 us -> 17.7 us  [swap(): return lax.ppermute(value, axis, [(i, i ^ distance) for i in range(size)])]
    pallas_call x12 -> x13, Pallas kernels: 7.86 us -> 7.89 us  [call(): pl.pallas_call(kernel, out_shape=outs, in_specs=specs(len(args), ()), out...]
  transfers between devices with their start and end apart: 14 -> 15, of which waited for: 10 -> 9; matrix products, arithmetic and copies ran while one was open for 0% -> 0% of each run, Pallas kernels for 9% -> 9%
where the time goes in v3:
time: 49.9 us; the launch traced here: 49.6 us
  waiting for transfers between devices  21.9 us (44%)
  starting transfers between devices  17.7 us (35%)
  Pallas kernels  7.89 us (16%)
  local copies, waits for them, and re-layouts  1.78 us (4%)
    ppermute x15, waiting for transfers between devices, swap(): return lax.ppermute(value, axis, [(i, i ^ distance) for i in range(size)])  21.9 us
    ppermute x15, starting transfers between devices, swap(): return lax.ppermute(value, axis, [(i, i ^ distance) for i in range(size)])  17.7 us
    pallas_call x13, Pallas kernels, call(): pl.pallas_call(kernel, out_shape=outs, in_specs=specs(len(args), ()), out...  7.89 us
    unnamed x20, local copies, waits for them, and re-layouts  1.7 us
  transfers between devices with their start and end apart: 15, of which 9 were waited for; matrix products, arithmetic and copies ran while one was open for 0% of the time, Pallas kernels for 9%

profile of v3, /device:TPU:0, one launch (start us, length us, event | category | flops | bytes accessed | tf_op | source)
XLA Modules:
  0.0 49.6 jit_solution(7711458926923542392)
XLA Ops:
  0.0 0.5 collective-permute-start
  0.6 0.7 %copy-done.3 = s32[1,1,8,128]{3,2,1,0:T(8,128)S(1)} copy-done((s32[1,1,8,128]{3,2,1,0:T(8,128)S(1)}, s32[1,1,8,128]{3,2,1,0:T(8,128)}, u32[]{:S(2)}) %copy-start.3) | copy-done | bytes 4120
  1.3 0.7 %copy-done.6 = s32[1,1,512]{2,1,0:T(1,128)S(1)} copy-done((s32[1,1,512]{2,1,0:T(1,128)S(1)}, s32[1,1,512]{2,1,0:T(1,128)}, u32[]{:S(2)}) %copy-start.6) | copy-done | bytes 2072
  2.0 0.4 shard_map.102.own_ref
  2.7 0.3 shard_map.107.rowhot_ref
  3.0 2.0 %shard_map.100 = (bf16[1024,1024]{1,0:T(8,128)(2,1)S(1)}, bf16[1024,1024]{1,0:T(8,128)(2,1)S(1)}, f32[512,256]{1,0:T(8,128)S(1)}, bf16[8,1,256]{2,1,0:T(2,128)(2,1)S(1)}, bf16[512,256]{1,0:T(8,128)(2,1)S(1)}) custom-call(s32[1,1024]{1,0:T(1,128)S(1)} %pad_add_fusion.slots_ref, f32[1,896]{1,0:T(1,128)S(1)} %pad_maximum_fusion.4.packed_ref, ...), custom_call_target="tpu_custom_call" | custom-call | bytes 5320192 | tf_op jit(solution)/shard_map/pallas_call | solution.py:28
  5.0 0.4 shard_map.103
  5.4 3.0 %collective-permute-start.2 = (bf16[2,128,256]{2,1,0:T(8,128)(2,1)S(1)}, bf16[2,128,256]{2,1,0:T(8,128)(2,1)S(1)}, u32[]{:S(2)}, u32[]{:S(2)}) collective-permute-start(bf16[2,128,256]{2,1,0:T(8,128)(2,1)S(1)} %get-tuple-element.26), channel_id=1, source_target_pairs={{0,2},{1,3},{2,0},{3,1},{4,6},{5,7},{6,4},{7,5},{8,10},{9,11},{10,... | collective-permute-start | bytes 393224 | tf_op jit(solution)/shard_map/ppermute | solution.py:259
  8.4 1.5 %collective-permute-start.3 = (bf16[2,128,256]{2,1,0:T(8,128)(2,1)S(1)}, bf16[2,128,256]{2,1,0:T(8,128)(2,1)S(1)}, u32[]{:S(2)}, u32[]{:S(2)}) collective-permute-start(bf16[2,128,256]{2,1,0:T(8,128)(2,1)S(1)} %get-tuple-element.28), channel_id=1, source_target_pairs={{0,4},{1,5},{2,6},{3,7},{4,0},{5,1},{6,2},{7,3},{8,12},{9,13},{10,... | collective-permute-start | bytes 393224 | tf_op jit(solution)/shard_map/ppermute | solution.py:259
  9.9 2.3 %collective-permute-done.2.near_ref = bf16[2,128,256]{2,1,0:T(8,128)(2,1)S(1)} collective-permute-done((bf16[2,128,256]{2,1,0:T(8,128)(2,1)S(1)}, bf16[2,128,256]{2,1,0:T(8,128)(2,1)S(1)}, u32[]{:S(2)}, u32[]{:S(2)}) %collective-permute-start.2) | collective-permute-done | bytes 131104 | tf_op jit(solution)/shard_map/ppermute | solution.py:259
  12.3 0.4 shard_map.104.rows_ref
  12.7 3.7 %collective-permute-done.3.refs_0_ = bf16[2,128,256]{2,1,0:T(8,128)(2,1)S(1)} collective-permute-done((bf16[2,128,256]{2,1,0:T(8,128)(2,1)S(1)}, bf16[2,128,256]{2,1,0:T(8,128)(2,1)S(1)}, u32[]{:S(2)}, u32[]{:S(2)}) %collective-permute-start.3) | collective-permute-done | bytes 131104 | tf_op jit(solution)/shard_map/ppermute | solution.py:259
  16.4 1.5 %shard_map.105 = (bf16[4,129,256]{2,1,0:T(8,128)(2,1)S(1)}, bf16[1024,256]{1,0:T(8,128)(2,1)S(1)}) custom-call(f32[1024,256]{1,0:T(8,128)S(1)} %shard_map.104.rows_ref, bf16[2,128,256]{2,1,0:T(8,128)(2,1)S(1)} %collective-permute-done.3.refs_0_, bf16[2,128,256]{2,1,0:T(8,128)(2,1)S(1)} %collective-permute-done.4.refs_1_, ...), custom_call_target="tpu_custom_call" | custom-call | flops 12884901888 | bytes 7084032 | tf_op jit(solution)/shard_map/pallas_call | solution.py:28
  17.9 0.5 shard_map.106
  18.4 1.1 %collective-permute-done.5 = bf16[4,129,256]{2,1,0:T(8,128)(2,1)S(1)} collective-permute-done((bf16[4,129,256]{2,1,0:T(8,128)(2,1)S(1)}, bf16[4,129,256]{2,1,0:T(8,128)(2,1)S(1)}, u32[]{:S(2)}, u32[]{:S(2)}) %collective-permute-start.5) | collective-permute-done | bytes 264224 | tf_op jit(solution)/shard_map/ppermute | solution.py:259
  19.5 1.6 %collective-permute-start.8 = (bf16[258,256]{1,0:T(8,128)(2,1)S(1)}, bf16[258,256]{1,0:T(8,128)(2,1)S(1)}, u32[]{:S(2)}, u32[]{:S(2)}) collective-permute-start(bf16[258,256]{1,0:T(8,128)(2,1)S(1)} %pad_maximum_fusion.3), channel_id=1, source_target_pairs={{0,6},{1,7},{2,4},{3,5},{4,2},{5,3},{6,0},{7,1},{8,14},{9,15},{10,... | collective-permute-start | bytes 396296 | tf_op jit(solution)/shard_map/ppermute | solution.py:259
  21.1 1.5 %collective-permute-start.6 = (bf16[258,256]{1,0:T(8,128)(2,1)S(1)}, bf16[258,256]{1,0:T(8,128)(2,1)S(1)}, u32[]{:S(2)}, u32[]{:S(2)}) collective-permute-start(bf16[258,256]{1,0:T(8,128)(2,1)S(1)} %pad_maximum_fusion.1), channel_id=1, source_target_pairs={{0,2},{1,3},{2,0},{3,1},{4,6},{5,7},{6,4},{7,5},{8,10},{9,11},{10,... | collective-permute-start | bytes 396296 | tf_op jit(solution)/shard_map/ppermute | solution.py:259
  22.7 0.6 %collective-permute-start.7 = (bf16[258,256]{1,0:T(8,128)(2,1)S(1)}, bf16[258,256]{1,0:T(8,128)(2,1)S(1)}, u32[]{:S(2)}, u32[]{:S(2)}) collective-permute-start(bf16[258,256]{1,0:T(8,128)(2,1)S(1)} %pad_maximum_fusion.2), channel_id=1, source_target_pairs={{0,4},{1,5},{2,6},{3,7},{4,0},{5,1},{6,2},{7,3},{8,12},{9,13},{10,... | collective-permute-start | bytes 396296 | tf_op jit(solution)/shard_map/ppermute | solution.py:259
  23.3 5.8 %collective-permute-done.6.near_ref = bf16[258,256]{1,0:T(8,128)(2,1)S(1)} collective-permute-done((bf16[258,256]{1,0:T(8,128)(2,1)S(1)}, bf16[258,256]{1,0:T(8,128)(2,1)S(1)}, u32[]{:S(2)}, u32[]{:S(2)}) %collective-permute-start.6) | collective-permute-done | bytes 132128 | tf_op jit(solution)/shard_map/ppermute | solution.py:259
  29.1 0.4 shard_map.108
  29.6 0.5 shard_map.109.mean_ref
  30.1 2.7 %collective-permute-start.10 = (bf16[128,256]{1,0:T(8,128)(2,1)S(1)}, bf16[128,256]{1,0:T(8,128)(2,1)S(1)}, u32[]{:S(2)}, u32[]{:S(2)}) collective-permute-start(bf16[128,256]{1,0:T(8,128)(2,1)S(1)} %get-tuple-element.52), channel_id=1, source_target_pairs={{0,16},{8,24},{16,0},{24,8},{1,17},{9,25},{17,1},{25,9},{2,18},{10... | collective-permute-start | bytes 196616 | tf_op jit(solution)/shard_map/ppermute | solution.py:259
  32.8 1.3 %collective-permute-start.11 = (bf16[128,256]{1,0:T(8,128)(2,1)S(1)}, bf16[128,256]{1,0:T(8,128)(2,1)S(1)}, u32[]{:S(2)}, u32[]{:S(2)}) collective-permute-start(bf16[128,256]{1,0:T(8,128)(2,1)S(1)} %get-tuple-element.51), channel_id=1, source_target_pairs={{0,24},{8,16},{16,8},{24,0},{1,25},{9,17},{17,9},{25,1},{2,26},{10... | collective-permute-start | bytes 196616 | tf_op jit(solution)/shard_map/ppermute | solution.py:259
  34.3 0.3 shard_map.110
  34.7 0.7 %collective-permute-done.10.refs_1_ = bf16[128,256]{1,0:T(8,128)(2,1)S(1)} collective-permute-done((bf16[128,256]{1,0:T(8,128)(2,1)S(1)}, bf16[128,256]{1,0:T(8,128)(2,1)S(1)}, u32[]{:S(2)}, u32[]{:S(2)}) %collective-permute-start.10) | collective-permute-done | bytes 65568 | tf_op jit(solution)/shard_map/ppermute | solution.py:259
  35.4 3.6 %collective-permute-done.11.refs_2_ = bf16[128,256]{1,0:T(8,128)(2,1)S(1)} collective-permute-done((bf16[128,256]{1,0:T(8,128)(2,1)S(1)}, bf16[128,256]{1,0:T(8,128)(2,1)S(1)}, u32[]{:S(2)}, u32[]{:S(2)}) %collective-permute-start.11) | collective-permute-done | bytes 65568 | tf_op jit(solution)/shard_map/ppermute | solution.py:259
  39.1 0.4 shard_map.111
  39.7 2.8 %collective-permute-start.13 = (f16[128,256]{1,0:T(8,128)(2,1)S(1)}, f16[128,256]{1,0:T(8,128)(2,1)S(1)}, u32[]{:S(2)}, u32[]{:S(2)}) collective-permute-start(f16[128,256]{1,0:T(8,128)(2,1)S(1)} %convert_element_type.20), channel_id=1, source_target_pairs={{0,16},{8,24},{16,0},{24,8},{1,17},{9,25},{17,1},{25,9},{2,18},{10... | collective-permute-start | bytes 196616 | tf_op jit(solution)/shard_map/ppermute | solution.py:259
  42.5 1.6 %collective-permute-start.14 = (f16[128,256]{1,0:T(8,128)(2,1)S(1)}, f16[128,256]{1,0:T(8,128)(2,1)S(1)}, u32[]{:S(2)}, u32[]{:S(2)}) collective-permute-start(f16[128,256]{1,0:T(8,128)(2,1)S(1)} %convert_element_type.22), channel_id=1, source_target_pairs={{0,24},{8,16},{16,8},{24,0},{1,25},{9,17},{17,9},{25,1},{2,26},{10... | collective-permute-start | bytes 196616 | tf_op jit(solution)/shard_map/ppermute | solution.py:259
  44.1 3.2 %collective-permute-done.13 = f16[128,256]{1,0:T(8,128)(2,1)S(1)} collective-permute-done((f16[128,256]{1,0:T(8,128)(2,1)S(1)}, f16[128,256]{1,0:T(8,128)(2,1)S(1)}, u32[]{:S(2)}, u32[]{:S(2)}) %collective-permute-start.13) | collective-permute-done | bytes 65568 | tf_op jit(solution)/shard_map/ppermute | solution.py:259
  47.4 1.4 %collective-permute-done.14 = f16[128,256]{1,0:T(8,128)(2,1)S(1)} collective-permute-done((f16[128,256]{1,0:T(8,128)(2,1)S(1)}, f16[128,256]{1,0:T(8,128)(2,1)S(1)}, u32[]{:S(2)}, u32[]{:S(2)}) %collective-permute-start.14) | collective-permute-done | bytes 65568 | tf_op jit(solution)/shard_map/ppermute | solution.py:259
  48.8 0.9 %shard_map.112 = f32[512,256]{1,0:T(8,128)} custom-call(f32[512,256]{1,0:T(8,128)S(1)} %get-tuple-element.37.keep_all_ref.keep_ref, f32[512,256]{1,0:T(8,128)S(1)} %get-tuple-element.38.write_all_ref.write_ref, f32[128,256]{1,0:T(8,128)S(1)} %get-tuple-element.39.refs_0_, f32[128,256]{1,0:T(8,128)S(1)} %convert_element_type.19.refs_1_, ...), custom_call_target="tpu_custom_call" | custom-call | bytes 2097152 | tf_op jit(solution)/shard_map/pallas_call | solution.py:28
  (48 shorter events, 1.4 us)
Async XLA Ops:
  0.0 1.9 %copy-start.1 = (f32[512,256]{1,0:T(8,128)S(1)}, f32[512,256]{1,0:T(8,128)}, u32[]{:S(2)}) copy-start(f32[512,256]{1,0:T(8,128)} %memory_ref.3) | copy-start | bytes 1572868
  0.0 5.0 %collective-permute-start = (s32[8,128]{1,0:T(8,128)}, s32[8,128]{1,0:T(8,128)S(1)}, u32[]{:S(2)}, u32[]{:S(2)}) collective-permute-start(s32[8,128]{1,0:T(8,128)} %bitcast.40), channel_id=1, source_target_pairs={{0,1},{1,0},{2,3},{3,2},{4,5},{5,4},{6,7},{7,6},{8,9},{9,8},{10,11... | collective-permute-start | bytes 12296 | tf_op jit(solution)/shard_map/ppermute | solution.py:259
  0.5 4.5 %collective-permute-start.1 = (f32[512,256]{1,0:T(8,128)}, f32[512,256]{1,0:T(8,128)S(1)}, u32[]{:S(2)}, u32[]{:S(2)}) collective-permute-start(f32[512,256]{1,0:T(8,128)} %memory_ref.3), channel_id=1, source_target_pairs={{0,1},{1,0},{2,3},{3,2},{4,5},{5,4},{6,7},{7,6},{8,9},{9,8},{10,11... | collective-permute-start | bytes 1572872 | tf_op jit(solution)/shard_map/ppermute | solution.py:259
  0.6 0.7 %copy-start.3 = (s32[1,1,8,128]{3,2,1,0:T(8,128)S(1)}, s32[1,1,8,128]{3,2,1,0:T(8,128)}, u32[]{:S(2)}) copy-start(s32[1,1,8,128]{3,2,1,0:T(8,128)} %param.14) | copy-start | bytes 12292
  1.2 0.7 %copy-start.6 = (s32[1,1,512]{2,1,0:T(1,128)S(1)}, s32[1,1,512]{2,1,0:T(1,128)}, u32[]{:S(2)}) copy-start(s32[1,1,512]{2,1,0:T(1,128)} %param.12) | copy-start | bytes 6148
  1.2 0.7 %copy-start.7 = (s32[1,1,512]{2,1,0:T(1,128)S(1)}, s32[1,1,512]{2,1,0:T(1,128)}, u32[]{:S(2)}) copy-start(s32[1,1,512]{2,1,0:T(1,128)} %param.11) | copy-start | bytes 6148
  1.9 0.7 %copy-start.5 = (f32[1,1,512]{2,1,0:T(1,128)S(1)}, f32[1,1,512]{2,1,0:T(1,128)}, u32[]{:S(2)}) copy-start(f32[1,1,512]{2,1,0:T(1,128)} %param.13) | copy-start | bytes 6148
  2.0 0.7 %copy-start.8 = (f32[256]{0:T(256)S(1)}, f32[256]{0:T(256)}, u32[]{:S(2)}) copy-start(f32[256]{0:T(256)} %param.17) | copy-start | bytes 3076
  2.0 0.7 %copy-start.9 = (f32[128]{0:T(128)S(1)}, f32[128]{0:T(128)}, u32[]{:S(2)}) copy-start(f32[128]{0:T(128)} %param.15) | copy-start | bytes 1540
  2.0 1.0 %copy-start = (bf16[640,256]{1,0:T(8,128)(2,1)S(1)}, bf16[640,256]{1,0:T(8,128)(2,1)}, u32[]{:S(2)}) copy-start(bf16[640,256]{1,0:T(8,128)(2,1)} %weight_ref.3) | copy-start | bytes 983044
  5.4 6.9 %collective-permute-start.2 = (bf16[2,128,256]{2,1,0:T(8,128)(2,1)S(1)}, bf16[2,128,256]{2,1,0:T(8,128)(2,1)S(1)}, u32[]{:S(2)}, u32[]{:S(2)}) collective-permute-start(bf16[2,128,256]{2,1,0:T(8,128)(2,1)S(1)} %get-tuple-element.26), channel_id=1, source_target_pairs={{0,2},{1,3},{2,0},{3,1},{4,6},{5,7},{6,4},{7,5},{8,10},{9,11},{10,... | collective-permute-start | bytes 393224 | tf_op jit(solution)/shard_map/ppermute | solution.py:259
  8.4 8.0 %collective-permute-start.3 = (bf16[2,128,256]{2,1,0:T(8,128)(2,1)S(1)}, bf16[2,128,256]{2,1,0:T(8,128)(2,1)S(1)}, u32[]{:S(2)}, u32[]{:S(2)}) collective-permute-start(bf16[2,128,256]{2,1,0:T(8,128)(2,1)S(1)} %get-tuple-element.28), channel_id=1, source_target_pairs={{0,4},{1,5},{2,6},{3,7},{4,0},{5,1},{6,2},{7,3},{8,12},{9,13},{10,... | collective-permute-start | bytes 393224 | tf_op jit(solution)/shard_map/ppermute | solution.py:259
  9.9 6.5 %collective-permute-start.4 = (bf16[2,128,256]{2,1,0:T(8,128)(2,1)S(1)}, bf16[2,128,256]{2,1,0:T(8,128)(2,1)S(1)}, u32[]{:S(2)}, u32[]{:S(2)}) collective-permute-start(bf16[2,128,256]{2,1,0:T(8,128)(2,1)S(1)} %get-tuple-element.29), channel_id=1, source_target_pairs={{0,6},{1,7},{2,4},{3,5},{4,2},{5,3},{6,0},{7,1},{8,14},{9,15},{10,... | collective-permute-start | bytes 393224 | tf_op jit(solution)/shard_map/ppermute | solution.py:259
  17.9 1.6 %collective-permute-start.5 = (bf16[4,129,256]{2,1,0:T(8,128)(2,1)S(1)}, bf16[4,129,256]{2,1,0:T(8,128)(2,1)S(1)}, u32[]{:S(2)}, u32[]{:S(2)}) collective-permute-start(bf16[4,129,256]{2,1,0:T(8,128)(2,1)S(1)} %get-tuple-element.34), channel_id=1, source_target_pairs={{0,1},{1,0},{2,3},{3,2},{4,5},{5,4},{6,7},{7,6},{8,9},{9,8},{10,11... | collective-permute-start | bytes 792584 | tf_op jit(solution)/shard_map/ppermute | solution.py:259
  19.5 10.0 %collective-permute-start.8 = (bf16[258,256]{1,0:T(8,128)(2,1)S(1)}, bf16[258,256]{1,0:T(8,128)(2,1)S(1)}, u32[]{:S(2)}, u32[]{:S(2)}) collective-permute-start(bf16[258,256]{1,0:T(8,128)(2,1)S(1)} %pad_maximum_fusion.3), channel_id=1, source_target_pairs={{0,6},{1,7},{2,4},{3,5},{4,2},{5,3},{6,0},{7,1},{8,14},{9,15},{10,... | collective-permute-start | bytes 396296 | tf_op jit(solution)/shard_map/ppermute | solution.py:259
  21.1 8.0 %collective-permute-start.6 = (bf16[258,256]{1,0:T(8,128)(2,1)S(1)}, bf16[258,256]{1,0:T(8,128)(2,1)S(1)}, u32[]{:S(2)}, u32[]{:S(2)}) collective-permute-start(bf16[258,256]{1,0:T(8,128)(2,1)S(1)} %pad_maximum_fusion.1), channel_id=1, source_target_pairs={{0,2},{1,3},{2,0},{3,1},{4,6},{5,7},{6,4},{7,5},{8,10},{9,11},{10,... | collective-permute-start | bytes 396296 | tf_op jit(solution)/shard_map/ppermute | solution.py:259
  22.7 6.9 %collective-permute-start.7 = (bf16[258,256]{1,0:T(8,128)(2,1)S(1)}, bf16[258,256]{1,0:T(8,128)(2,1)S(1)}, u32[]{:S(2)}, u32[]{:S(2)}) collective-permute-start(bf16[258,256]{1,0:T(8,128)(2,1)S(1)} %pad_maximum_fusion.2), channel_id=1, source_target_pairs={{0,4},{1,5},{2,6},{3,7},{4,0},{5,1},{6,2},{7,3},{8,12},{9,13},{10,... | collective-permute-start | bytes 396296 | tf_op jit(solution)/shard_map/ppermute | solution.py:259
  29.6 4.8 %copy-start.2 = (bf16[256,512]{1,0:T(8,128)(2,1)S(1)}, bf16[256,512]{1,0:T(8,128)(2,1)}, u32[]{:S(2)}) copy-start(bf16[256,512]{1,0:T(8,128)(2,1)} %weight_ref.5) | copy-start | bytes 786436
  29.6 4.8 %copy-start.4 = (f32[256]{0:T(256)S(1)}, f32[256]{0:T(256)}, u32[]{:S(2)}) copy-start(f32[256]{0:T(256)} %param.19) | copy-start | bytes 3076
  30.1 5.3 %collective-permute-start.10 = (bf16[128,256]{1,0:T(8,128)(2,1)S(1)}, bf16[128,256]{1,0:T(8,128)(2,1)S(1)}, u32[]{:S(2)}, u32[]{:S(2)}) collective-permute-start(bf16[128,256]{1,0:T(8,128)(2,1)S(1)} %get-tuple-element.52), channel_id=1, source_target_pairs={{0,16},{8,24},{16,0},{24,8},{1,17},{9,25},{17,1},{25,9},{2,18},{10... | collective-permute-start | bytes 196616 | tf_op jit(solution)/shard_map/ppermute | solution.py:259
  32.8 6.2 %collective-permute-start.11 = (bf16[128,256]{1,0:T(8,128)(2,1)S(1)}, bf16[128,256]{1,0:T(8,128)(2,1)S(1)}, u32[]{:S(2)}, u32[]{:S(2)}) collective-permute-start(bf16[128,256]{1,0:T(8,128)(2,1)S(1)} %get-tuple-element.51), channel_id=1, source_target_pairs={{0,24},{8,16},{16,8},{24,0},{1,25},{9,17},{17,9},{25,1},{2,26},{10... | collective-permute-start | bytes 196616 | tf_op jit(solution)/shard_map/ppermute | solution.py:259
  34.1 5.0 %collective-permute-start.9 = (bf16[128,256]{1,0:T(8,128)(2,1)S(1)}, bf16[128,256]{1,0:T(8,128)(2,1)S(1)}, u32[]{:S(2)}, u32[]{:S(2)}) collective-permute-start(bf16[128,256]{1,0:T(8,128)(2,1)S(1)} %get-tuple-element.53), channel_id=1, source_target_pairs={{0,8},{8,0},{16,24},{24,16},{1,9},{9,1},{17,25},{25,17},{2,10},{10... | collective-permute-start | bytes 196616 | tf_op jit(solution)/shard_map/ppermute | solution.py:259
  39.5 4.6 %collective-permute-start.12 = (f16[128,256]{1,0:T(8,128)(2,1)S(1)}, f16[128,256]{1,0:T(8,128)(2,1)S(1)}, u32[]{:S(2)}, u32[]{:S(2)}) collective-permute-start(f16[128,256]{1,0:T(8,128)(2,1)S(1)} %convert_element_type.18), channel_id=1, source_target_pairs={{0,8},{8,0},{16,24},{24,16},{1,9},{9,1},{17,25},{25,17},{2,10},{10... | collective-permute-start | bytes 196616 | tf_op jit(solution)/shard_map/ppermute | solution.py:259
  39.7 7.6 %collective-permute-start.13 = (f16[128,256]{1,0:T(8,128)(2,1)S(1)}, f16[128,256]{1,0:T(8,128)(2,1)S(1)}, u32[]{:S(2)}, u32[]{:S(2)}) collective-permute-start(f16[128,256]{1,0:T(8,128)(2,1)S(1)} %convert_element_type.20), channel_id=1, source_target_pairs={{0,16},{8,24},{16,0},{24,8},{1,17},{9,25},{17,1},{25,9},{2,18},{10... | collective-permute-start | bytes 196616 | tf_op jit(solution)/shard_map/ppermute | solution.py:259
  42.5 6.2 %collective-permute-start.14 = (f16[128,256]{1,0:T(8,128)(2,1)S(1)}, f16[128,256]{1,0:T(8,128)(2,1)S(1)}, u32[]{:S(2)}, u32[]{:S(2)}) collective-permute-start(f16[128,256]{1,0:T(8,128)(2,1)S(1)} %convert_element_type.22), channel_id=1, source_target_pairs={{0,24},{8,16},{16,8},{24,0},{1,25},{9,17},{17,9},{25,1},{2,26},{10... | collective-permute-start | bytes 196616 | tf_op jit(solution)/shard_map/ppermute | solution.py:259

commit v4 on v3

--- a/solution.py
+++ b/solution.py
@@ -16,7 +16,7 @@
     return lax.dot_general(a, b, (dims, ((), ())), preferred_element_type=F32)
 
 
-def call(kernel, outs, *args, flops=0, scratch=(), raw_out=()):
+def call(kernel, outs, *args, flops=0, scratch=(), raw_in=(), raw_out=(), aliases={}):
     outs = [jax.ShapeDtypeStruct(shape, dtype) for shape, dtype in outs]
     moved = sum(x.size * x.dtype.itemsize for x in [*args, *outs])
 
@@ -28,9 +28,10 @@
     return pl.pallas_call(
         kernel,
         out_shape=outs,
-        in_specs=specs(len(args), ()),
+        in_specs=specs(len(args), raw_in),
         out_specs=specs(len(outs), raw_out),
         scratch_shapes=list(scratch),
+        input_output_aliases=aliases,
         cost_estimate=pl.CostEstimate(flops=WEIGHT * flops, bytes_accessed=moved, transcendentals=0),
         compiler_params=pltpu.CompilerParams(vmem_limit_bytes=VMEM_LIMIT),
     )(*args)
@@ -239,19 +240,44 @@
         out[...] = state_ref[me ^ k]
 
 
+def share_copy(keep_ref, write_ref, before, k, made_ref, out_any, sems):
+    share = made_ref.shape[1]
+    start = (lax.axis_index("tm") ^ k) * share
+    rows = pl.ds(pl.multiple_of(start, share), share)
+    made_ref[k] = keep_ref[rows] * before(rows) + write_ref[rows]
+    return pltpu.make_async_copy(made_ref.at[k], out_any.at[rows], sems.at[k])
+
+
+def early_kernel(keep_ref, write_ref, memory_ref, own_ref, out_any, made_ref, sems):
+    own = share_copy(keep_ref, write_ref, lambda rows: own_ref[...], 0, made_ref, out_any, sems)
+    own.start()
+
+    @pl.when(lax.axis_index("tm") == 0)
+    def _():
+        copies = []
+        for k in range(1, made_ref.shape[0]):
+            before = lambda rows: memory_ref[rows]
+            copies.append(share_copy(keep_ref, write_ref, before, k, made_ref, out_any, sems))
+            copies[-1].start()
+        for copy in copies:
+            copy.wait()
+
+    own.wait()
+
+
 def final_kernel(keep_ref, write_ref, *refs):
-    periods = (len(refs) - 3)
-    befores, (out_any, made_ref, sems) = refs[:periods], refs[periods:]
-    me = lax.axis_index("tm")
-    share = befores[0].shape[0]
-    copies = []
-    for k, before in enumerate(befores):
-        rows = pl.ds(pl.multiple_of((me ^ k) * share, share), share)
-        made_ref[k] = keep_ref[rows] * before[...] + write_ref[rows]
-        copies.append(pltpu.make_async_copy(made_ref.at[k], out_any.at[rows], sems.at[k]))
-        copies[-1].start()
-    for copy in copies:
-        copy.wait()
+    befores, (prior_any, out_any, made_ref, sems) = refs[:-4], refs[-4:]
+    del prior_any
+
+    @pl.when(lax.axis_index("tm") != 0)
+    def _():
+        copies = []
+        for k, came in enumerate(befores, 1):
+            before = lambda rows, came=came: came[...]
+            copies.append(share_copy(keep_ref, write_ref, before, k, made_ref, out_any, sems))
+            copies[-1].start()
+        for copy in copies:
+            copy.wait()
 
 
 def swap(axis, value, distance):
@@ -391,18 +417,30 @@
         flops=4 * node_rows * breadth * breadth,
         scratch=[pltpu.VMEM((periods, share, breadth), F32)] * 3,
     )
-    befores = [states[0]] + [
-        swap("tm", states[k].astype(jnp.float16), k).astype(F32)
-        for k in range(1, periods)
-    ]
+    befores = [swap("tm", states[k].astype(jnp.float16), k).astype(F32) for k in range(1, periods)]
+    made = [pltpu.VMEM((periods, share, breadth), F32), pltpu.SemaphoreType.DMA((periods,))]
+    early = call(
+        early_kernel,
+        [((node_rows, breadth), F32)],
+        keep,
+        write,
+        memory,
+        states[0],
+        scratch=made,
+        raw_out=(0,),
+        flops=4 * node_rows * breadth,
+    )[0]
     result = call(
         final_kernel,
         [((node_rows, breadth), F32)],
         keep,
         write,
         *befores,
-        scratch=[pltpu.VMEM((periods, share, breadth), F32), pltpu.SemaphoreType.DMA((periods,))],
+        early,
+        scratch=made,
+        raw_in=(periods + 1,),
         raw_out=(0,),
+        aliases={periods + 1: 0},
     )[0]
     return result[None]
 

time: 49.9 us -> 49.1 us (0.984)
  waiting for transfers between devices: 21.9 us -> 21 us
    ppermute x15, waiting for transfers between devices: 21.9 us -> 21 us  [swap(): return lax.ppermute(value, axis, [(i, i ^ distance) for i in range(size)])]
    pallas_call x13 -> x14, Pallas kernels: 7.89 us -> 7.93 us  [call(): pl.pallas_call(kernel, out_shape=outs, in_specs=specs(len(args), raw_in),...]
  transfers between devices with their start and end apart: 15 -> 15, of which waited for: 9 -> 9; matrix products, arithmetic and copies ran while one was open for 0% -> 0% of each run, Pallas kernels for 9% -> 11%
where the time goes in v4:
time: 49.1 us; the launch traced here: 48.8 us
  waiting for transfers between devices  21 us (43%)
  starting transfers between devices  17.7 us (36%)
  Pallas kernels  7.93 us (16%)
  local copies, waits for them, and re-layouts  1.78 us (4%)
    ppermute x15, waiting for transfers between devices, swap(): return lax.ppermute(value, axis, [(i, i ^ distance) for i in range(size)])  21 us
    ppermute x15, starting transfers between devices, swap(): return lax.ppermute(value, axis, [(i, i ^ distance) for i in range(size)])  17.7 us
    pallas_call x14, Pallas kernels, call(): pl.pallas_call(kernel, out_shape=outs, in_specs=specs(len(args), raw_in),...  7.93 us
    unnamed x20, local copies, waits for them, and re-layouts  1.7 us
  transfers between devices with their start and end apart: 15, of which 9 were waited for; matrix products, arithmetic and copies ran while one was open for 0% of the time, Pallas kernels for 11%

profile of v4, /device:TPU:0, one launch (start us, length us, event | category | flops | bytes accessed | tf_op | source)
XLA Modules:
  0.0 48.8 jit_solution(10457514820296408788)
XLA Ops:
  0.0 0.5 %collective-permute-start = (s32[8,128]{1,0:T(8,128)}, s32[8,128]{1,0:T(8,128)S(1)}, u32[]{:S(2)}, u32[]{:S(2)}) collective-permute-start(s32[8,128]{1,0:T(8,128)} %bitcast.40), channel_id=1, source_target_pairs={{0,1},{1,0},{2,3},{3,2},{4,5},{5,4},{6,7},{7,6},{8,9},{9,8},{10,11... | collective-permute-start | bytes 12296 | tf_op jit(solution)/shard_map/ppermute | solution.py:285
  0.6 0.7 %copy-done.3 = s32[1,1,8,128]{3,2,1,0:T(8,128)S(1)} copy-done((s32[1,1,8,128]{3,2,1,0:T(8,128)S(1)}, s32[1,1,8,128]{3,2,1,0:T(8,128)}, u32[]{:S(2)}) %copy-start.3) | copy-done | bytes 4120
  1.3 0.7 %copy-done.6 = s32[1,1,512]{2,1,0:T(1,128)S(1)} copy-done((s32[1,1,512]{2,1,0:T(1,128)S(1)}, s32[1,1,512]{2,1,0:T(1,128)}, u32[]{:S(2)}) %copy-start.6) | copy-done | bytes 2072
  2.0 0.4 shard_map.102.own_ref
  2.7 0.3 shard_map.107.rowhot_ref
  3.0 2.0 %shard_map.100 = (bf16[1024,1024]{1,0:T(8,128)(2,1)S(1)}, bf16[1024,1024]{1,0:T(8,128)(2,1)S(1)}, f32[512,256]{1,0:T(8,128)S(1)}, bf16[8,1,256]{2,1,0:T(2,128)(2,1)S(1)}, bf16[512,256]{1,0:T(8,128)(2,1)S(1)}) custom-call(s32[1,1024]{1,0:T(1,128)S(1)} %pad_add_fusion.slots_ref, f32[1,896]{1,0:T(1,128)S(1)} %pad_maximum_fusion.4.packed_ref, ...), custom_call_target="tpu_custom_call" | custom-call | bytes 5320192 | tf_op jit(solution)/shard_map/pallas_call | solution.py:28
  5.0 0.4 shard_map.103
  5.4 3.0 %collective-permute-start.2 = (bf16[2,128,256]{2,1,0:T(8,128)(2,1)S(1)}, bf16[2,128,256]{2,1,0:T(8,128)(2,1)S(1)}, u32[]{:S(2)}, u32[]{:S(2)}) collective-permute-start(bf16[2,128,256]{2,1,0:T(8,128)(2,1)S(1)} %get-tuple-element.26), channel_id=1, source_target_pairs={{0,2},{1,3},{2,0},{3,1},{4,6},{5,7},{6,4},{7,5},{8,10},{9,11},{10,... | collective-permute-start | bytes 393224 | tf_op jit(solution)/shard_map/ppermute | solution.py:285
  8.4 1.5 %collective-permute-start.3 = (bf16[2,128,256]{2,1,0:T(8,128)(2,1)S(1)}, bf16[2,128,256]{2,1,0:T(8,128)(2,1)S(1)}, u32[]{:S(2)}, u32[]{:S(2)}) collective-permute-start(bf16[2,128,256]{2,1,0:T(8,128)(2,1)S(1)} %get-tuple-element.28), channel_id=1, source_target_pairs={{0,4},{1,5},{2,6},{3,7},{4,0},{5,1},{6,2},{7,3},{8,12},{9,13},{10,... | collective-permute-start | bytes 393224 | tf_op jit(solution)/shard_map/ppermute | solution.py:285
  9.9 2.3 %collective-permute-done.2.near_ref = bf16[2,128,256]{2,1,0:T(8,128)(2,1)S(1)} collective-permute-done((bf16[2,128,256]{2,1,0:T(8,128)(2,1)S(1)}, bf16[2,128,256]{2,1,0:T(8,128)(2,1)S(1)}, u32[]{:S(2)}, u32[]{:S(2)}) %collective-permute-start.2) | collective-permute-done | bytes 131104 | tf_op jit(solution)/shard_map/ppermute | solution.py:285
  12.3 0.4 shard_map.104.rows_ref
  12.7 3.7 %collective-permute-done.3.refs_0_ = bf16[2,128,256]{2,1,0:T(8,128)(2,1)S(1)} collective-permute-done((bf16[2,128,256]{2,1,0:T(8,128)(2,1)S(1)}, bf16[2,128,256]{2,1,0:T(8,128)(2,1)S(1)}, u32[]{:S(2)}, u32[]{:S(2)}) %collective-permute-start.3) | collective-permute-done | bytes 131104 | tf_op jit(solution)/shard_map/ppermute | solution.py:285
  16.4 1.5 %shard_map.105 = (bf16[4,129,256]{2,1,0:T(8,128)(2,1)S(1)}, bf16[1024,256]{1,0:T(8,128)(2,1)S(1)}) custom-call(f32[1024,256]{1,0:T(8,128)S(1)} %shard_map.104.rows_ref, bf16[2,128,256]{2,1,0:T(8,128)(2,1)S(1)} %collective-permute-done.3.refs_0_, bf16[2,128,256]{2,1,0:T(8,128)(2,1)S(1)} %collective-permute-done.4.refs_1_, ...), custom_call_target="tpu_custom_call" | custom-call | flops 12884901888 | bytes 7084032 | tf_op jit(solution)/shard_map/pallas_call | solution.py:28
  17.9 0.5 shard_map.106
  18.4 1.1 %collective-permute-done.5 = bf16[4,129,256]{2,1,0:T(8,128)(2,1)S(1)} collective-permute-done((bf16[4,129,256]{2,1,0:T(8,128)(2,1)S(1)}, bf16[4,129,256]{2,1,0:T(8,128)(2,1)S(1)}, u32[]{:S(2)}, u32[]{:S(2)}) %collective-permute-start.5) | collective-permute-done | bytes 264224 | tf_op jit(solution)/shard_map/ppermute | solution.py:285
  19.5 1.6 %collective-permute-start.8 = (bf16[258,256]{1,0:T(8,128)(2,1)S(1)}, bf16[258,256]{1,0:T(8,128)(2,1)S(1)}, u32[]{:S(2)}, u32[]{:S(2)}) collective-permute-start(bf16[258,256]{1,0:T(8,128)(2,1)S(1)} %pad_maximum_fusion.3), channel_id=1, source_target_pairs={{0,6},{1,7},{2,4},{3,5},{4,2},{5,3},{6,0},{7,1},{8,14},{9,15},{10,... | collective-permute-start | bytes 396296 | tf_op jit(solution)/shard_map/ppermute | solution.py:285
  21.1 1.5 %collective-permute-start.6 = (bf16[258,256]{1,0:T(8,128)(2,1)S(1)}, bf16[258,256]{1,0:T(8,128)(2,1)S(1)}, u32[]{:S(2)}, u32[]{:S(2)}) collective-permute-start(bf16[258,256]{1,0:T(8,128)(2,1)S(1)} %pad_maximum_fusion.1), channel_id=1, source_target_pairs={{0,2},{1,3},{2,0},{3,1},{4,6},{5,7},{6,4},{7,5},{8,10},{9,11},{10,... | collective-permute-start | bytes 396296 | tf_op jit(solution)/shard_map/ppermute | solution.py:285
  22.7 0.6 %collective-permute-start.7 = (bf16[258,256]{1,0:T(8,128)(2,1)S(1)}, bf16[258,256]{1,0:T(8,128)(2,1)S(1)}, u32[]{:S(2)}, u32[]{:S(2)}) collective-permute-start(bf16[258,256]{1,0:T(8,128)(2,1)S(1)} %pad_maximum_fusion.2), channel_id=1, source_target_pairs={{0,4},{1,5},{2,6},{3,7},{4,0},{5,1},{6,2},{7,3},{8,12},{9,13},{10,... | collective-permute-start | bytes 396296 | tf_op jit(solution)/shard_map/ppermute | solution.py:285
  23.3 5.8 %collective-permute-done.6.near_ref = bf16[258,256]{1,0:T(8,128)(2,1)S(1)} collective-permute-done((bf16[258,256]{1,0:T(8,128)(2,1)S(1)}, bf16[258,256]{1,0:T(8,128)(2,1)S(1)}, u32[]{:S(2)}, u32[]{:S(2)}) %collective-permute-start.6) | collective-permute-done | bytes 132128 | tf_op jit(solution)/shard_map/ppermute | solution.py:285
  29.1 0.4 shard_map.108
  29.6 0.5 shard_map.109.mean_ref
  30.1 2.7 %collective-permute-start.10 = (bf16[128,256]{1,0:T(8,128)(2,1)S(1)}, bf16[128,256]{1,0:T(8,128)(2,1)S(1)}, u32[]{:S(2)}, u32[]{:S(2)}) collective-permute-start(bf16[128,256]{1,0:T(8,128)(2,1)S(1)} %get-tuple-element.52), channel_id=1, source_target_pairs={{0,16},{8,24},{16,0},{24,8},{1,17},{9,25},{17,1},{25,9},{2,18},{10... | collective-permute-start | bytes 196616 | tf_op jit(solution)/shard_map/ppermute | solution.py:285
  32.8 1.3 %collective-permute-start.11 = (bf16[128,256]{1,0:T(8,128)(2,1)S(1)}, bf16[128,256]{1,0:T(8,128)(2,1)S(1)}, u32[]{:S(2)}, u32[]{:S(2)}) collective-permute-start(bf16[128,256]{1,0:T(8,128)(2,1)S(1)} %get-tuple-element.51), channel_id=1, source_target_pairs={{0,24},{8,16},{16,8},{24,0},{1,25},{9,17},{17,9},{25,1},{2,26},{10... | collective-permute-start | bytes 196616 | tf_op jit(solution)/shard_map/ppermute | solution.py:285
  34.3 0.3 shard_map.110
  34.7 0.7 %collective-permute-done.10.refs_1_ = bf16[128,256]{1,0:T(8,128)(2,1)S(1)} collective-permute-done((bf16[128,256]{1,0:T(8,128)(2,1)S(1)}, bf16[128,256]{1,0:T(8,128)(2,1)S(1)}, u32[]{:S(2)}, u32[]{:S(2)}) %collective-permute-start.10) | collective-permute-done | bytes 65568 | tf_op jit(solution)/shard_map/ppermute | solution.py:285
  35.4 3.6 %collective-permute-done.11.refs_2_ = bf16[128,256]{1,0:T(8,128)(2,1)S(1)} collective-permute-done((bf16[128,256]{1,0:T(8,128)(2,1)S(1)}, bf16[128,256]{1,0:T(8,128)(2,1)S(1)}, u32[]{:S(2)}, u32[]{:S(2)}) %collective-permute-start.11) | collective-permute-done | bytes 65568 | tf_op jit(solution)/shard_map/ppermute | solution.py:285
  39.1 0.4 shard_map.111
  39.7 2.8 %collective-permute-start.13 = (f16[128,256]{1,0:T(8,128)(2,1)S(1)}, f16[128,256]{1,0:T(8,128)(2,1)S(1)}, u32[]{:S(2)}, u32[]{:S(2)}) collective-permute-start(f16[128,256]{1,0:T(8,128)(2,1)S(1)} %convert_element_type.20), channel_id=1, source_target_pairs={{0,16},{8,24},{16,0},{24,8},{1,17},{9,25},{17,1},{25,9},{2,18},{10... | collective-permute-start | bytes 196616 | tf_op jit(solution)/shard_map/ppermute | solution.py:285
  42.5 1.6 %collective-permute-start.14 = (f16[128,256]{1,0:T(8,128)(2,1)S(1)}, f16[128,256]{1,0:T(8,128)(2,1)S(1)}, u32[]{:S(2)}, u32[]{:S(2)}) collective-permute-start(f16[128,256]{1,0:T(8,128)(2,1)S(1)} %convert_element_type.22), channel_id=1, source_target_pairs={{0,24},{8,16},{16,8},{24,0},{1,25},{9,17},{17,9},{25,1},{2,26},{10... | collective-permute-start | bytes 196616 | tf_op jit(solution)/shard_map/ppermute | solution.py:285
  44.1 0.8 %shard_map.112.refs_3_ = f32[512,256]{1,0:T(8,128)} custom-call(f32[512,256]{1,0:T(8,128)S(1)} %get-tuple-element.37.keep_all_ref.keep_ref, f32[512,256]{1,0:T(8,128)S(1)} %get-tuple-element.38.write_all_ref.write_ref, f32[512,256]{1,0:T(8,128)S(1)} %copy-done, f32[128,256]{1,0:T(8,128)S(1)} %get-tuple-element.42.own_ref), custom_call_target="tpu_custom_call" | custom-call | flops 8388608 | bytes 2228224 | tf_op jit(solution)/shard_map/pallas_call | solution.py:28
  45.0 2.4 %collective-permute-done.13 = f16[128,256]{1,0:T(8,128)(2,1)S(1)} collective-permute-done((f16[128,256]{1,0:T(8,128)(2,1)S(1)}, f16[128,256]{1,0:T(8,128)(2,1)S(1)}, u32[]{:S(2)}, u32[]{:S(2)}) %collective-permute-start.13) | collective-permute-done | bytes 65568 | tf_op jit(solution)/shard_map/ppermute | solution.py:285
  47.4 1.4 %collective-permute-done.14 = f16[128,256]{1,0:T(8,128)(2,1)S(1)} collective-permute-done((f16[128,256]{1,0:T(8,128)(2,1)S(1)}, f16[128,256]{1,0:T(8,128)(2,1)S(1)}, u32[]{:S(2)}, u32[]{:S(2)}) %collective-permute-start.14) | collective-permute-done | bytes 65568 | tf_op jit(solution)/shard_map/ppermute | solution.py:285
  (49 shorter events, 1.4 us)
Async XLA Ops:
  0.0 1.9 %copy-start = (f32[512,256]{1,0:T(8,128)S(1)}, f32[512,256]{1,0:T(8,128)}, u32[]{:S(2)}) copy-start(f32[512,256]{1,0:T(8,128)} %memory_ref.5) | copy-start | bytes 1572868
  0.0 5.0 %collective-permute-start = (s32[8,128]{1,0:T(8,128)}, s32[8,128]{1,0:T(8,128)S(1)}, u32[]{:S(2)}, u32[]{:S(2)}) collective-permute-start(s32[8,128]{1,0:T(8,128)} %bitcast.40), channel_id=1, source_target_pairs={{0,1},{1,0},{2,3},{3,2},{4,5},{5,4},{6,7},{7,6},{8,9},{9,8},{10,11... | collective-permute-start | bytes 12296 | tf_op jit(solution)/shard_map/ppermute | solution.py:285
  0.5 4.5 %collective-permute-start.1 = (f32[512,256]{1,0:T(8,128)}, f32[512,256]{1,0:T(8,128)S(1)}, u32[]{:S(2)}, u32[]{:S(2)}) collective-permute-start(f32[512,256]{1,0:T(8,128)} %memory_ref.5), channel_id=1, source_target_pairs={{0,1},{1,0},{2,3},{3,2},{4,5},{5,4},{6,7},{7,6},{8,9},{9,8},{10,11... | collective-permute-start | bytes 1572872 | tf_op jit(solution)/shard_map/ppermute | solution.py:285
  0.6 0.7 %copy-start.3 = (s32[1,1,8,128]{3,2,1,0:T(8,128)S(1)}, s32[1,1,8,128]{3,2,1,0:T(8,128)}, u32[]{:S(2)}) copy-start(s32[1,1,8,128]{3,2,1,0:T(8,128)} %param.14) | copy-start | bytes 12292
  1.2 0.7 %copy-start.6 = (s32[1,1,512]{2,1,0:T(1,128)S(1)}, s32[1,1,512]{2,1,0:T(1,128)}, u32[]{:S(2)}) copy-start(s32[1,1,512]{2,1,0:T(1,128)} %param.12) | copy-start | bytes 6148
  1.2 0.7 %copy-start.7 = (s32[1,1,512]{2,1,0:T(1,128)S(1)}, s32[1,1,512]{2,1,0:T(1,128)}, u32[]{:S(2)}) copy-start(s32[1,1,512]{2,1,0:T(1,128)} %param.11) | copy-start | bytes 6148
  1.9 0.7 %copy-start.5 = (f32[1,1,512]{2,1,0:T(1,128)S(1)}, f32[1,1,512]{2,1,0:T(1,128)}, u32[]{:S(2)}) copy-start(f32[1,1,512]{2,1,0:T(1,128)} %param.13) | copy-start | bytes 6148
  2.0 0.7 %copy-start.8 = (f32[256]{0:T(256)S(1)}, f32[256]{0:T(256)}, u32[]{:S(2)}) copy-start(f32[256]{0:T(256)} %param.17) | copy-start | bytes 3076
  2.0 0.7 %copy-start.9 = (f32[128]{0:T(128)S(1)}, f32[128]{0:T(128)}, u32[]{:S(2)}) copy-start(f32[128]{0:T(128)} %param.15) | copy-start | bytes 1540
  2.0 1.0 %copy-start.1 = (bf16[640,256]{1,0:T(8,128)(2,1)S(1)}, bf16[640,256]{1,0:T(8,128)(2,1)}, u32[]{:S(2)}) copy-start(bf16[640,256]{1,0:T(8,128)(2,1)} %weight_ref.3) | copy-start | bytes 983044
  5.4 6.9 %collective-permute-start.2 = (bf16[2,128,256]{2,1,0:T(8,128)(2,1)S(1)}, bf16[2,128,256]{2,1,0:T(8,128)(2,1)S(1)}, u32[]{:S(2)}, u32[]{:S(2)}) collective-permute-start(bf16[2,128,256]{2,1,0:T(8,128)(2,1)S(1)} %get-tuple-element.26), channel_id=1, source_target_pairs={{0,2},{1,3},{2,0},{3,1},{4,6},{5,7},{6,4},{7,5},{8,10},{9,11},{10,... | collective-permute-start | bytes 393224 | tf_op jit(solution)/shard_map/ppermute | solution.py:285
  8.4 8.0 %collective-permute-start.3 = (bf16[2,128,256]{2,1,0:T(8,128)(2,1)S(1)}, bf16[2,128,256]{2,1,0:T(8,128)(2,1)S(1)}, u32[]{:S(2)}, u32[]{:S(2)}) collective-permute-start(bf16[2,128,256]{2,1,0:T(8,128)(2,1)S(1)} %get-tuple-element.28), channel_id=1, source_target_pairs={{0,4},{1,5},{2,6},{3,7},{4,0},{5,1},{6,2},{7,3},{8,12},{9,13},{10,... | collective-permute-start | bytes 393224 | tf_op jit(solution)/shard_map/ppermute | solution.py:285
  9.9 6.5 %collective-permute-start.4 = (bf16[2,128,256]{2,1,0:T(8,128)(2,1)S(1)}, bf16[2,128,256]{2,1,0:T(8,128)(2,1)S(1)}, u32[]{:S(2)}, u32[]{:S(2)}) collective-permute-start(bf16[2,128,256]{2,1,0:T(8,128)(2,1)S(1)} %get-tuple-element.29), channel_id=1, source_target_pairs={{0,6},{1,7},{2,4},{3,5},{4,2},{5,3},{6,0},{7,1},{8,14},{9,15},{10,... | collective-permute-start | bytes 393224 | tf_op jit(solution)/shard_map/ppermute | solution.py:285
  17.9 1.6 %collective-permute-start.5 = (bf16[4,129,256]{2,1,0:T(8,128)(2,1)S(1)}, bf16[4,129,256]{2,1,0:T(8,128)(2,1)S(1)}, u32[]{:S(2)}, u32[]{:S(2)}) collective-permute-start(bf16[4,129,256]{2,1,0:T(8,128)(2,1)S(1)} %get-tuple-element.34), channel_id=1, source_target_pairs={{0,1},{1,0},{2,3},{3,2},{4,5},{5,4},{6,7},{7,6},{8,9},{9,8},{10,11... | collective-permute-start | bytes 792584 | tf_op jit(solution)/shard_map/ppermute | solution.py:285
  19.5 10.0 %collective-permute-start.8 = (bf16[258,256]{1,0:T(8,128)(2,1)S(1)}, bf16[258,256]{1,0:T(8,128)(2,1)S(1)}, u32[]{:S(2)}, u32[]{:S(2)}) collective-permute-start(bf16[258,256]{1,0:T(8,128)(2,1)S(1)} %pad_maximum_fusion.3), channel_id=1, source_target_pairs={{0,6},{1,7},{2,4},{3,5},{4,2},{5,3},{6,0},{7,1},{8,14},{9,15},{10,... | collective-permute-start | bytes 396296 | tf_op jit(solution)/shard_map/ppermute | solution.py:285
  21.1 8.0 %collective-permute-start.6 = (bf16[258,256]{1,0:T(8,128)(2,1)S(1)}, bf16[258,256]{1,0:T(8,128)(2,1)S(1)}, u32[]{:S(2)}, u32[]{:S(2)}) collective-permute-start(bf16[258,256]{1,0:T(8,128)(2,1)S(1)} %pad_maximum_fusion.1), channel_id=1, source_target_pairs={{0,2},{1,3},{2,0},{3,1},{4,6},{5,7},{6,4},{7,5},{8,10},{9,11},{10,... | collective-permute-start | bytes 396296 | tf_op jit(solution)/shard_map/ppermute | solution.py:285
  22.7 6.9 %collective-permute-start.7 = (bf16[258,256]{1,0:T(8,128)(2,1)S(1)}, bf16[258,256]{1,0:T(8,128)(2,1)S(1)}, u32[]{:S(2)}, u32[]{:S(2)}) collective-permute-start(bf16[258,256]{1,0:T(8,128)(2,1)S(1)} %pad_maximum_fusion.2), channel_id=1, source_target_pairs={{0,4},{1,5},{2,6},{3,7},{4,0},{5,1},{6,2},{7,3},{8,12},{9,13},{10,... | collective-permute-start | bytes 396296 | tf_op jit(solution)/shard_map/ppermute | solution.py:285
  29.6 4.8 %copy-start.2 = (bf16[256,512]{1,0:T(8,128)(2,1)S(1)}, bf16[256,512]{1,0:T(8,128)(2,1)}, u32[]{:S(2)}) copy-start(bf16[256,512]{1,0:T(8,128)(2,1)} %weight_ref.5) | copy-start | bytes 786436
  29.6 4.8 %copy-start.4 = (f32[256]{0:T(256)S(1)}, f32[256]{0:T(256)}, u32[]{:S(2)}) copy-start(f32[256]{0:T(256)} %param.19) | copy-start | bytes 3076
  30.1 5.3 %collective-permute-start.10 = (bf16[128,256]{1,0:T(8,128)(2,1)S(1)}, bf16[128,256]{1,0:T(8,128)(2,1)S(1)}, u32[]{:S(2)}, u32[]{:S(2)}) collective-permute-start(bf16[128,256]{1,0:T(8,128)(2,1)S(1)} %get-tuple-element.52), channel_id=1, source_target_pairs={{0,16},{8,24},{16,0},{24,8},{1,17},{9,25},{17,1},{25,9},{2,18},{10... | collective-permute-start | bytes 196616 | tf_op jit(solution)/shard_map/ppermute | solution.py:285
  32.8 6.2 %collective-permute-start.11 = (bf16[128,256]{1,0:T(8,128)(2,1)S(1)}, bf16[128,256]{1,0:T(8,128)(2,1)S(1)}, u32[]{:S(2)}, u32[]{:S(2)}) collective-permute-start(bf16[128,256]{1,0:T(8,128)(2,1)S(1)} %get-tuple-element.51), channel_id=1, source_target_pairs={{0,24},{8,16},{16,8},{24,0},{1,25},{9,17},{17,9},{25,1},{2,26},{10... | collective-permute-start | bytes 196616 | tf_op jit(solution)/shard_map/ppermute | solution.py:285
  34.1 5.0 %collective-permute-start.9 = (bf16[128,256]{1,0:T(8,128)(2,1)S(1)}, bf16[128,256]{1,0:T(8,128)(2,1)S(1)}, u32[]{:S(2)}, u32[]{:S(2)}) collective-permute-start(bf16[128,256]{1,0:T(8,128)(2,1)S(1)} %get-tuple-element.53), channel_id=1, source_target_pairs={{0,8},{8,0},{16,24},{24,16},{1,9},{9,1},{17,25},{25,17},{2,10},{10... | collective-permute-start | bytes 196616 | tf_op jit(solution)/shard_map/ppermute | solution.py:285
  39.5 5.5 %collective-permute-start.12 = (f16[128,256]{1,0:T(8,128)(2,1)S(1)}, f16[128,256]{1,0:T(8,128)(2,1)S(1)}, u32[]{:S(2)}, u32[]{:S(2)}) collective-permute-start(f16[128,256]{1,0:T(8,128)(2,1)S(1)} %convert_element_type.18), channel_id=1, source_target_pairs={{0,8},{8,0},{16,24},{24,16},{1,9},{9,1},{17,25},{25,17},{2,10},{10... | collective-permute-start | bytes 196616 | tf_op jit(solution)/shard_map/ppermute | solution.py:285
  39.7 7.6 %collective-permute-start.13 = (f16[128,256]{1,0:T(8,128)(2,1)S(1)}, f16[128,256]{1,0:T(8,128)(2,1)S(1)}, u32[]{:S(2)}, u32[]{:S(2)}) collective-permute-start(f16[128,256]{1,0:T(8,128)(2,1)S(1)} %convert_element_type.20), channel_id=1, source_target_pairs={{0,16},{8,24},{16,0},{24,8},{1,17},{9,25},{17,1},{25,9},{2,18},{10... | collective-permute-start | bytes 196616 | tf_op jit(solution)/shard_map/ppermute | solution.py:285
  42.5 6.2 %collective-permute-start.14 = (f16[128,256]{1,0:T(8,128)(2,1)S(1)}, f16[128,256]{1,0:T(8,128)(2,1)S(1)}, u32[]{:S(2)}, u32[]{:S(2)}) collective-permute-start(f16[128,256]{1,0:T(8,128)(2,1)S(1)} %convert_element_type.22), channel_id=1, source_target_pairs={{0,24},{8,16},{16,8},{24,0},{1,25},{9,17},{17,9},{25,1},{2,26},{10... | collective-permute-start | bytes 196616 | tf_op jit(solution)/shard_map/ppermute | solution.py:285

commit v5 on v4

--- a/solution.py
+++ b/solution.py
@@ -1,3 +1,5 @@
+import functools
+
 import jax
 import jax.numpy as jnp
 from jax import lax
@@ -127,6 +129,15 @@
     rows_ref[...] = gathered(turned_ref, 0, tables)
 
 
+def other_sums(chosen, hot_ref, messages, code_ref, out_ref):
+    capacity = code_ref.shape[2] // 2
+    for i, chip in enumerate(chosen):
+        j = 2 * chip + 1
+        sums = dot(hot_ref[j * capacity : (j + 1) * capacity], messages)
+        out_ref[i, :capacity] = sums.astype(BF16)
+        out_ref[i, capacity:] = code_ref[j]
+
+
 def message_kernel(rows_ref, *refs):
     tables, (turned_ref, hot_ref, weight_ref, base_ref, code_ref) = refs[:-7], refs[-7:-2]
     other_ref, message_ref = refs[-2:]
@@ -139,12 +150,11 @@
     base = base_ref[...]
     message_ref[:events] = jnp.maximum(first[:events] + second[events:] + base, 0.0).astype(BF16)
     message_ref[events:] = jnp.maximum(first[events:] + second[:events] + base, 0.0).astype(BF16)
-    messages = message_ref[...]
-    for chip in range(other_ref.shape[0]):
-        j = 2 * chip + 1
-        sums = dot(hot_ref[j * capacity : (j + 1) * capacity], messages)
-        other_ref[chip, :capacity] = sums.astype(BF16)
-        other_ref[chip, capacity:] = code_ref[j]
+    other_sums([1], hot_ref, message_ref[...], code_ref, other_ref)
+
+
+def rest_kernel(chosen, hot_ref, message_ref, code_ref, other_ref):
+    other_sums(chosen, hot_ref, message_ref[...], code_ref, other_ref)
 
 
 def own_kernel(hot_ref, message_ref, own_ref):
@@ -349,7 +359,7 @@
     )[0]
     other, messages = call(
         message_kernel,
-        [((chips, capacity + 1, breadth), BF16), ((ends, breadth), BF16)],
+        [((1, capacity + 1, breadth), BF16), ((ends, breadth), BF16)],
         rows,
         *tables[2:],
         turned,
@@ -359,7 +369,18 @@
         code,
         flops=ends * slots * breadth * 3,
     )
-    partner = swap("node", other, 1)
+    chosen = [chip for chip in range(chips) if chip != 1]
+    rest = call(
+        functools.partial(rest_kernel, chosen),
+        [((chips - 1, capacity + 1, breadth), BF16)],
+        hot,
+        messages,
+        code,
+        flops=ends * slots * breadth,
+    )[0]
+    came = swap("node", other, 1)
+    rest = swap("node", rest, 1)
+    partner = {1: came[0]} | {chip: rest[i] for i, chip in enumerate(chosen)}
     own_sums = call(
         own_kernel,
         [((chips, capacity, breadth), BF16)],
@@ -369,8 +390,9 @@
     )[0]
     loads = []
     for chip in range(chips):
+        theirs = partner[chip]
         load = jnp.concatenate(
-            [own_sums[chip], partner[chip, :capacity], code[2 * chip], partner[chip, capacity:]], 0
+            [own_sums[chip], theirs[:capacity], code[2 * chip], theirs[capacity:]], 0
         )
         loads.append(swap("node", load, 2 * chip) if chip else load)
     rowhot = call(rows_kernel, [((node_rows, slots), BF16)], lists)[0]

time: 49.1 us -> 51.1 us (1.041)
  waiting for transfers between devices: 21 us -> 22.2 us
  starting transfers between devices: 17.7 us -> 18.4 us
    ppermute x15 -> x16, waiting for transfers between devices: 21 us -> 22.2 us  [swap(): return lax.ppermute(value, axis, [(i, i ^ distance) for i in range(size)])]
    ppermute x15 -> x16, starting transfers between devices: 17.7 us -> 18.4 us  [swap(): return lax.ppermute(value, axis, [(i, i ^ distance) for i in range(size)])]
    pallas_call x14 -> x15, Pallas kernels: 7.93 us -> 8.08 us  [call(): pl.pallas_call(kernel, out_shape=outs, in_specs=specs(len(args), raw_in),...]
  transfers between devices with their start and end apart: 15 -> 16, of which waited for: 9 -> 10; matrix products, arithmetic and copies ran while one was open for 0% -> 0% of each run, Pallas kernels for 11% -> 9%
where the time goes in v5:
time: 51.1 us; the launch traced here: 50.9 us
  waiting for transfers between devices  22.2 us (43%)
  starting transfers between devices  18.4 us (36%)
  Pallas kernels  8.08 us (16%)
  local copies, waits for them, and re-layouts  1.78 us (3%)
    ppermute x16, waiting for transfers between devices, swap(): return lax.ppermute(value, axis, [(i, i ^ distance) for i in range(size)])  22.2 us
    ppermute x16, starting transfers between devices, swap(): return lax.ppermute(value, axis, [(i, i ^ distance) for i in range(size)])  18.4 us
    pallas_call x15, Pallas kernels, call(): pl.pallas_call(kernel, out_shape=outs, in_specs=specs(len(args), raw_in),...  8.08 us
    unnamed x20, local copies, waits for them, and re-layouts  1.7 us
  transfers between devices with their start and end apart: 16, of which 10 were waited for; matrix products, arithmetic and copies ran while one was open for 0% of the time, Pallas kernels for 9%

profile of v5, /device:TPU:0, one launch (start us, length us, event | category | flops | bytes accessed | tf_op | source)
XLA Modules:
  0.0 50.9 jit_solution(3731906036584424597)
XLA Ops:
  0.0 0.5 collective-permute-start
  0.6 0.7 %copy-done.3 = s32[1,1,8,128]{3,2,1,0:T(8,128)S(1)} copy-done((s32[1,1,8,128]{3,2,1,0:T(8,128)S(1)}, s32[1,1,8,128]{3,2,1,0:T(8,128)}, u32[]{:S(2)}) %copy-start.3) | copy-done | bytes 4120
  1.3 0.7 %copy-done.6 = s32[1,1,512]{2,1,0:T(1,128)S(1)} copy-done((s32[1,1,512]{2,1,0:T(1,128)S(1)}, s32[1,1,512]{2,1,0:T(1,128)}, u32[]{:S(2)}) %copy-start.6) | copy-done | bytes 2072
  3.0 2.0 %shard_map.100 = (bf16[1024,1024]{1,0:T(8,128)(2,1)S(1)}, bf16[1024,1024]{1,0:T(8,128)(2,1)S(1)}, f32[512,256]{1,0:T(8,128)S(1)}, bf16[8,1,256]{2,1,0:T(2,128)(2,1)S(1)}, bf16[512,256]{1,0:T(8,128)(2,1)S(1)}) custom-call(s32[1,1024]{1,0:T(1,128)S(1)} %pad_add_fusion.slots_ref, f32[1,896]{1,0:T(1,128)S(1)} %pad_maximum_fusion.4.packed_ref, ...), custom_call_target="tpu_custom_call" | custom-call | bytes 5320192 | tf_op jit(solution)/shard_map/pallas_call | solution.py:30
  5.0 0.4 shard_map.103
  5.4 3.0 %collective-permute-start.2 = (bf16[2,128,256]{2,1,0:T(8,128)(2,1)S(1)}, bf16[2,128,256]{2,1,0:T(8,128)(2,1)S(1)}, u32[]{:S(2)}, u32[]{:S(2)}) collective-permute-start(bf16[2,128,256]{2,1,0:T(8,128)(2,1)S(1)} %get-tuple-element.26), channel_id=1, source_target_pairs={{0,2},{1,3},{2,0},{3,1},{4,6},{5,7},{6,4},{7,5},{8,10},{9,11},{10,... | collective-permute-start | bytes 393224 | tf_op jit(solution)/shard_map/ppermute | solution.py:295
  8.4 1.5 %collective-permute-start.3 = (bf16[2,128,256]{2,1,0:T(8,128)(2,1)S(1)}, bf16[2,128,256]{2,1,0:T(8,128)(2,1)S(1)}, u32[]{:S(2)}, u32[]{:S(2)}) collective-permute-start(bf16[2,128,256]{2,1,0:T(8,128)(2,1)S(1)} %get-tuple-element.28), channel_id=1, source_target_pairs={{0,4},{1,5},{2,6},{3,7},{4,0},{5,1},{6,2},{7,3},{8,12},{9,13},{10,... | collective-permute-start | bytes 393224 | tf_op jit(solution)/shard_map/ppermute | solution.py:295
  9.9 2.3 %collective-permute-done.2.near_ref = bf16[2,128,256]{2,1,0:T(8,128)(2,1)S(1)} collective-permute-done((bf16[2,128,256]{2,1,0:T(8,128)(2,1)S(1)}, bf16[2,128,256]{2,1,0:T(8,128)(2,1)S(1)}, u32[]{:S(2)}, u32[]{:S(2)}) %collective-permute-start.2) | collective-permute-done | bytes 131104 | tf_op jit(solution)/shard_map/ppermute | solution.py:295
  12.3 0.4 shard_map.104.rows_ref
  12.7 3.7 %collective-permute-done.3.refs_0_ = bf16[2,128,256]{2,1,0:T(8,128)(2,1)S(1)} collective-permute-done((bf16[2,128,256]{2,1,0:T(8,128)(2,1)S(1)}, bf16[2,128,256]{2,1,0:T(8,128)(2,1)S(1)}, u32[]{:S(2)}, u32[]{:S(2)}) %collective-permute-start.3) | collective-permute-done | bytes 131104 | tf_op jit(solution)/shard_map/ppermute | solution.py:295
  16.4 1.3 %shard_map.105 = (bf16[1,129,256]{2,1,0:T(8,128)(2,1)S(1)}, bf16[1024,256]{1,0:T(8,128)(2,1)S(1)}) custom-call(f32[1024,256]{1,0:T(8,128)S(1)} %shard_map.104.rows_ref, bf16[2,128,256]{2,1,0:T(8,128)(2,1)S(1)} %collective-permute-done.3.refs_0_, bf16[2,128,256]{2,1,0:T(8,128)(2,1)S(1)} %collective-permute-done.4.refs_1_, ...), custom_call_target="tpu_custom_call" | custom-call | flops 12884901888 | bytes 6885888 | tf_op jit(solution)/shard_map/pallas_call | solution.py:30
  17.6 0.4 shard_map.107
  18.0 0.5 shard_map.106
  18.6 0.5 collective-permute-start.6
  19.1 1.0 %collective-permute-done.6 = bf16[1,129,256]{2,1,0:T(8,128)(2,1)S(1)} collective-permute-done((bf16[1,129,256]{2,1,0:T(8,128)(2,1)S(1)}, bf16[1,129,256]{2,1,0:T(8,128)(2,1)S(1)}, u32[]{:S(2)}, u32[]{:S(2)}) %collective-permute-start.6) | collective-permute-done | bytes 66080 | tf_op jit(solution)/shard_map/ppermute | solution.py:295
  20.2 1.3 %collective-permute-start.7 = (bf16[258,256]{1,0:T(8,128)(2,1)S(1)}, bf16[258,256]{1,0:T(8,128)(2,1)S(1)}, u32[]{:S(2)}, u32[]{:S(2)}) collective-permute-start(bf16[258,256]{1,0:T(8,128)(2,1)S(1)} %pad_maximum_fusion.1), channel_id=1, source_target_pairs={{0,2},{1,3},{2,0},{3,1},{4,6},{5,7},{6,4},{7,5},{8,10},{9,11},{10,... | collective-permute-start | bytes 396296 | tf_op jit(solution)/shard_map/ppermute | solution.py:295
  21.5 1.8 %collective-permute-start.9 = (bf16[258,256]{1,0:T(8,128)(2,1)S(1)}, bf16[258,256]{1,0:T(8,128)(2,1)S(1)}, u32[]{:S(2)}, u32[]{:S(2)}) collective-permute-start(bf16[258,256]{1,0:T(8,128)(2,1)S(1)} %pad_maximum_fusion.3), channel_id=1, source_target_pairs={{0,6},{1,7},{2,4},{3,5},{4,2},{5,3},{6,0},{7,1},{8,14},{9,15},{10,... | collective-permute-start | bytes 396296 | tf_op jit(solution)/shard_map/ppermute | solution.py:295
  23.3 0.6 %collective-permute-start.8 = (bf16[258,256]{1,0:T(8,128)(2,1)S(1)}, bf16[258,256]{1,0:T(8,128)(2,1)S(1)}, u32[]{:S(2)}, u32[]{:S(2)}) collective-permute-start(bf16[258,256]{1,0:T(8,128)(2,1)S(1)} %pad_maximum_fusion.2), channel_id=1, source_target_pairs={{0,4},{1,5},{2,6},{3,7},{4,0},{5,1},{6,2},{7,3},{8,12},{9,13},{10,... | collective-permute-start | bytes 396296 | tf_op jit(solution)/shard_map/ppermute | solution.py:295
  23.9 2.8 %collective-permute-done.7.near_ref = bf16[258,256]{1,0:T(8,128)(2,1)S(1)} collective-permute-done((bf16[258,256]{1,0:T(8,128)(2,1)S(1)}, bf16[258,256]{1,0:T(8,128)(2,1)S(1)}, u32[]{:S(2)}, u32[]{:S(2)}) %collective-permute-start.7) | collective-permute-done | bytes 132128 | tf_op jit(solution)/shard_map/ppermute | solution.py:295
  26.7 0.4 shard_map.109
  27.1 2.7 %collective-permute-done.9.refs_1_ = bf16[258,256]{1,0:T(8,128)(2,1)S(1)} collective-permute-done((bf16[258,256]{1,0:T(8,128)(2,1)S(1)}, bf16[258,256]{1,0:T(8,128)(2,1)S(1)}, u32[]{:S(2)}, u32[]{:S(2)}) %collective-permute-start.9) | collective-permute-done | bytes 132128 | tf_op jit(solution)/shard_map/ppermute | solution.py:295
  29.9 1.6 %collective-permute-done.8.refs_0_ = bf16[258,256]{1,0:T(8,128)(2,1)S(1)} collective-permute-done((bf16[258,256]{1,0:T(8,128)(2,1)S(1)}, bf16[258,256]{1,0:T(8,128)(2,1)S(1)}, u32[]{:S(2)}, u32[]{:S(2)}) %collective-permute-start.8) | collective-permute-done | bytes 132128 | tf_op jit(solution)/shard_map/ppermute | solution.py:295
  31.4 0.5 shard_map.110.mean_ref
  32.0 1.6 %collective-permute-start.10 = (bf16[128,256]{1,0:T(8,128)(2,1)S(1)}, bf16[128,256]{1,0:T(8,128)(2,1)S(1)}, u32[]{:S(2)}, u32[]{:S(2)}) collective-permute-start(bf16[128,256]{1,0:T(8,128)(2,1)S(1)} %get-tuple-element.45), channel_id=1, source_target_pairs={{0,8},{8,0},{16,24},{24,16},{1,9},{9,1},{17,25},{25,17},{2,10},{10... | collective-permute-start | bytes 196616 | tf_op jit(solution)/shard_map/ppermute | solution.py:295
  33.6 2.6 %collective-permute-start.11 = (bf16[128,256]{1,0:T(8,128)(2,1)S(1)}, bf16[128,256]{1,0:T(8,128)(2,1)S(1)}, u32[]{:S(2)}, u32[]{:S(2)}) collective-permute-start(bf16[128,256]{1,0:T(8,128)(2,1)S(1)} %get-tuple-element.44), channel_id=1, source_target_pairs={{0,16},{8,24},{16,0},{24,8},{1,17},{9,25},{17,1},{25,9},{2,18},{10... | collective-permute-start | bytes 196616 | tf_op jit(solution)/shard_map/ppermute | solution.py:295
  36.9 3.3 %collective-permute-done.11.refs_1_ = bf16[128,256]{1,0:T(8,128)(2,1)S(1)} collective-permute-done((bf16[128,256]{1,0:T(8,128)(2,1)S(1)}, bf16[128,256]{1,0:T(8,128)(2,1)S(1)}, u32[]{:S(2)}, u32[]{:S(2)}) %collective-permute-start.11) | collective-permute-done | bytes 65568 | tf_op jit(solution)/shard_map/ppermute | solution.py:295
  40.2 2.0 %collective-permute-done.12.refs_2_ = bf16[128,256]{1,0:T(8,128)(2,1)S(1)} collective-permute-done((bf16[128,256]{1,0:T(8,128)(2,1)S(1)}, bf16[128,256]{1,0:T(8,128)(2,1)S(1)}, u32[]{:S(2)}, u32[]{:S(2)}) %collective-permute-start.12) | collective-permute-done | bytes 65568 | tf_op jit(solution)/shard_map/ppermute | solution.py:295
  42.2 0.4 shard_map.112
  42.8 1.8 %collective-permute-start.14 = (f16[128,256]{1,0:T(8,128)(2,1)S(1)}, f16[128,256]{1,0:T(8,128)(2,1)S(1)}, u32[]{:S(2)}, u32[]{:S(2)}) collective-permute-start(f16[128,256]{1,0:T(8,128)(2,1)S(1)} %convert_element_type.20), channel_id=1, source_target_pairs={{0,16},{8,24},{16,0},{24,8},{1,17},{9,25},{17,1},{25,9},{2,18},{10... | collective-permute-start | bytes 196616 | tf_op jit(solution)/shard_map/ppermute | solution.py:295
  44.6 2.7 %collective-permute-start.15 = (f16[128,256]{1,0:T(8,128)(2,1)S(1)}, f16[128,256]{1,0:T(8,128)(2,1)S(1)}, u32[]{:S(2)}, u32[]{:S(2)}) collective-permute-start(f16[128,256]{1,0:T(8,128)(2,1)S(1)} %convert_element_type.22), channel_id=1, source_target_pairs={{0,24},{8,16},{16,8},{24,0},{1,25},{9,17},{17,9},{25,1},{2,26},{10... | collective-permute-start | bytes 196616 | tf_op jit(solution)/shard_map/ppermute | solution.py:295
  47.3 0.8 %shard_map.113.refs_3_ = f32[512,256]{1,0:T(8,128)} custom-call(f32[512,256]{1,0:T(8,128)S(1)} %get-tuple-element.37.keep_all_ref.keep_ref, f32[512,256]{1,0:T(8,128)S(1)} %get-tuple-element.38.write_all_ref.write_ref, f32[512,256]{1,0:T(8,128)S(1)} %copy-done, f32[128,256]{1,0:T(8,128)S(1)} %get-tuple-element.42.own_ref), custom_call_target="tpu_custom_call" | custom-call | flops 8388608 | bytes 2228224 | tf_op jit(solution)/shard_map/pallas_call | solution.py:30
  48.2 2.6 %collective-permute-done.15 = f16[128,256]{1,0:T(8,128)(2,1)S(1)} collective-permute-done((f16[128,256]{1,0:T(8,128)(2,1)S(1)}, f16[128,256]{1,0:T(8,128)(2,1)S(1)}, u32[]{:S(2)}, u32[]{:S(2)}) %collective-permute-start.15) | collective-permute-done | bytes 65568 | tf_op jit(solution)/shard_map/ppermute | solution.py:295
  (54 shorter events, 2.2 us)
Async XLA Ops:
  0.0 1.9 %copy-start = (f32[512,256]{1,0:T(8,128)S(1)}, f32[512,256]{1,0:T(8,128)}, u32[]{:S(2)}) copy-start(f32[512,256]{1,0:T(8,128)} %memory_ref.5) | copy-start | bytes 1572868
  0.0 5.0 %collective-permute-start = (s32[8,128]{1,0:T(8,128)}, s32[8,128]{1,0:T(8,128)S(1)}, u32[]{:S(2)}, u32[]{:S(2)}) collective-permute-start(s32[8,128]{1,0:T(8,128)} %bitcast.40), channel_id=1, source_target_pairs={{0,1},{1,0},{2,3},{3,2},{4,5},{5,4},{6,7},{7,6},{8,9},{9,8},{10,11... | collective-permute-start | bytes 12296 | tf_op jit(solution)/shard_map/ppermute | solution.py:295
  0.5 4.5 %collective-permute-start.1 = (f32[512,256]{1,0:T(8,128)}, f32[512,256]{1,0:T(8,128)S(1)}, u32[]{:S(2)}, u32[]{:S(2)}) collective-permute-start(f32[512,256]{1,0:T(8,128)} %memory_ref.5), channel_id=1, source_target_pairs={{0,1},{1,0},{2,3},{3,2},{4,5},{5,4},{6,7},{7,6},{8,9},{9,8},{10,11... | collective-permute-start | bytes 1572872 | tf_op jit(solution)/shard_map/ppermute | solution.py:295
  0.6 0.7 %copy-start.3 = (s32[1,1,8,128]{3,2,1,0:T(8,128)S(1)}, s32[1,1,8,128]{3,2,1,0:T(8,128)}, u32[]{:S(2)}) copy-start(s32[1,1,8,128]{3,2,1,0:T(8,128)} %param.14) | copy-start | bytes 12292
  1.2 0.7 %copy-start.6 = (s32[1,1,512]{2,1,0:T(1,128)S(1)}, s32[1,1,512]{2,1,0:T(1,128)}, u32[]{:S(2)}) copy-start(s32[1,1,512]{2,1,0:T(1,128)} %param.12) | copy-start | bytes 6148
  1.2 0.7 %copy-start.7 = (s32[1,1,512]{2,1,0:T(1,128)S(1)}, s32[1,1,512]{2,1,0:T(1,128)}, u32[]{:S(2)}) copy-start(s32[1,1,512]{2,1,0:T(1,128)} %param.11) | copy-start | bytes 6148
  1.9 0.7 %copy-start.5 = (f32[1,1,512]{2,1,0:T(1,128)S(1)}, f32[1,1,512]{2,1,0:T(1,128)}, u32[]{:S(2)}) copy-start(f32[1,1,512]{2,1,0:T(1,128)} %param.13) | copy-start | bytes 6148
  2.0 0.7 %copy-start.8 = (f32[256]{0:T(256)S(1)}, f32[256]{0:T(256)}, u32[]{:S(2)}) copy-start(f32[256]{0:T(256)} %param.17) | copy-start | bytes 3076
  2.0 0.7 %copy-start.9 = (f32[128]{0:T(128)S(1)}, f32[128]{0:T(128)}, u32[]{:S(2)}) copy-start(f32[128]{0:T(128)} %param.15) | copy-start | bytes 1540
  2.0 1.0 %copy-start.1 = (bf16[640,256]{1,0:T(8,128)(2,1)S(1)}, bf16[640,256]{1,0:T(8,128)(2,1)}, u32[]{:S(2)}) copy-start(bf16[640,256]{1,0:T(8,128)(2,1)} %weight_ref.3) | copy-start | bytes 983044
  5.4 6.9 %collective-permute-start.2 = (bf16[2,128,256]{2,1,0:T(8,128)(2,1)S(1)}, bf16[2,128,256]{2,1,0:T(8,128)(2,1)S(1)}, u32[]{:S(2)}, u32[]{:S(2)}) collective-permute-start(bf16[2,128,256]{2,1,0:T(8,128)(2,1)S(1)} %get-tuple-element.26), channel_id=1, source_target_pairs={{0,2},{1,3},{2,0},{3,1},{4,6},{5,7},{6,4},{7,5},{8,10},{9,11},{10,... | collective-permute-start | bytes 393224 | tf_op jit(solution)/shard_map/ppermute | solution.py:295
  8.4 8.0 %collective-permute-start.3 = (bf16[2,128,256]{2,1,0:T(8,128)(2,1)S(1)}, bf16[2,128,256]{2,1,0:T(8,128)(2,1)S(1)}, u32[]{:S(2)}, u32[]{:S(2)}) collective-permute-start(bf16[2,128,256]{2,1,0:T(8,128)(2,1)S(1)} %get-tuple-element.28), channel_id=1, source_target_pairs={{0,4},{1,5},{2,6},{3,7},{4,0},{5,1},{6,2},{7,3},{8,12},{9,13},{10,... | collective-permute-start | bytes 393224 | tf_op jit(solution)/shard_map/ppermute | solution.py:295
  9.9 6.5 %collective-permute-start.4 = (bf16[2,128,256]{2,1,0:T(8,128)(2,1)S(1)}, bf16[2,128,256]{2,1,0:T(8,128)(2,1)S(1)}, u32[]{:S(2)}, u32[]{:S(2)}) collective-permute-start(bf16[2,128,256]{2,1,0:T(8,128)(2,1)S(1)} %get-tuple-element.29), channel_id=1, source_target_pairs={{0,6},{1,7},{2,4},{3,5},{4,2},{5,3},{6,0},{7,1},{8,14},{9,15},{10,... | collective-permute-start | bytes 393224 | tf_op jit(solution)/shard_map/ppermute | solution.py:295
  18.5 2.9 %collective-permute-start.5 = (bf16[3,129,256]{2,1,0:T(8,128)(2,1)S(1)}, bf16[3,129,256]{2,1,0:T(8,128)(2,1)S(1)}, u32[]{:S(2)}, u32[]{:S(2)}) collective-permute-start(bf16[3,129,256]{2,1,0:T(8,128)(2,1)S(1)} %shard_map.107), channel_id=1, source_target_pairs={{0,1},{1,0},{2,3},{3,2},{4,5},{5,4},{6,7},{7,6},{8,9},{9,8},{10,11... | collective-permute-start | bytes 594440 | tf_op jit(solution)/shard_map/ppermute | solution.py:295
  18.6 1.5 %collective-permute-start.6 = (bf16[1,129,256]{2,1,0:T(8,128)(2,1)S(1)}, bf16[1,129,256]{2,1,0:T(8,128)(2,1)S(1)}, u32[]{:S(2)}, u32[]{:S(2)}) collective-permute-start(bf16[1,129,256]{2,1,0:T(8,128)(2,1)S(1)} %get-tuple-element.34), channel_id=1, source_target_pairs={{0,1},{1,0},{2,3},{3,2},{4,5},{5,4},{6,7},{7,6},{8,9},{9,8},{10,11... | collective-permute-start | bytes 198152 | tf_op jit(solution)/shard_map/ppermute | solution.py:295
  20.2 6.5 %collective-permute-start.7 = (bf16[258,256]{1,0:T(8,128)(2,1)S(1)}, bf16[258,256]{1,0:T(8,128)(2,1)S(1)}, u32[]{:S(2)}, u32[]{:S(2)}) collective-permute-start(bf16[258,256]{1,0:T(8,128)(2,1)S(1)} %pad_maximum_fusion.1), channel_id=1, source_target_pairs={{0,2},{1,3},{2,0},{3,1},{4,6},{5,7},{6,4},{7,5},{8,10},{9,11},{10,... | collective-permute-start | bytes 396296 | tf_op jit(solution)/shard_map/ppermute | solution.py:295
  21.5 8.4 %collective-permute-start.9 = (bf16[258,256]{1,0:T(8,128)(2,1)S(1)}, bf16[258,256]{1,0:T(8,128)(2,1)S(1)}, u32[]{:S(2)}, u32[]{:S(2)}) collective-permute-start(bf16[258,256]{1,0:T(8,128)(2,1)S(1)} %pad_maximum_fusion.3), channel_id=1, source_target_pairs={{0,6},{1,7},{2,4},{3,5},{4,2},{5,3},{6,0},{7,1},{8,14},{9,15},{10,... | collective-permute-start | bytes 396296 | tf_op jit(solution)/shard_map/ppermute | solution.py:295
  23.3 8.1 %collective-permute-start.8 = (bf16[258,256]{1,0:T(8,128)(2,1)S(1)}, bf16[258,256]{1,0:T(8,128)(2,1)S(1)}, u32[]{:S(2)}, u32[]{:S(2)}) collective-permute-start(bf16[258,256]{1,0:T(8,128)(2,1)S(1)} %pad_maximum_fusion.2), channel_id=1, source_target_pairs={{0,4},{1,5},{2,6},{3,7},{4,0},{5,1},{6,2},{7,3},{8,12},{9,13},{10,... | collective-permute-start | bytes 396296 | tf_op jit(solution)/shard_map/ppermute | solution.py:295
  31.4 5.0 %copy-start.2 = (bf16[256,512]{1,0:T(8,128)(2,1)S(1)}, bf16[256,512]{1,0:T(8,128)(2,1)}, u32[]{:S(2)}) copy-start(bf16[256,512]{1,0:T(8,128)(2,1)} %weight_ref.5) | copy-start | bytes 786436
  31.4 5.0 %copy-start.4 = (f32[256]{0:T(256)S(1)}, f32[256]{0:T(256)}, u32[]{:S(2)}) copy-start(f32[256]{0:T(256)} %param.19) | copy-start | bytes 3076
  32.0 5.0 %collective-permute-start.10 = (bf16[128,256]{1,0:T(8,128)(2,1)S(1)}, bf16[128,256]{1,0:T(8,128)(2,1)S(1)}, u32[]{:S(2)}, u32[]{:S(2)}) collective-permute-start(bf16[128,256]{1,0:T(8,128)(2,1)S(1)} %get-tuple-element.45), channel_id=1, source_target_pairs={{0,8},{8,0},{16,24},{24,16},{1,9},{9,1},{17,25},{25,17},{2,10},{10... | collective-permute-start | bytes 196616 | tf_op jit(solution)/shard_map/ppermute | solution.py:295
  33.6 6.6 %collective-permute-start.11 = (bf16[128,256]{1,0:T(8,128)(2,1)S(1)}, bf16[128,256]{1,0:T(8,128)(2,1)S(1)}, u32[]{:S(2)}, u32[]{:S(2)}) collective-permute-start(bf16[128,256]{1,0:T(8,128)(2,1)S(1)} %get-tuple-element.44), channel_id=1, source_target_pairs={{0,16},{8,24},{16,0},{24,8},{1,17},{9,25},{17,1},{25,9},{2,18},{10... | collective-permute-start | bytes 196616 | tf_op jit(solution)/shard_map/ppermute | solution.py:295
  36.2 6.1 %collective-permute-start.12 = (bf16[128,256]{1,0:T(8,128)(2,1)S(1)}, bf16[128,256]{1,0:T(8,128)(2,1)S(1)}, u32[]{:S(2)}, u32[]{:S(2)}) collective-permute-start(bf16[128,256]{1,0:T(8,128)(2,1)S(1)} %get-tuple-element.43), channel_id=1, source_target_pairs={{0,24},{8,16},{16,8},{24,0},{1,25},{9,17},{17,9},{25,1},{2,26},{10... | collective-permute-start | bytes 196616 | tf_op jit(solution)/shard_map/ppermute | solution.py:295
  42.7 5.5 %collective-permute-start.13 = (f16[128,256]{1,0:T(8,128)(2,1)S(1)}, f16[128,256]{1,0:T(8,128)(2,1)S(1)}, u32[]{:S(2)}, u32[]{:S(2)}) collective-permute-start(f16[128,256]{1,0:T(8,128)(2,1)S(1)} %convert_element_type.18), channel_id=1, source_target_pairs={{0,8},{8,0},{16,24},{24,16},{1,9},{9,1},{17,25},{25,17},{2,10},{10... | collective-permute-start | bytes 196616 | tf_op jit(solution)/shard_map/ppermute | solution.py:295
  42.8 5.4 %collective-permute-start.14 = (f16[128,256]{1,0:T(8,128)(2,1)S(1)}, f16[128,256]{1,0:T(8,128)(2,1)S(1)}, u32[]{:S(2)}, u32[]{:S(2)}) collective-permute-start(f16[128,256]{1,0:T(8,128)(2,1)S(1)} %convert_element_type.20), channel_id=1, source_target_pairs={{0,16},{8,24},{16,0},{24,8},{1,17},{9,25},{17,1},{25,9},{2,18},{10... | collective-permute-start | bytes 196616 | tf_op jit(solution)/shard_map/ppermute | solution.py:295
  44.6 6.2 %collective-permute-start.15 = (f16[128,256]{1,0:T(8,128)(2,1)S(1)}, f16[128,256]{1,0:T(8,128)(2,1)S(1)}, u32[]{:S(2)}, u32[]{:S(2)}) collective-permute-start(f16[128,256]{1,0:T(8,128)(2,1)S(1)} %convert_element_type.22), channel_id=1, source_target_pairs={{0,24},{8,16},{16,8},{24,0},{1,25},{9,17},{17,9},{25,1},{2,26},{10... | collective-permute-start | bytes 196616 | tf_op jit(solution)/shard_map/ppermute | solution.py:295
